TPU v7x, 256 devices: a whole 4x4x8 slice. The times are simulated.
256 devices in a mesh: row: 32 (over z_hi, x, core), col: 8 (over z_lo, y).
Axes of the slice: x: 4, y: 4, z: 8 (z_hi: 4, z_lo: 2; z = z_hi * 2 + z_lo), core: 2. Of those that a mesh axis runs over, the one named last changes fastest.
Arguments:
- blocks: bfloat16 [32, 512, 128, 128], P('row', 'col')
- block_rows: int32 [32, 512], P('row', 'col'), may hold values from 0 to 255, as said below
- block_cols: int32 [32, 512], P('row', 'col'), may hold values from 0 to 255, as said below
- counts: int32 [32, 8], P('row', 'col'), may hold values from 1 to 64, as said below
- trials: bfloat16 [32768, 256], P(('col', 'row')), may hold values from -6 to 6
Outputs:
- basis: float32 [32768, 256], P(('col', 'row'))
- factor: float32 [256, 256], replicated
Inputs may be any that keep to these rules, and one draw needn't show every extreme that they name: The live slots of a device are its first counts[r, c] slots, and at least one device has all 64 slots live. `block_rows`: for the device at grid position (r, c), every slot's block row leaves remainder r on division by the size of axis row. The live slots of a device name distinct blocks with block row at most block column; slots past the count hold arbitrary blocks whose coordinates have the same form. `block_cols`: for the device at grid position (r, c), every slot's block column divided by the size of axis row gives c.
All inputs are finite; a program needn't handle non-finite values.
Results may differ from a plain program's by a relative error of at most 0.0003.
Values may be sent and summed in bfloat16 or wider, within the bound.
No kernel may reach another device: no remote copies, remote signals or barrier semaphores. Data moves between devices by JAX's collectives and lax.ppermute only.
A program may use at most 64 MiB of HBM per device.

v0:
```python
import jax
import jax.numpy as jnp
from jax import lax
from jax.experimental import pallas as pl
from jax.experimental.pallas import tpu as pltpu
from jax.sharding import PartitionSpec as P


N_ZH, N_X, N_CORE, N_ZL, N_Y = 4, 4, 2, 2, 4
N_ROW = N_ZH * N_X * N_CORE
N_COL = N_ZL * N_Y
F32 = jnp.float32
BLOCK, SUB, LANES = 64, 8, 128
STEP = SUB


def row_at(z, x, c):
    return ((z % N_ZH) * N_X + x % N_X) * N_CORE + c


def col_at(zl, y):
    return zl * N_Y + y % N_Y


def row_pairs(move):
    return [(row_at(z, x, c), row_at(*move(z, x, c))) for z in range(N_ZH) for x in range(N_X) for c in range(N_CORE)]


def to_z(v, k):
    return lax.ppermute(v, "row", row_pairs(lambda z, x, c: (z + k, x, c)))


def to_x(v, k):
    return lax.ppermute(v, "row", row_pairs(lambda z, x, c: (z, x + k, c)))


def to_core(v):
    return lax.ppermute(v, "row", row_pairs(lambda z, x, c: (z, x, 1 - c)))


def to_y(v, k):
    return lax.ppermute(v, "col", [(col_at(zl, y), col_at(zl, y + k)) for zl in range(N_ZL) for y in range(N_Y)])


def to_zl(v):
    return lax.ppermute(v, "col", [(col_at(zl, y), col_at(1 - zl, y)) for zl in range(N_ZL) for y in range(N_Y)])


def ring_sum(parts):
    return (parts[0] + parts[2]) + (parts[1] + parts[3])


def clear(acc):
    def one(n, carry):
        acc[n] = jnp.zeros(acc.shape[1:], acc.dtype)
        return carry

    lax.fori_loop(0, acc.shape[0], one, 0)


def hand_out(acc, outs):
    for k, out in enumerate(outs):
        size = out.shape[0]

        def one(n, carry):
            out[n] = acc[k * size + n]
            return carry

        lax.fori_loop(0, size, one, 0)


def slot_loop(counts, rows, cols, blocks, add):
    live = counts[0, 0]

    def visit(s):
        i, j = rows[0, s], cols[0, s]
        q = jnp.where(s < live, jnp.where(i == j, 0.5, 1.0), 0.0)
        tile = jnp.where(q > 0.0, blocks[s].astype(F32) * q, 0.0).astype(jnp.bfloat16)
        add(tile, i >> 5, j & (N_ROW - 1))

    def group(g, carry):
        for u in range(4):
            visit(g * 4 + u)
        return carry

    lax.fori_loop(0, (live + 3) // 4, group, 0)


def row_spot(place, rp):
    return ((rp - place[1]) & 3) * N_ZL + ((rp >> 2) ^ (place[1] >> 2))


def col_spot(place, cp):
    r = place[0]
    zk, xk, cx = ((cp >> 3) - (r >> 3)) & 3, ((cp >> 1) - (r >> 1)) & 3, (cp ^ r) & 1
    return cx * N_X * N_ZH, xk, zk


def mirror_kernel(place, counts, rows, cols, blocks, *refs):
    pieces, outs, vectors, acc = refs[:N_Y], refs[N_Y:-2], refs[-2], refs[-1]
    clear(acc)
    for k, piece in enumerate(pieces):
        vectors[k * N_ZL : (k + 1) * N_ZL] = piece[...]

    def add(tile, rp, cp):
        base, xk, zk = col_spot(place, cp)
        acc[base + xk * N_ZH + zk] += lax.dot_general(
            tile, vectors[row_spot(place, rp)], (((0,), (0,)), ((), ())), preferred_element_type=F32
        )

    slot_loop(counts, rows, cols, blocks, add)
    hand_out(acc, outs)


def direct_kernel(place, counts, rows, cols, blocks, *refs):
    n = N_CORE * N_ZH
    pieces, outs, vectors, acc = refs[:n], refs[n : n + N_Y], refs[-2], refs[-1]
    clear(acc)
    for k, piece in enumerate(pieces):
        vectors[k * N_X : (k + 1) * N_X] = piece[...]

    def add(tile, rp, cp):
        base, xk, zk = col_spot(place, cp)
        acc[row_spot(place, rp)] += jnp.dot(tile, vectors[base + zk * N_X + xk], preferred_element_type=F32)

    slot_loop(counts, rows, cols, blocks, add)
    hand_out(acc, outs)


def products_of(kernel, scalars, blocks, pieces, n_out, out_blocks):
    edge, width = pieces[0].shape[1:]
    smem = pl.BlockSpec(memory_space=pltpu.SMEM)
    vmem = pl.BlockSpec(memory_space=pltpu.VMEM)
    n_in = len(pieces) * pieces[0].shape[0]
    return pl.pallas_call(
        kernel,
        out_shape=(jax.ShapeDtypeStruct((out_blocks, edge, width), F32),) * n_out,
        in_specs=[smem] * 4 + [vmem] * (1 + len(pieces)),
        out_specs=(vmem,) * n_out,
        scratch_shapes=[
            pltpu.VMEM((n_in, edge, width), jnp.bfloat16),
            pltpu.VMEM((n_out * out_blocks, edge, width), F32),
        ],
        cost_estimate=pl.CostEstimate(
            flops=2 * blocks.shape[0] * edge * edge * width,
            bytes_accessed=2 * blocks.size + 2 * n_in * edge * width + 4 * n_out * out_blocks * edge * width,
            transcendentals=0,
        ),
        compiler_params=pltpu.CompilerParams(vmem_limit_bytes=16 << 20),
    )(*scalars, blocks, *pieces)


def spread(v):
    return jnp.broadcast_to(v, (SUB, LANES))


def eliminate(tiles, done):
    for g in range(BLOCK // STEP):
        k = lane = g * STEP
        head = tiles[g]
        rows = [spread(head[a : a + 1, :]) for a in range(STEP)]
        pivot = [[spread(head[a : a + 1, lane + b : lane + b + 1]) for b in range(a + 1)] for a in range(STEP)]
        rest = list(range(g + 1, len(tiles)))
        cols = {i: [spread(tiles[i][:, lane + a : lane + a + 1]) for a in range(STEP)] for i in rest}
        inverse = []
        for a in range(STEP):
            inverse.append(1.0 / pivot[a][a])
            for n in range(a + 1, STEP):
                ratio = pivot[n][a] * inverse[a]
                for b in range(a + 1, n + 1):
                    pivot[n][b] = pivot[n][b] - ratio * pivot[b][a]
                rows[n] = rows[n] - ratio * rows[a]
                for i in rest:
                    cols[i][n] = cols[i][n] - ratio * cols[i][a]
        for a in range(STEP):
            done[k + a : k + a + 1, :] = (rows[a] * lax.rsqrt(pivot[a][a]))[0:1, :]
        scaled = [rows[a] * inverse[a] for a in range(STEP)]
        for i in rest:
            terms = [cols[i][a] * scaled[a] for a in range(STEP)]
            while len(terms) > 1:
                terms = [terms[m] + terms[m + 1] for m in range(0, len(terms), 2)]
            tiles[i] = tiles[i] - terms[0]


def set_stage(work, stage, top):
    tile, offset = top // LANES * LANES, top % LANES
    part = work[top : top + BLOCK, tile : tile + LANES]
    if offset:
        part = pltpu.roll(part, BLOCK, 1)
    lanes = lax.broadcasted_iota(jnp.int32, (BLOCK, LANES), 1)
    unit = jnp.where(lanes == lax.broadcasted_iota(jnp.int32, (BLOCK, LANES), 0) + BLOCK, 1.0, 0.0)
    stage[...] = jnp.where(lanes < BLOCK, part, unit)


def apply_block(work, stage, done, factor, top):
    size = factor.shape[1]
    lanes = lax.broadcasted_iota(jnp.int32, (BLOCK, LANES), 1)
    inverse = jnp.where(lanes < BLOCK, 0.0, done[...])
    panel = work[top : top + BLOCK, :]
    upper = jnp.dot(
        inverse, jnp.concatenate([panel, panel], 0), precision=lax.Precision.HIGHEST, preferred_element_type=F32
    )
    rows = lax.broadcasted_iota(jnp.int32, (BLOCK, size), 0) + top
    keep = lax.broadcasted_iota(jnp.int32, (BLOCK, size), 1) >= rows
    head = jnp.where(keep, upper[:, :size], 0.0)
    factor[top : top + BLOCK, :] = head
    work[top : top + BLOCK, size:] = upper[:, size:]
    if top + BLOCK < size:
        low = (top + BLOCK) // LANES * LANES
        full = jnp.concatenate([head, upper[:, size:]], 1)
        take = lax.dot_general(
            head[:, low:],
            full[:, low:],
            (((0,), (0,)), ((), ())),
            precision=lax.Precision.HIGHEST,
            preferred_element_type=F32,
        )
        work[top + BLOCK :, low:] = work[top + BLOCK :, low:] - take[top + BLOCK - low :, :]
        set_stage(work, stage, top + BLOCK)


def factor_kernel(place, piece0, piece1, piece2, piece3, products, basis, factor, work, stage, done):
    edge, size = products.shape
    rows = size // (N_CORE * N_Y)
    my_core, my_y = place[0] & (N_CORE - 1), place[1] & (N_Y - 1)
    for k, piece in enumerate((piece0, piece1, piece2, piece3)):
        for side in range(N_CORE):
            at = (((my_core + side) & 1) * N_Y + ((my_y + k) & (N_Y - 1))) * rows
            work[pl.ds(pl.multiple_of(at, rows), rows), :size] = piece[side] * (1.0 / (N_ROW * N_COL * edge))
    work[:, size:] = products[...].T
    set_stage(work, stage, 0)

    def block(p, carry):
        eliminate([stage[i * SUB : (i + 1) * SUB, :] for i in range(BLOCK // SUB)], done)
        for q in range(size // BLOCK):
            pl.when(p == q)(lambda q=q: apply_block(work, stage, done, factor, q * BLOCK))
        return carry

    lax.fori_loop(0, size // BLOCK, block, 0)
    basis[...] = work[:, size:].T


def factor_and_basis(place, pieces, products):
    edge, size = products.shape
    vmem = pl.BlockSpec(memory_space=pltpu.VMEM)
    return pl.pallas_call(
        factor_kernel,
        out_shape=(jax.ShapeDtypeStruct((edge, size), F32), jax.ShapeDtypeStruct((size, size), F32)),
        in_specs=[pl.BlockSpec(memory_space=pltpu.SMEM)] + [vmem] * 5,
        out_specs=(vmem, vmem),
        scratch_shapes=[pltpu.VMEM((size, size + edge), F32)] + [pltpu.VMEM((BLOCK, LANES), F32)] * 2,
        compiler_params=pltpu.CompilerParams(vmem_limit_bytes=8 << 20),
        name="factor",
    )(place, *pieces, products)


def gram_pieces(products, place):
    width = products.shape[1]
    half, piece = width // N_CORE, width // (N_CORE * N_Y)
    my_core, my_y = place[0] & (N_CORE - 1), place[1] & (N_Y - 1)
    local = jnp.dot(products.T, products, precision=lax.Precision.HIGHEST, preferred_element_type=F32)
    mine = lax.dynamic_slice_in_dim(local, my_core * half, half, 0)
    other = lax.dynamic_slice_in_dim(local, (1 - my_core) * half, half, 0)
    pair = mine + to_core(other)
    parts = [lax.dynamic_slice_in_dim(pair, ((my_y + k) & (N_Y - 1)) * piece, piece, 0) for k in range(N_Y)]
    got = ring_sum([parts[0]] + [to_y(parts[k], k) for k in range(1, N_Y)])
    got = ring_sum([got] + [to_x(got, k) for k in range(1, N_X)])
    got = got + to_zl(got)
    got = ring_sum([got] + [to_z(got, k) for k in range(1, N_ZH)])
    both = jnp.stack([got, to_core(got)])
    return [both] + [to_y(both, -k) for k in range(1, N_Y)]


def body(blocks, block_rows, block_cols, counts, trials):
    place = jnp.stack([lax.axis_index("row"), lax.axis_index("col")]).astype(jnp.int32)
    scalars = (place, counts, block_rows, block_cols)
    first = jnp.stack([trials, to_zl(trials)])
    xs = jnp.stack([trials] + [to_x(trials, -k) for k in range(1, N_X)])
    row_pieces = [first] + [to_y(first, -k) for k in range(1, N_Y)]
    col_pieces = [xs] + [to_z(xs, -k) for k in range(1, N_ZH)]
    outs = products_of(mirror_kernel, scalars, blocks[0], row_pieces, N_CORE * N_X, N_ZH)
    keep, send = outs[:N_X], outs[N_X:]
    col_pieces = col_pieces + [to_core(v) for v in col_pieces]
    row_outs = products_of(direct_kernel, scalars, blocks[0], col_pieces, N_Y, N_ZL)
    theirs = {k: to_core(send[k]) for k in (1, 3, 2, 0)}
    sent = {k: to_x(keep[k] + theirs[k], k) for k in (1, 3, 2)}
    got = ring_sum([keep[0] + theirs[0]] + [sent[k] for k in range(1, N_X)])
    rows = ring_sum([row_outs[0]] + [to_y(row_outs[k], k) for k in range(1, N_Y)])
    row_sum = rows[0] + to_zl(rows[1])
    col_sum = ring_sum([got[0]] + [to_z(got[k], k) for k in range(1, N_ZH)])
    products = row_sum + col_sum
    return factor_and_basis(place, gram_pieces(products, place), products)


def solution(mesh):
    return jax.shard_map(
        body,
        mesh=mesh,
        in_specs=(
            P("row", "col", None, None),
            P("row", "col"),
            P("row", "col"),
            P("row", "col"),
            P(("col", "row"), None),
        ),
        out_specs=(P(("col", "row"), None), P()),
        check_vma=False,
    )
```

profile of v0, /device:TPU:2, one launch (start us, length us, event | category | flops | bytes accessed | tf_op | source)
XLA Modules:
  0.0 158.1 jit_solution(17679946118806108542)
XLA Ops:
  0.6 1.6 collective-permute-start.2
  2.2 2.8 %collective-permute-start.1 = (bf16[128,256]{1,0:T(8,128)(2,1)}, bf16[128,256]{1,0:T(8,128)(2,1)S(1)}, u32[]{:S(2)}, u32[]{:S(2)}) collective-permute-start(bf16[128,256]{1,0:T(8,128)(2,1)} %param.9), channel_id=1, source_target_pairs={{0,32},{8,40},{16,48},{24,56},{32,0},{40,8},{48,16},{56,24},{64,96... | collective-permute-start | bytes 196616 | tf_op jit(solution)/shard_map/ppermute | solution.py:34
  5.5 1.9 %collective-permute-start.14 = (bf16[128,256]{1,0:T(8,128)(2,1)}, bf16[128,256]{1,0:T(8,128)(2,1)S(1)}, u32[]{:S(2)}, u32[]{:S(2)}) collective-permute-start(bf16[128,256]{1,0:T(8,128)(2,1)} %param.9), channel_id=1, source_target_pairs={{0,4},{1,5},{2,6},{3,7},{4,0},{5,1},{6,2},{7,3},{8,12},{9,13},{10,... | collective-permute-start | bytes 196616 | tf_op jit(solution)/shard_map/ppermute | solution.py:46
  8.2 1.3 collective-permute-done
  10.4 5.4 %collective-permute-start.3 = (bf16[4,128,256]{2,1,0:T(8,128)(2,1)S(1)}, bf16[4,128,256]{2,1,0:T(8,128)(2,1)S(1)}, u32[]{:S(2)}, u32[]{:S(2)}) collective-permute-start(bf16[4,128,256]{2,1,0:T(8,128)(2,1)S(1)} %pad_maximum_fusion.refs_0_), channel_id=1, source_target_pairs={{0,192},{8,200},{16,208},{24,216},{32,224},{40,232},{48,240},{56,2... | collective-permute-start | bytes 786440 | tf_op jit(solution)/shard_map/ppermute | solution.py:30
  16.6 3.1 %collective-permute-start.15 = (bf16[2,128,256]{2,1,0:T(8,128)(2,1)S(1)}, bf16[2,128,256]{2,1,0:T(8,128)(2,1)S(1)}, u32[]{:S(2)}, u32[]{:S(2)}) collective-permute-start(bf16[2,128,256]{2,1,0:T(8,128)(2,1)S(1)} %pad_maximum_fusion.1.refs_0_), channel_id=1, source_target_pairs={{0,3},{1,0},{2,1},{3,2},{4,7},{5,4},{6,5},{7,6},{8,11},{9,8},{10,9... | collective-permute-start | bytes 393224 | tf_op jit(solution)/shard_map/ppermute | solution.py:42
  20.3 1.0 collective-permute-start.17
  21.3 1.6 %collective-permute-start.4 = (bf16[4,128,256]{2,1,0:T(8,128)(2,1)S(1)}, bf16[4,128,256]{2,1,0:T(8,128)(2,1)S(1)}, u32[]{:S(2)}, u32[]{:S(2)}) collective-permute-start(bf16[4,128,256]{2,1,0:T(8,128)(2,1)S(1)} %pad_maximum_fusion.refs_0_), channel_id=1, source_target_pairs={{0,128},{8,136},{16,144},{24,152},{32,160},{40,168},{48,176},{56,1... | collective-permute-start | bytes 786440 | tf_op jit(solution)/shard_map/ppermute | solution.py:30
  23.6 1.5 collective-permute-start.5
  26.3 10.2 %collective-permute-done.3.refs_1_ = bf16[4,128,256]{2,1,0:T(8,128)(2,1)S(1)} collective-permute-done((bf16[4,128,256]{2,1,0:T(8,128)(2,1)S(1)}, bf16[4,128,256]{2,1,0:T(8,128)(2,1)S(1)}, u32[]{:S(2)}, u32[]{:S(2)}) %collective-permute-start.3) | collective-permute-done | bytes 262176 | tf_op jit(solution)/shard_map/ppermute | solution.py:30
  36.5 1.6 %copy-done = bf16[1,64,128,128]{3,2,1,0:T(8,128)(2,1)S(1)} copy-done((bf16[1,64,128,128]{3,2,1,0:T(8,128)(2,1)S(1)}, bf16[1,64,128,128]{3,2,1,0:T(8,128)(2,1)}, u32[]{:S(2)}) %copy-start) | copy-done | bytes 2097176
  39.4 3.2 %shard_map.69 = (f32[4,128,256]{2,1,0:T(8,128)S(1)}, f32[4,128,256]{2,1,0:T(8,128)S(1)}, f32[4,128,256]{2,1,0:T(8,128)S(1)}, f32[4,128,256]{2,1,0:T(8,128)S(1)},...) custom-call(s32[2]{0:T(128)S(1)} %pad_add_fusion.place, ...), custom_call_target="tpu_custom_call" | custom-call | flops 536870912 | bytes 6815744 | tf_op jit(solution)/shard_map/pallas_call | solution.py:135
  45.7 2.5 %shard_map.68 = (f32[2,128,256]{2,1,0:T(8,128)S(1)}, f32[2,128,256]{2,1,0:T(8,128)S(1)}, f32[2,128,256]{2,1,0:T(8,128)S(1)}, f32[2,128,256]{2,1,0:T(8,128)S(1)}) custom-call(s32[2]{0:T(128)S(1)} %pad_add_fusion.place, s32[1,1]{1,0:T(1,128)S(6)} %copy.7.counts, s32[1,64]{1,0:T(1,128)S(1)} %copy-done.1, s32[1,64]{1,0:T(1,128)S(1)} %copy-done.2, ...), custom_call_target="tpu_custom_call" | custom-call | flops 536870912 | bytes 5242880 | tf_op jit(solution)/shard_map/pallas_call | solution.py:135
  48.3 2.9 %collective-permute-start.11 = (f32[2,128,256]{2,1,0:T(8,128)S(1)}, f32[2,128,256]{2,1,0:T(8,128)S(1)}, u32[]{:S(2)}, u32[]{:S(2)}) collective-permute-start(f32[2,128,256]{2,1,0:T(8,128)S(1)} %get-tuple-element.16), channel_id=1, source_target_pairs={{0,1},{1,2},{2,3},{3,0},{4,5},{5,6},{6,7},{7,4},{8,9},{9,10},{10,1... | collective-permute-start | bytes 786440 | tf_op jit(solution)/shard_map/ppermute | solution.py:42
  51.8 3.1 %collective-permute-start.10 = (f32[2,128,256]{2,1,0:T(8,128)S(1)}, f32[2,128,256]{2,1,0:T(8,128)S(1)}, u32[]{:S(2)}, u32[]{:S(2)}) collective-permute-start(f32[2,128,256]{2,1,0:T(8,128)S(1)} %get-tuple-element.15), channel_id=1, source_target_pairs={{0,2},{1,3},{2,0},{3,1},{4,6},{5,7},{6,4},{7,5},{8,10},{9,11},{10,... | collective-permute-start | bytes 786440 | tf_op jit(solution)/shard_map/ppermute | solution.py:42
  55.1 1.8 %collective-permute-start.22 = (f32[4,128,256]{2,1,0:T(8,128)S(1)}, f32[4,128,256]{2,1,0:T(8,128)S(1)}, u32[]{:S(2)}, u32[]{:S(2)}) collective-permute-start(f32[4,128,256]{2,1,0:T(8,128)S(1)} %add.112), channel_id=1, source_target_pairs={{0,16},{8,24},{16,32},{24,40},{32,48},{40,56},{48,0},{56,8},{64,80... | collective-permute-start | bytes 1572872 | tf_op jit(solution)/shard_map/ppermute | solution.py:34
  57.0 1.6 %collective-permute-done.11 = f32[2,128,256]{2,1,0:T(8,128)S(1)} collective-permute-done((f32[2,128,256]{2,1,0:T(8,128)S(1)}, f32[2,128,256]{2,1,0:T(8,128)S(1)}, u32[]{:S(2)}, u32[]{:S(2)}) %collective-permute-start.11) | collective-permute-done | bytes 262176 | tf_op jit(solution)/shard_map/ppermute | solution.py:42
  58.6 1.5 collective-permute-start.24
  60.1 3.5 %collective-permute-done.12 = f32[2,128,256]{2,1,0:T(8,128)S(1)} collective-permute-done((f32[2,128,256]{2,1,0:T(8,128)S(1)}, f32[2,128,256]{2,1,0:T(8,128)S(1)}, u32[]{:S(2)}, u32[]{:S(2)}) %collective-permute-start.12) | collective-permute-done | bytes 262176 | tf_op jit(solution)/shard_map/ppermute | solution.py:42
  63.6 3.6 %collective-permute-start.20 = (f32[4,128,256]{2,1,0:T(8,128)S(1)}, f32[4,128,256]{2,1,0:T(8,128)S(1)}, u32[]{:S(2)}, u32[]{:S(2)}) collective-permute-start(f32[4,128,256]{2,1,0:T(8,128)S(1)} %add.110), channel_id=1, source_target_pairs={{0,32},{8,40},{16,48},{24,56},{32,0},{40,8},{48,16},{56,24},{64,96... | collective-permute-start | bytes 1572872 | tf_op jit(solution)/shard_map/ppermute | solution.py:34
  67.4 3.1 %collective-permute-done.22 = f32[4,128,256]{2,1,0:T(8,128)S(1)} collective-permute-done((f32[4,128,256]{2,1,0:T(8,128)S(1)}, f32[4,128,256]{2,1,0:T(8,128)S(1)}, u32[]{:S(2)}, u32[]{:S(2)}) %collective-permute-start.22) | collective-permute-done | bytes 524320 | tf_op jit(solution)/shard_map/ppermute | solution.py:34
  70.5 3.1 %collective-permute-done.24 = f32[4,128,256]{2,1,0:T(8,128)S(1)} collective-permute-done((f32[4,128,256]{2,1,0:T(8,128)S(1)}, f32[4,128,256]{2,1,0:T(8,128)S(1)}, u32[]{:S(2)}, u32[]{:S(2)}) %collective-permute-start.24) | collective-permute-done | bytes 524320 | tf_op jit(solution)/shard_map/ppermute | solution.py:34
  73.5 10.9 %collective-permute-done.20 = f32[4,128,256]{2,1,0:T(8,128)S(1)} collective-permute-done((f32[4,128,256]{2,1,0:T(8,128)S(1)}, f32[4,128,256]{2,1,0:T(8,128)S(1)}, u32[]{:S(2)}, u32[]{:S(2)}) %collective-permute-start.20) | collective-permute-done | bytes 524320 | tf_op jit(solution)/shard_map/ppermute | solution.py:34
  84.6 3.4 %collective-permute-start.25 = (f32[128,256]{1,0:T(8,128)S(1)}, f32[128,256]{1,0:T(8,128)S(1)}, u32[]{:S(2)}, u32[]{:S(2)}) collective-permute-start(f32[128,256]{1,0:T(8,128)S(1)} %get-tuple-element.28), channel_id=1, source_target_pairs={{0,128},{8,136},{16,144},{24,152},{32,160},{40,168},{48,176},{56,1... | collective-permute-start | bytes 393224 | tf_op jit(solution)/shard_map/ppermute | solution.py:30
  88.0 4.0 %collective-permute-start.26 = (f32[128,256]{1,0:T(8,128)S(1)}, f32[128,256]{1,0:T(8,128)S(1)}, u32[]{:S(2)}, u32[]{:S(2)}) collective-permute-start(f32[128,256]{1,0:T(8,128)S(1)} %get-tuple-element.27), channel_id=1, source_target_pairs={{0,64},{8,72},{16,80},{24,88},{32,96},{40,104},{48,112},{56,120},{... | collective-permute-start | bytes 393224 | tf_op jit(solution)/shard_map/ppermute | solution.py:30
  92.2 2.7 %collective-permute-done.25 = f32[128,256]{1,0:T(8,128)S(1)} collective-permute-done((f32[128,256]{1,0:T(8,128)S(1)}, f32[128,256]{1,0:T(8,128)S(1)}, u32[]{:S(2)}, u32[]{:S(2)}) %collective-permute-start.25) | collective-permute-done | bytes 131104 | tf_op jit(solution)/shard_map/ppermute | solution.py:30
  94.9 2.8 %collective-permute-done.26 = f32[128,256]{1,0:T(8,128)S(1)} collective-permute-done((f32[128,256]{1,0:T(8,128)S(1)}, f32[128,256]{1,0:T(8,128)S(1)}, u32[]{:S(2)}, u32[]{:S(2)}) %collective-permute-start.26) | collective-permute-done | bytes 131104 | tf_op jit(solution)/shard_map/ppermute | solution.py:30
  97.7 0.9 collective-permute-done.27
  99.2 1.3 collective-permute-done.28
  100.6 5.7 %collective-permute-start.30 = (f32[32,256]{1,0:T(8,128)S(1)}, f32[32,256]{1,0:T(8,128)S(1)}, u32[]{:S(2)}, u32[]{:S(2)}) collective-permute-start(f32[32,256]{1,0:T(8,128)S(1)} %get-tuple-element.31), channel_id=1, source_target_pairs={{0,1},{1,2},{2,3},{3,0},{4,5},{5,6},{6,7},{7,4},{8,9},{9,10},{10,1... | collective-permute-start | bytes 98312 | tf_op jit(solution)/shard_map/ppermute | solution.py:42
  106.3 4.5 %collective-permute-start.29 = (f32[32,256]{1,0:T(8,128)S(1)}, f32[32,256]{1,0:T(8,128)S(1)}, u32[]{:S(2)}, u32[]{:S(2)}) collective-permute-start(f32[32,256]{1,0:T(8,128)S(1)} %get-tuple-element.29), channel_id=1, source_target_pairs={{0,2},{1,3},{2,0},{3,1},{4,6},{5,7},{6,4},{7,5},{8,10},{9,11},{10,... | collective-permute-start | bytes 98312 | tf_op jit(solution)/shard_map/ppermute | solution.py:42
  110.8 1.9 %collective-permute-done.29 = f32[32,256]{1,0:T(8,128)S(1)} collective-permute-done((f32[32,256]{1,0:T(8,128)S(1)}, f32[32,256]{1,0:T(8,128)S(1)}, u32[]{:S(2)}, u32[]{:S(2)}) %collective-permute-start.29) | collective-permute-done | bytes 32800 | tf_op jit(solution)/shard_map/ppermute | solution.py:42
  112.8 2.0 %collective-permute-start.34 = (f32[32,256]{1,0:T(8,128)S(1)}, f32[32,256]{1,0:T(8,128)S(1)}, u32[]{:S(2)}, u32[]{:S(2)}) collective-permute-start(f32[32,256]{1,0:T(8,128)S(1)} %add_add_fusion.4), channel_id=1, source_target_pairs={{0,48},{8,56},{16,0},{24,8},{32,16},{40,24},{48,32},{56,40},{64,11... | collective-permute-start | bytes 98312 | tf_op jit(solution)/shard_map/ppermute | solution.py:34
  114.8 1.3 collective-permute-start.32
  116.8 3.4 %collective-permute-done.32 = f32[32,256]{1,0:T(8,128)S(1)} collective-permute-done((f32[32,256]{1,0:T(8,128)S(1)}, f32[32,256]{1,0:T(8,128)S(1)}, u32[]{:S(2)}, u32[]{:S(2)}) %collective-permute-start.32) | collective-permute-done | bytes 32800 | tf_op jit(solution)/shard_map/ppermute | solution.py:34
  120.3 1.9 %collective-permute-start.35 = (f32[32,256]{1,0:T(8,128)S(1)}, f32[32,256]{1,0:T(8,128)S(1)}, u32[]{:S(2)}, u32[]{:S(2)}) collective-permute-start(f32[32,256]{1,0:T(8,128)S(1)} %add_add_fusion.3), channel_id=1, source_target_pairs={{0,4},{1,5},{2,6},{3,7},{4,0},{5,1},{6,2},{7,3},{8,12},{9,13},{10,... | collective-permute-start | bytes 98312 | tf_op jit(solution)/shard_map/ppermute | solution.py:46
  122.2 2.1 %collective-permute-done.35 = f32[32,256]{1,0:T(8,128)S(1)} collective-permute-done((f32[32,256]{1,0:T(8,128)S(1)}, f32[32,256]{1,0:T(8,128)S(1)}, u32[]{:S(2)}, u32[]{:S(2)}) %collective-permute-start.35) | collective-permute-done | bytes 32800 | tf_op jit(solution)/shard_map/ppermute | solution.py:46
  124.3 2.2 %collective-permute-start.37 = (f32[32,256]{1,0:T(8,128)S(1)}, f32[32,256]{1,0:T(8,128)S(1)}, u32[]{:S(2)}, u32[]{:S(2)}) collective-permute-start(f32[32,256]{1,0:T(8,128)S(1)} %add.136), channel_id=1, source_target_pairs={{0,64},{8,72},{16,80},{24,88},{32,96},{40,104},{48,112},{56,120},{... | collective-permute-start | bytes 98312 | tf_op jit(solution)/shard_map/ppermute | solution.py:30
  126.5 2.0 %collective-permute-start.38 = (f32[32,256]{1,0:T(8,128)S(1)}, f32[32,256]{1,0:T(8,128)S(1)}, u32[]{:S(2)}, u32[]{:S(2)}) collective-permute-start(f32[32,256]{1,0:T(8,128)S(1)} %add.136), channel_id=1, source_target_pairs={{0,192},{8,200},{16,208},{24,216},{32,224},{40,232},{48,240},{56,2... | collective-permute-start | bytes 98312 | tf_op jit(solution)/shard_map/ppermute | solution.py:30
  128.4 5.3 %collective-permute-start.36 = (f32[32,256]{1,0:T(8,128)S(1)}, f32[32,256]{1,0:T(8,128)S(1)}, u32[]{:S(2)}, u32[]{:S(2)}) collective-permute-start(f32[32,256]{1,0:T(8,128)S(1)} %add.136), channel_id=1, source_target_pairs={{0,128},{8,136},{16,144},{24,152},{32,160},{40,168},{48,176},{56,1... | collective-permute-start | bytes 98312 | tf_op jit(solution)/shard_map/ppermute | solution.py:30
  133.7 2.5 %collective-permute-done.36 = f32[32,256]{1,0:T(8,128)S(1)} collective-permute-done((f32[32,256]{1,0:T(8,128)S(1)}, f32[32,256]{1,0:T(8,128)S(1)}, u32[]{:S(2)}, u32[]{:S(2)}) %collective-permute-start.36) | collective-permute-done | bytes 32800 | tf_op jit(solution)/shard_map/ppermute | solution.py:30
  136.4 1.2 collective-permute-done.39
  137.6 2.2 %collective-permute-start.40 = (f32[2,32,256]{2,1,0:T(8,128)S(1)}, f32[2,32,256]{2,1,0:T(8,128)S(1)}, u32[]{:S(2)}, u32[]{:S(2)}) collective-permute-start(f32[2,32,256]{2,1,0:T(8,128)S(1)} %pad_maximum_fusion.2.piece0), channel_id=1, source_target_pairs={{0,3},{1,0},{2,1},{3,2},{4,7},{5,4},{6,5},{7,6},{8,11},{9,8},{10,9... | collective-permute-start | bytes 196616 | tf_op jit(solution)/shard_map/ppermute | solution.py:42
  139.7 1.5 collective-permute-start.41
  141.2 1.3 collective-permute-start.42
  142.5 3.4 %collective-permute-done.41.piece2 = f32[2,32,256]{2,1,0:T(8,128)S(1)} collective-permute-done((f32[2,32,256]{2,1,0:T(8,128)S(1)}, f32[2,32,256]{2,1,0:T(8,128)S(1)}, u32[]{:S(2)}, u32[]{:S(2)}) %collective-permute-start.41) | collective-permute-done | bytes 65568 | tf_op jit(solution)/shard_map/ppermute | solution.py:42
  145.9 1.0 collective-permute-done.42.piece3
  146.9 11.2 %factor.1 = (f32[128,256]{1,0:T(8,128)}, f32[256,256]{1,0:T(8,128)}) custom-call(s32[2]{0:T(128)S(1)} %pad_add_fusion.place, f32[2,32,256]{2,1,0:T(8,128)S(1)} %pad_maximum_fusion.2.piece0, f32[2,32,256]{2,1,0:T(8,128)S(1)} %collective-permute-done.40.piece1, f32[2,32,256]{2,1,0:T(8,128)S(1)} %collective-permute-done.41.piece2, ...), custom_call_target="tpu_custom_call" | custom-call | tf_op jit(solution)/shard_map/factor/pallas_call | solution.py:246
  (67 shorter events, 12.2 us)
Async XLA Ops:
  0.6 6.8 %collective-permute-start.2 = (bf16[128,256]{1,0:T(8,128)(2,1)}, bf16[128,256]{1,0:T(8,128)(2,1)S(1)}, u32[]{:S(2)}, u32[]{:S(2)}) collective-permute-start(bf16[128,256]{1,0:T(8,128)(2,1)} %param.9), channel_id=1, source_target_pairs={{0,16},{8,24},{16,32},{24,40},{32,48},{40,56},{48,0},{56,8},{64,80... | collective-permute-start | bytes 196616 | tf_op jit(solution)/shard_map/ppermute | solution.py:34
  2.2 6.0 %collective-permute-start.1 = (bf16[128,256]{1,0:T(8,128)(2,1)}, bf16[128,256]{1,0:T(8,128)(2,1)S(1)}, u32[]{:S(2)}, u32[]{:S(2)}) collective-permute-start(bf16[128,256]{1,0:T(8,128)(2,1)} %param.9), channel_id=1, source_target_pairs={{0,32},{8,40},{16,48},{24,56},{32,0},{40,8},{48,16},{56,24},{64,96... | collective-permute-start | bytes 196616 | tf_op jit(solution)/shard_map/ppermute | solution.py:34
  5.0 4.5 %collective-permute-start = (bf16[128,256]{1,0:T(8,128)(2,1)}, bf16[128,256]{1,0:T(8,128)(2,1)S(1)}, u32[]{:S(2)}, u32[]{:S(2)}) collective-permute-start(bf16[128,256]{1,0:T(8,128)(2,1)} %param.9), channel_id=1, source_target_pairs={{0,48},{8,56},{16,0},{24,8},{32,16},{40,24},{48,32},{56,40},{64,11... | collective-permute-start | bytes 196616 | tf_op jit(solution)/shard_map/ppermute | solution.py:34
  5.5 10.3 %collective-permute-start.14 = (bf16[128,256]{1,0:T(8,128)(2,1)}, bf16[128,256]{1,0:T(8,128)(2,1)S(1)}, u32[]{:S(2)}, u32[]{:S(2)}) collective-permute-start(bf16[128,256]{1,0:T(8,128)(2,1)} %param.9), channel_id=1, source_target_pairs={{0,4},{1,5},{2,6},{3,7},{4,0},{5,1},{6,2},{7,3},{8,12},{9,13},{10,... | collective-permute-start | bytes 196616 | tf_op jit(solution)/shard_map/ppermute | solution.py:46
  10.4 26.1 %collective-permute-start.3 = (bf16[4,128,256]{2,1,0:T(8,128)(2,1)S(1)}, bf16[4,128,256]{2,1,0:T(8,128)(2,1)S(1)}, u32[]{:S(2)}, u32[]{:S(2)}) collective-permute-start(bf16[4,128,256]{2,1,0:T(8,128)(2,1)S(1)} %pad_maximum_fusion.refs_0_), channel_id=1, source_target_pairs={{0,192},{8,200},{16,208},{24,216},{32,224},{40,232},{48,240},{56,2... | collective-permute-start | bytes 786440 | tf_op jit(solution)/shard_map/ppermute | solution.py:30
  16.6 7.0 %collective-permute-start.15 = (bf16[2,128,256]{2,1,0:T(8,128)(2,1)S(1)}, bf16[2,128,256]{2,1,0:T(8,128)(2,1)S(1)}, u32[]{:S(2)}, u32[]{:S(2)}) collective-permute-start(bf16[2,128,256]{2,1,0:T(8,128)(2,1)S(1)} %pad_maximum_fusion.1.refs_0_), channel_id=1, source_target_pairs={{0,3},{1,0},{2,1},{3,2},{4,7},{5,4},{6,5},{7,6},{8,11},{9,8},{10,9... | collective-permute-start | bytes 393224 | tf_op jit(solution)/shard_map/ppermute | solution.py:42
  19.7 6.6 %collective-permute-start.16 = (bf16[2,128,256]{2,1,0:T(8,128)(2,1)S(1)}, bf16[2,128,256]{2,1,0:T(8,128)(2,1)S(1)}, u32[]{:S(2)}, u32[]{:S(2)}) collective-permute-start(bf16[2,128,256]{2,1,0:T(8,128)(2,1)S(1)} %pad_maximum_fusion.1.refs_0_), channel_id=1, source_target_pairs={{0,2},{1,3},{2,0},{3,1},{4,6},{5,7},{6,4},{7,5},{8,10},{9,11},{10,... | collective-permute-start | bytes 393224 | tf_op jit(solution)/shard_map/ppermute | solution.py:42
  20.3 16.2 %collective-permute-start.17 = (bf16[2,128,256]{2,1,0:T(8,128)(2,1)S(1)}, bf16[2,128,256]{2,1,0:T(8,128)(2,1)S(1)}, u32[]{:S(2)}, u32[]{:S(2)}) collective-permute-start(bf16[2,128,256]{2,1,0:T(8,128)(2,1)S(1)} %pad_maximum_fusion.1.refs_0_), channel_id=1, source_target_pairs={{0,1},{1,2},{2,3},{3,0},{4,5},{5,6},{6,7},{7,4},{8,9},{9,10},{10,1... | collective-permute-start | bytes 393224 | tf_op jit(solution)/shard_map/ppermute | solution.py:42
  21.3 22.1 %collective-permute-start.4 = (bf16[4,128,256]{2,1,0:T(8,128)(2,1)S(1)}, bf16[4,128,256]{2,1,0:T(8,128)(2,1)S(1)}, u32[]{:S(2)}, u32[]{:S(2)}) collective-permute-start(bf16[4,128,256]{2,1,0:T(8,128)(2,1)S(1)} %pad_maximum_fusion.refs_0_), channel_id=1, source_target_pairs={{0,128},{8,136},{16,144},{24,152},{32,160},{40,168},{48,176},{56,1... | collective-permute-start | bytes 786440 | tf_op jit(solution)/shard_map/ppermute | solution.py:30
  23.6 19.9 %collective-permute-start.5 = (bf16[4,128,256]{2,1,0:T(8,128)(2,1)S(1)}, bf16[4,128,256]{2,1,0:T(8,128)(2,1)S(1)}, u32[]{:S(2)}, u32[]{:S(2)}) collective-permute-start(bf16[4,128,256]{2,1,0:T(8,128)(2,1)S(1)} %pad_maximum_fusion.refs_0_), channel_id=1, source_target_pairs={{0,64},{8,72},{16,80},{24,88},{32,96},{40,104},{48,112},{56,120},{... | collective-permute-start | bytes 786440 | tf_op jit(solution)/shard_map/ppermute | solution.py:30
  26.3 17.7 %collective-permute-start.6 = (bf16[4,128,256]{2,1,0:T(8,128)(2,1)S(1)}, bf16[4,128,256]{2,1,0:T(8,128)(2,1)S(1)}, u32[]{:S(2)}, u32[]{:S(2)}) collective-permute-start(bf16[4,128,256]{2,1,0:T(8,128)(2,1)S(1)} %pad_maximum_fusion.refs_0_), channel_id=1, source_target_pairs={{0,8},{8,0},{16,24},{24,16},{32,40},{40,32},{48,56},{56,48},{64,72... | collective-permute-start | bytes 786440 | tf_op jit(solution)/shard_map/ppermute | solution.py:38
  36.5 7.6 %collective-permute-start.7 = (bf16[4,128,256]{2,1,0:T(8,128)(2,1)S(1)}, bf16[4,128,256]{2,1,0:T(8,128)(2,1)S(1)}, u32[]{:S(2)}, u32[]{:S(2)}) collective-permute-start(bf16[4,128,256]{2,1,0:T(8,128)(2,1)S(1)} %collective-permute-done.3.refs_1_), channel_id=1, source_target_pairs={{0,8},{8,0},{16,24},{24,16},{32,40},{40,32},{48,56},{56,48},{64,72... | collective-permute-start | bytes 786440 | tf_op jit(solution)/shard_map/ppermute | solution.py:38
  36.5 1.6 %copy-start = (bf16[1,64,128,128]{3,2,1,0:T(8,128)(2,1)S(1)}, bf16[1,64,128,128]{3,2,1,0:T(8,128)(2,1)}, u32[]{:S(2)}) copy-start(bf16[1,64,128,128]{3,2,1,0:T(8,128)(2,1)} %param.5) | copy-start | bytes 6291460
  38.1 0.7 copy-start.1
  38.7 0.7 copy-start.2
  42.6 9.2 %collective-permute-start.21 = (f32[4,128,256]{2,1,0:T(8,128)S(1)}, f32[4,128,256]{2,1,0:T(8,128)S(1)}, u32[]{:S(2)}, u32[]{:S(2)}) collective-permute-start(f32[4,128,256]{2,1,0:T(8,128)S(1)} %get-tuple-element.23), channel_id=1, source_target_pairs={{0,8},{8,0},{16,24},{24,16},{32,40},{40,32},{48,56},{56,48},{64,72... | collective-permute-start | bytes 1572872 | tf_op jit(solution)/shard_map/ppermute | solution.py:38
  43.4 1.9 %collective-permute-start.8 = (bf16[4,128,256]{2,1,0:T(8,128)(2,1)S(1)}, bf16[4,128,256]{2,1,0:T(8,128)(2,1)S(1)}, u32[]{:S(2)}, u32[]{:S(2)}) collective-permute-start(bf16[4,128,256]{2,1,0:T(8,128)(2,1)S(1)} %collective-permute-done.4.refs_2_), channel_id=1, source_target_pairs={{0,8},{8,0},{16,24},{24,16},{32,40},{40,32},{48,56},{56,48},{64,72... | collective-permute-start | bytes 786440 | tf_op jit(solution)/shard_map/ppermute | solution.py:38
  43.6 2.2 %collective-permute-start.9 = (bf16[4,128,256]{2,1,0:T(8,128)(2,1)S(1)}, bf16[4,128,256]{2,1,0:T(8,128)(2,1)S(1)}, u32[]{:S(2)}, u32[]{:S(2)}) collective-permute-start(bf16[4,128,256]{2,1,0:T(8,128)(2,1)S(1)} %collective-permute-done.5.refs_3_), channel_id=1, source_target_pairs={{0,8},{8,0},{16,24},{24,16},{32,40},{40,32},{48,56},{56,48},{64,72... | collective-permute-start | bytes 786440 | tf_op jit(solution)/shard_map/ppermute | solution.py:38
  44.0 11.0 %collective-permute-start.23 = (f32[4,128,256]{2,1,0:T(8,128)S(1)}, f32[4,128,256]{2,1,0:T(8,128)S(1)}, u32[]{:S(2)}, u32[]{:S(2)}) collective-permute-start(f32[4,128,256]{2,1,0:T(8,128)S(1)} %get-tuple-element.25), channel_id=1, source_target_pairs={{0,8},{8,0},{16,24},{24,16},{32,40},{40,32},{48,56},{56,48},{64,72... | collective-permute-start | bytes 1572872 | tf_op jit(solution)/shard_map/ppermute | solution.py:38
  44.1 11.1 %collective-permute-start.19 = (f32[4,128,256]{2,1,0:T(8,128)S(1)}, f32[4,128,256]{2,1,0:T(8,128)S(1)}, u32[]{:S(2)}, u32[]{:S(2)}) collective-permute-start(f32[4,128,256]{2,1,0:T(8,128)S(1)} %get-tuple-element.21), channel_id=1, source_target_pairs={{0,8},{8,0},{16,24},{24,16},{32,40},{40,32},{48,56},{56,48},{64,72... | collective-permute-start | bytes 1572872 | tf_op jit(solution)/shard_map/ppermute | solution.py:38
  48.3 10.4 %collective-permute-start.11 = (f32[2,128,256]{2,1,0:T(8,128)S(1)}, f32[2,128,256]{2,1,0:T(8,128)S(1)}, u32[]{:S(2)}, u32[]{:S(2)}) collective-permute-start(f32[2,128,256]{2,1,0:T(8,128)S(1)} %get-tuple-element.16), channel_id=1, source_target_pairs={{0,1},{1,2},{2,3},{3,0},{4,5},{5,6},{6,7},{7,4},{8,9},{9,10},{10,1... | collective-permute-start | bytes 786440 | tf_op jit(solution)/shard_map/ppermute | solution.py:42
  51.2 12.4 %collective-permute-start.12 = (f32[2,128,256]{2,1,0:T(8,128)S(1)}, f32[2,128,256]{2,1,0:T(8,128)S(1)}, u32[]{:S(2)}, u32[]{:S(2)}) collective-permute-start(f32[2,128,256]{2,1,0:T(8,128)S(1)} %get-tuple-element.17), channel_id=1, source_target_pairs={{0,3},{1,0},{2,1},{3,2},{4,7},{5,4},{6,5},{7,6},{8,11},{9,8},{10,9... | collective-permute-start | bytes 786440 | tf_op jit(solution)/shard_map/ppermute | solution.py:42
  51.8 15.5 %collective-permute-start.10 = (f32[2,128,256]{2,1,0:T(8,128)S(1)}, f32[2,128,256]{2,1,0:T(8,128)S(1)}, u32[]{:S(2)}, u32[]{:S(2)}) collective-permute-start(f32[2,128,256]{2,1,0:T(8,128)S(1)} %get-tuple-element.15), channel_id=1, source_target_pairs={{0,2},{1,3},{2,0},{3,1},{4,6},{5,7},{6,4},{7,5},{8,10},{9,11},{10,... | collective-permute-start | bytes 786440 | tf_op jit(solution)/shard_map/ppermute | solution.py:42
  54.9 12.5 %collective-permute-start.18 = (f32[4,128,256]{2,1,0:T(8,128)S(1)}, f32[4,128,256]{2,1,0:T(8,128)S(1)}, u32[]{:S(2)}, u32[]{:S(2)}) collective-permute-start(f32[4,128,256]{2,1,0:T(8,128)S(1)} %get-tuple-element.19), channel_id=1, source_target_pairs={{0,8},{8,0},{16,24},{24,16},{32,40},{40,32},{48,56},{56,48},{64,72... | collective-permute-start | bytes 1572872 | tf_op jit(solution)/shard_map/ppermute | solution.py:38
  55.1 15.3 %collective-permute-start.22 = (f32[4,128,256]{2,1,0:T(8,128)S(1)}, f32[4,128,256]{2,1,0:T(8,128)S(1)}, u32[]{:S(2)}, u32[]{:S(2)}) collective-permute-start(f32[4,128,256]{2,1,0:T(8,128)S(1)} %add.112), channel_id=1, source_target_pairs={{0,16},{8,24},{16,32},{24,40},{32,48},{40,56},{48,0},{56,8},{64,80... | collective-permute-start | bytes 1572872 | tf_op jit(solution)/shard_map/ppermute | solution.py:34
  58.6 14.9 %collective-permute-start.24 = (f32[4,128,256]{2,1,0:T(8,128)S(1)}, f32[4,128,256]{2,1,0:T(8,128)S(1)}, u32[]{:S(2)}, u32[]{:S(2)}) collective-permute-start(f32[4,128,256]{2,1,0:T(8,128)S(1)} %add.113), channel_id=1, source_target_pairs={{0,48},{8,56},{16,0},{24,8},{32,16},{40,24},{48,32},{56,40},{64,11... | collective-permute-start | bytes 1572872 | tf_op jit(solution)/shard_map/ppermute | solution.py:34
  63.6 20.8 %collective-permute-start.20 = (f32[4,128,256]{2,1,0:T(8,128)S(1)}, f32[4,128,256]{2,1,0:T(8,128)S(1)}, u32[]{:S(2)}, u32[]{:S(2)}) collective-permute-start(f32[4,128,256]{2,1,0:T(8,128)S(1)} %add.110), channel_id=1, source_target_pairs={{0,32},{8,40},{16,48},{24,56},{32,0},{40,8},{48,16},{56,24},{64,96... | collective-permute-start | bytes 1572872 | tf_op jit(solution)/shard_map/ppermute | solution.py:34
  67.3 24.9 %collective-permute-start.13 = (f32[128,256]{1,0:T(8,128)S(1)}, f32[128,256]{1,0:T(8,128)S(1)}, u32[]{:S(2)}, u32[]{:S(2)}) collective-permute-start(f32[128,256]{1,0:T(8,128)S(1)} %slice_bitcast_fusion.4), channel_id=1, source_target_pairs={{0,4},{1,5},{2,6},{3,7},{4,0},{5,1},{6,2},{7,3},{8,12},{9,13},{10,... | collective-permute-start | bytes 393224 | tf_op jit(solution)/shard_map/ppermute | solution.py:46
  84.6 10.3 %collective-permute-start.25 = (f32[128,256]{1,0:T(8,128)S(1)}, f32[128,256]{1,0:T(8,128)S(1)}, u32[]{:S(2)}, u32[]{:S(2)}) collective-permute-start(f32[128,256]{1,0:T(8,128)S(1)} %get-tuple-element.28), channel_id=1, source_target_pairs={{0,128},{8,136},{16,144},{24,152},{32,160},{40,168},{48,176},{56,1... | collective-permute-start | bytes 393224 | tf_op jit(solution)/shard_map/ppermute | solution.py:30
  88.0 9.6 %collective-permute-start.26 = (f32[128,256]{1,0:T(8,128)S(1)}, f32[128,256]{1,0:T(8,128)S(1)}, u32[]{:S(2)}, u32[]{:S(2)}) collective-permute-start(f32[128,256]{1,0:T(8,128)S(1)} %get-tuple-element.27), channel_id=1, source_target_pairs={{0,64},{8,72},{16,80},{24,88},{32,96},{40,104},{48,112},{56,120},{... | collective-permute-start | bytes 393224 | tf_op jit(solution)/shard_map/ppermute | solution.py:30
  92.0 6.6 %collective-permute-start.27 = (f32[128,256]{1,0:T(8,128)S(1)}, f32[128,256]{1,0:T(8,128)S(1)}, u32[]{:S(2)}, u32[]{:S(2)}) collective-permute-start(f32[128,256]{1,0:T(8,128)S(1)} %get-tuple-element.26), channel_id=1, source_target_pairs={{0,192},{8,200},{16,208},{24,216},{32,224},{40,232},{48,240},{56,2... | collective-permute-start | bytes 393224 | tf_op jit(solution)/shard_map/ppermute | solution.py:30
  99.1 1.4 collective-permute-start.28
  100.6 10.3 %collective-permute-start.30 = (f32[32,256]{1,0:T(8,128)S(1)}, f32[32,256]{1,0:T(8,128)S(1)}, u32[]{:S(2)}, u32[]{:S(2)}) collective-permute-start(f32[32,256]{1,0:T(8,128)S(1)} %get-tuple-element.31), channel_id=1, source_target_pairs={{0,1},{1,2},{2,3},{3,0},{4,5},{5,6},{6,7},{7,4},{8,9},{9,10},{10,1... | collective-permute-start | bytes 98312 | tf_op jit(solution)/shard_map/ppermute | solution.py:42
  106.3 4.6 %collective-permute-start.31 = (f32[32,256]{1,0:T(8,128)S(1)}, f32[32,256]{1,0:T(8,128)S(1)}, u32[]{:S(2)}, u32[]{:S(2)}) collective-permute-start(f32[32,256]{1,0:T(8,128)S(1)} %get-tuple-element.30), channel_id=1, source_target_pairs={{0,3},{1,0},{2,1},{3,2},{4,7},{5,4},{6,5},{7,6},{8,11},{9,8},{10,9... | collective-permute-start | bytes 98312 | tf_op jit(solution)/shard_map/ppermute | solution.py:42
  106.3 6.4 %collective-permute-start.29 = (f32[32,256]{1,0:T(8,128)S(1)}, f32[32,256]{1,0:T(8,128)S(1)}, u32[]{:S(2)}, u32[]{:S(2)}) collective-permute-start(f32[32,256]{1,0:T(8,128)S(1)} %get-tuple-element.29), channel_id=1, source_target_pairs={{0,2},{1,3},{2,0},{3,1},{4,6},{5,7},{6,4},{7,5},{8,10},{9,11},{10,... | collective-permute-start | bytes 98312 | tf_op jit(solution)/shard_map/ppermute | solution.py:42
  112.7 4.0 %collective-permute-start.33 = (f32[32,256]{1,0:T(8,128)S(1)}, f32[32,256]{1,0:T(8,128)S(1)}, u32[]{:S(2)}, u32[]{:S(2)}) collective-permute-start(f32[32,256]{1,0:T(8,128)S(1)} %add_add_fusion.4), channel_id=1, source_target_pairs={{0,16},{8,24},{16,32},{24,40},{32,48},{40,56},{48,0},{56,8},{64,80... | collective-permute-start | bytes 98312 | tf_op jit(solution)/shard_map/ppermute | solution.py:34
  112.8 4.0 %collective-permute-start.34 = (f32[32,256]{1,0:T(8,128)S(1)}, f32[32,256]{1,0:T(8,128)S(1)}, u32[]{:S(2)}, u32[]{:S(2)}) collective-permute-start(f32[32,256]{1,0:T(8,128)S(1)} %add_add_fusion.4), channel_id=1, source_target_pairs={{0,48},{8,56},{16,0},{24,8},{32,16},{40,24},{48,32},{56,40},{64,11... | collective-permute-start | bytes 98312 | tf_op jit(solution)/shard_map/ppermute | solution.py:34
  114.8 5.4 %collective-permute-start.32 = (f32[32,256]{1,0:T(8,128)S(1)}, f32[32,256]{1,0:T(8,128)S(1)}, u32[]{:S(2)}, u32[]{:S(2)}) collective-permute-start(f32[32,256]{1,0:T(8,128)S(1)} %add_add_fusion.4), channel_id=1, source_target_pairs={{0,32},{8,40},{16,48},{24,56},{32,0},{40,8},{48,16},{56,24},{64,96... | collective-permute-start | bytes 98312 | tf_op jit(solution)/shard_map/ppermute | solution.py:34
  120.3 4.0 %collective-permute-start.35 = (f32[32,256]{1,0:T(8,128)S(1)}, f32[32,256]{1,0:T(8,128)S(1)}, u32[]{:S(2)}, u32[]{:S(2)}) collective-permute-start(f32[32,256]{1,0:T(8,128)S(1)} %add_add_fusion.3), channel_id=1, source_target_pairs={{0,4},{1,5},{2,6},{3,7},{4,0},{5,1},{6,2},{7,3},{8,12},{9,13},{10,... | collective-permute-start | bytes 98312 | tf_op jit(solution)/shard_map/ppermute | solution.py:46
  124.3 9.4 %collective-permute-start.37 = (f32[32,256]{1,0:T(8,128)S(1)}, f32[32,256]{1,0:T(8,128)S(1)}, u32[]{:S(2)}, u32[]{:S(2)}) collective-permute-start(f32[32,256]{1,0:T(8,128)S(1)} %add.136), channel_id=1, source_target_pairs={{0,64},{8,72},{16,80},{24,88},{32,96},{40,104},{48,112},{56,120},{... | collective-permute-start | bytes 98312 | tf_op jit(solution)/shard_map/ppermute | solution.py:30
  126.5 7.3 %collective-permute-start.38 = (f32[32,256]{1,0:T(8,128)S(1)}, f32[32,256]{1,0:T(8,128)S(1)}, u32[]{:S(2)}, u32[]{:S(2)}) collective-permute-start(f32[32,256]{1,0:T(8,128)S(1)} %add.136), channel_id=1, source_target_pairs={{0,192},{8,200},{16,208},{24,216},{32,224},{40,232},{48,240},{56,2... | collective-permute-start | bytes 98312 | tf_op jit(solution)/shard_map/ppermute | solution.py:30
  128.4 7.8 %collective-permute-start.36 = (f32[32,256]{1,0:T(8,128)S(1)}, f32[32,256]{1,0:T(8,128)S(1)}, u32[]{:S(2)}, u32[]{:S(2)}) collective-permute-start(f32[32,256]{1,0:T(8,128)S(1)} %add.136), channel_id=1, source_target_pairs={{0,128},{8,136},{16,144},{24,152},{32,160},{40,168},{48,176},{56,1... | collective-permute-start | bytes 98312 | tf_op jit(solution)/shard_map/ppermute | solution.py:30
  136.3 1.3 collective-permute-start.39
  137.6 5.0 %collective-permute-start.40 = (f32[2,32,256]{2,1,0:T(8,128)S(1)}, f32[2,32,256]{2,1,0:T(8,128)S(1)}, u32[]{:S(2)}, u32[]{:S(2)}) collective-permute-start(f32[2,32,256]{2,1,0:T(8,128)S(1)} %pad_maximum_fusion.2.piece0), channel_id=1, source_target_pairs={{0,3},{1,0},{2,1},{3,2},{4,7},{5,4},{6,5},{7,6},{8,11},{9,8},{10,9... | collective-permute-start | bytes 196616 | tf_op jit(solution)/shard_map/ppermute | solution.py:42
  139.7 6.2 %collective-permute-start.41 = (f32[2,32,256]{2,1,0:T(8,128)S(1)}, f32[2,32,256]{2,1,0:T(8,128)S(1)}, u32[]{:S(2)}, u32[]{:S(2)}) collective-permute-start(f32[2,32,256]{2,1,0:T(8,128)S(1)} %pad_maximum_fusion.2.piece0), channel_id=1, source_target_pairs={{0,2},{1,3},{2,0},{3,1},{4,6},{5,7},{6,4},{7,5},{8,10},{9,11},{10,... | collective-permute-start | bytes 196616 | tf_op jit(solution)/shard_map/ppermute | solution.py:42
  141.2 5.7 %collective-permute-start.42 = (f32[2,32,256]{2,1,0:T(8,128)S(1)}, f32[2,32,256]{2,1,0:T(8,128)S(1)}, u32[]{:S(2)}, u32[]{:S(2)}) collective-permute-start(f32[2,32,256]{2,1,0:T(8,128)S(1)} %pad_maximum_fusion.2.piece0), channel_id=1, source_target_pairs={{0,1},{1,2},{2,3},{3,0},{4,5},{5,6},{6,7},{7,4},{8,9},{9,10},{10,1... | collective-permute-start | bytes 196616 | tf_op jit(solution)/shard_map/ppermute | solution.py:42
where the time goes:
time: 159 us; the launch traced here: 158 us
  starting transfers between devices  73.1 us (46%)
  waiting for transfers between devices  60.9 us (38%)
  Pallas kernels  16.9 us (11%)
  local copies, waits for them, and re-layouts  2.98 us (2%)
  other arithmetic  2.36 us (1%)
    ppermute x12, starting transfers between devices, to_y(): lax.ppermute(v, 'col', [(col_at(zl, y), col_at(zl, y + k)) for zl in rang...  26.5 us
    ppermute x9, starting transfers between devices, to_z(): return lax.ppermute(v, 'row', row_pairs(lambda z, x, c: (z + k, x, c)))  25.5 us
    ppermute x9, waiting for transfers between devices, to_x(): return lax.ppermute(v, 'row', row_pairs(lambda z, x, c: (z, x + k, c)))  23.3 us
    ppermute x9, waiting for transfers between devices, to_z(): return lax.ppermute(v, 'row', row_pairs(lambda z, x, c: (z + k, x, c)))  19.2 us
    ppermute x9, starting transfers between devices, to_x(): return lax.ppermute(v, 'row', row_pairs(lambda z, x, c: (z, x + k, c)))  15.1 us
    ppermute x12, waiting for transfers between devices, to_y(): lax.ppermute(v, 'col', [(col_at(zl, y), col_at(zl, y + k)) for zl in rang...  12.5 us
    pallas_call x1, Pallas kernels, factor_and_basis(): pl.pallas_call(factor_kernel, out_shape=(jax.ShapeDtypeStruct((edge, size...  11.2 us
    pallas_call x2, Pallas kernels, products_of(): pl.pallas_call(kernel, out_shape=(jax.ShapeDtypeStruct((out_blocks, edge,...  5.69 us
  transfers between devices with their start and end apart: 43, of which 25 were waited for; matrix products, arithmetic and copies ran while one was open for 1% of the time, Pallas kernels for 4%

commit v1 on v0

--- a/solution.py
+++ b/solution.py
@@ -12,6 +12,7 @@
 F32 = jnp.float32
 BLOCK, SUB, LANES = 64, 8, 128
 STEP = SUB
+CHUNK = 8
 
 
 def row_at(z, x, c):
@@ -42,8 +43,14 @@
     return lax.ppermute(v, "col", [(col_at(zl, y), col_at(zl, y + k)) for zl in range(N_ZL) for y in range(N_Y)])
 
 
+def to_col(v, k, flip):
+    return lax.ppermute(
+        v, "col", [(col_at(zl, y), col_at(zl ^ flip, y + k)) for zl in range(N_ZL) for y in range(N_Y)]
+    )
+
+
 def to_zl(v):
-    return lax.ppermute(v, "col", [(col_at(zl, y), col_at(1 - zl, y)) for zl in range(N_ZL) for y in range(N_Y)])
+    return to_col(v, 0, 1)
 
 
 def ring_sum(parts):
@@ -69,77 +76,100 @@
         lax.fori_loop(0, size, one, 0)
 
 
-def slot_loop(counts, rows, cols, blocks, add):
-    live = counts[0, 0]
+def slot_loop(table, blocks, tiles, sems, prepare, add):
+    live = table[2, 0]
+    chunks = (live + CHUNK - 1) // CHUNK
+
+    def fetch(n):
+        return pltpu.make_async_copy(
+            blocks.at[pl.ds(n * CHUNK, CHUNK)], tiles.at[pl.ds(n * CHUNK, CHUNK)], sems.at[n]
+        )
+
+    def start(n, carry):
+        fetch(n).start()
+        return carry
 
     def visit(s):
-        i, j = rows[0, s], cols[0, s]
+        i, j = table[0, s], table[1, s]
         q = jnp.where(s < live, jnp.where(i == j, 0.5, 1.0), 0.0)
-        tile = jnp.where(q > 0.0, blocks[s].astype(F32) * q, 0.0).astype(jnp.bfloat16)
+        tile = jnp.where(q > 0.0, tiles[s].astype(F32) * q, 0.0).astype(jnp.bfloat16)
         add(tile, i >> 5, j & (N_ROW - 1))
 
-    def group(g, carry):
-        for u in range(4):
-            visit(g * 4 + u)
-        return carry
-
-    lax.fori_loop(0, (live + 3) // 4, group, 0)
-
-
-def row_spot(place, rp):
-    return ((rp - place[1]) & 3) * N_ZL + ((rp >> 2) ^ (place[1] >> 2))
-
-
-def col_spot(place, cp):
-    r = place[0]
+    def chunk(n, carry):
+        fetch(n).wait()
+
+        def group(g, inner):
+            for u in range(4):
+                visit(n * CHUNK + g * 4 + u)
+            return inner
+
+        return lax.fori_loop(0, CHUNK // 4, group, carry)
+
+    lax.fori_loop(0, chunks, start, 0)
+    prepare()
+    lax.fori_loop(0, chunks, chunk, 0)
+
+
+def row_spot(table, rp):
+    c = table[3, 1]
+    return ((rp - c) & 3) * N_ZL + ((rp ^ c) >> 2)
+
+
+def col_spot(table, cp):
+    r = table[3, 0]
     zk, xk, cx = ((cp >> 3) - (r >> 3)) & 3, ((cp >> 1) - (r >> 1)) & 3, (cp ^ r) & 1
     return cx * N_X * N_ZH, xk, zk
 
 
-def mirror_kernel(place, counts, rows, cols, blocks, *refs):
-    pieces, outs, vectors, acc = refs[:N_Y], refs[N_Y:-2], refs[-2], refs[-1]
-    clear(acc)
-    for k, piece in enumerate(pieces):
-        vectors[k * N_ZL : (k + 1) * N_ZL] = piece[...]
+def mirror_kernel(table, blocks, *refs):
+    pieces, outs, (vectors, acc, tiles, sems) = refs[:N_Y], refs[N_Y:-4], refs[-4:]
+
+    def prepare():
+        clear(acc)
+        for k, piece in enumerate(pieces):
+            vectors[k * N_ZL : (k + 1) * N_ZL] = piece[...]
 
     def add(tile, rp, cp):
-        base, xk, zk = col_spot(place, cp)
+        base, xk, zk = col_spot(table, cp)
         acc[base + xk * N_ZH + zk] += lax.dot_general(
-            tile, vectors[row_spot(place, rp)], (((0,), (0,)), ((), ())), preferred_element_type=F32
+            tile, vectors[row_spot(table, rp)], (((0,), (0,)), ((), ())), preferred_element_type=F32
         )
 
-    slot_loop(counts, rows, cols, blocks, add)
+    slot_loop(table, blocks, tiles, sems, prepare, add)
     hand_out(acc, outs)
 
 
-def direct_kernel(place, counts, rows, cols, blocks, *refs):
+def direct_kernel(table, blocks, *refs):
     n = N_CORE * N_ZH
-    pieces, outs, vectors, acc = refs[:n], refs[n : n + N_Y], refs[-2], refs[-1]
-    clear(acc)
-    for k, piece in enumerate(pieces):
-        vectors[k * N_X : (k + 1) * N_X] = piece[...]
+    pieces, outs, (vectors, acc, tiles, sems) = refs[:n], refs[n:-4], refs[-4:]
+
+    def prepare():
+        clear(acc)
+        for k, piece in enumerate(pieces):
+            vectors[k * N_X : (k + 1) * N_X] = piece[...]
 
     def add(tile, rp, cp):
-        base, xk, zk = col_spot(place, cp)
-        acc[row_spot(place, rp)] += jnp.dot(tile, vectors[base + zk * N_X + xk], preferred_element_type=F32)
-
-    slot_loop(counts, rows, cols, blocks, add)
+        base, xk, zk = col_spot(table, cp)
+        acc[row_spot(table, rp)] += jnp.dot(tile, vectors[base + zk * N_X + xk], preferred_element_type=F32)
+
+    slot_loop(table, blocks, tiles, sems, prepare, add)
     hand_out(acc, outs)
 
 
-def products_of(kernel, scalars, blocks, pieces, n_out, out_blocks):
+def products_of(kernel, table, blocks, pieces, n_out, out_blocks):
     edge, width = pieces[0].shape[1:]
-    smem = pl.BlockSpec(memory_space=pltpu.SMEM)
     vmem = pl.BlockSpec(memory_space=pltpu.VMEM)
     n_in = len(pieces) * pieces[0].shape[0]
     return pl.pallas_call(
         kernel,
         out_shape=(jax.ShapeDtypeStruct((out_blocks, edge, width), F32),) * n_out,
-        in_specs=[smem] * 4 + [vmem] * (1 + len(pieces)),
+        in_specs=[pl.BlockSpec(memory_space=pltpu.SMEM), pl.BlockSpec(memory_space=pltpu.HBM)] + [vmem] * len(pieces),
         out_specs=(vmem,) * n_out,
         scratch_shapes=[
             pltpu.VMEM((n_in, edge, width), jnp.bfloat16),
             pltpu.VMEM((n_out * out_blocks, edge, width), F32),
+            pltpu.VMEM(blocks.shape, blocks.dtype),
+            pltpu.SemaphoreType.DMA((blocks.shape[0] // CHUNK,)),
         ],
         cost_estimate=pl.CostEstimate(
             flops=2 * blocks.shape[0] * edge * edge * width,
@@ -147,7 +177,7 @@
             transcendentals=0,
         ),
         compiler_params=pltpu.CompilerParams(vmem_limit_bytes=16 << 20),
-    )(*scalars, blocks, *pieces)
+    )(table, pltpu.with_memory_space_constraint(blocks, pltpu.HBM), *pieces)
 
 
 def spread(v):
@@ -219,10 +249,10 @@
         set_stage(work, stage, top + BLOCK)
 
 
-def factor_kernel(place, piece0, piece1, piece2, piece3, products, basis, factor, work, stage, done):
+def factor_kernel(table, piece0, piece1, piece2, piece3, products, basis, factor, work, stage, done):
     edge, size = products.shape
     rows = size // (N_CORE * N_Y)
-    my_core, my_y = place[0] & (N_CORE - 1), place[1] & (N_Y - 1)
+    my_core, my_y = table[3, 0] & (N_CORE - 1), table[3, 1] & (N_Y - 1)
     for k, piece in enumerate((piece0, piece1, piece2, piece3)):
         for side in range(N_CORE):
             at = (((my_core + side) & 1) * N_Y + ((my_y + k) & (N_Y - 1))) * rows
@@ -240,7 +270,7 @@
     basis[...] = work[:, size:].T
 
 
-def factor_and_basis(place, pieces, products):
+def factor_and_basis(table, pieces, products):
     edge, size = products.shape
     vmem = pl.BlockSpec(memory_space=pltpu.VMEM)
     return pl.pallas_call(
@@ -251,13 +281,13 @@
         scratch_shapes=[pltpu.VMEM((size, size + edge), F32)] + [pltpu.VMEM((BLOCK, LANES), F32)] * 2,
         compiler_params=pltpu.CompilerParams(vmem_limit_bytes=8 << 20),
         name="factor",
-    )(place, *pieces, products)
-
-
-def gram_pieces(products, place):
+    )(table, *pieces, products)
+
+
+def gram_pieces(products, r, c):
     width = products.shape[1]
     half, piece = width // N_CORE, width // (N_CORE * N_Y)
-    my_core, my_y = place[0] & (N_CORE - 1), place[1] & (N_Y - 1)
+    my_core, my_y = r & (N_CORE - 1), c & (N_Y - 1)
     local = jnp.dot(products.T, products, precision=lax.Precision.HIGHEST, preferred_element_type=F32)
     mine = lax.dynamic_slice_in_dim(local, my_core * half, half, 0)
     other = lax.dynamic_slice_in_dim(local, (1 - my_core) * half, half, 0)
@@ -272,24 +302,30 @@
 
 
 def body(blocks, block_rows, block_cols, counts, trials):
-    place = jnp.stack([lax.axis_index("row"), lax.axis_index("col")]).astype(jnp.int32)
-    scalars = (place, counts, block_rows, block_cols)
+    r, c = lax.axis_index("row").astype(jnp.int32), lax.axis_index("col").astype(jnp.int32)
+    slots = block_rows.shape[1]
+    at = lax.broadcasted_iota(jnp.int32, (1, slots), 1)
+    table = jnp.concatenate(
+        [block_rows, block_cols, jnp.broadcast_to(counts, (1, slots)), jnp.where(at == 0, r, c)], 0
+    )
     first = jnp.stack([trials, to_zl(trials)])
     xs = jnp.stack([trials] + [to_x(trials, -k) for k in range(1, N_X)])
     row_pieces = [first] + [to_y(first, -k) for k in range(1, N_Y)]
     col_pieces = [xs] + [to_z(xs, -k) for k in range(1, N_ZH)]
-    outs = products_of(mirror_kernel, scalars, blocks[0], row_pieces, N_CORE * N_X, N_ZH)
+    outs = products_of(mirror_kernel, table, blocks[0], row_pieces, N_CORE * N_X, N_ZH)
     keep, send = outs[:N_X], outs[N_X:]
     col_pieces = col_pieces + [to_core(v) for v in col_pieces]
-    row_outs = products_of(direct_kernel, scalars, blocks[0], col_pieces, N_Y, N_ZL)
+    row_outs = products_of(direct_kernel, table, blocks[0], col_pieces, N_COL, 1)
     theirs = {k: to_core(send[k]) for k in (1, 3, 2, 0)}
     sent = {k: to_x(keep[k] + theirs[k], k) for k in (1, 3, 2)}
     got = ring_sum([keep[0] + theirs[0]] + [sent[k] for k in range(1, N_X)])
-    rows = ring_sum([row_outs[0]] + [to_y(row_outs[k], k) for k in range(1, N_Y)])
-    row_sum = rows[0] + to_zl(rows[1])
+    got_rows = [row_outs[0]]
+    for n in range(1, N_COL):
+        got_rows.append(to_col(row_outs[n], n // N_ZL, n % N_ZL))
+    row_sum = (ring_sum(got_rows[:4]) + ring_sum(got_rows[4:]))[0]
     col_sum = ring_sum([got[0]] + [to_z(got[k], k) for k in range(1, N_ZH)])
     products = row_sum + col_sum
-    return factor_and_basis(place, gram_pieces(products, place), products)
+    return factor_and_basis(table, gram_pieces(products, r, c), products)
 
 
 def solution(mesh):

time: 159 us -> 161 us (1.013)
  the two profiles are of different devices: /device:TPU:2 before, /device:TPU:70 now
where the time goes in v1:
time: 161 us; the launch traced here: 160 us
  starting transfers between devices  71.3 us (44%)
  waiting for transfers between devices  67.1 us (42%)
  Pallas kernels  16.9 us (10%)
  other arithmetic  3.02 us (2%)
    ppermute x9, waiting for transfers between devices, to_z(): return lax.ppermute(v, 'row', row_pairs(lambda z, x, c: (z + k, x, c)))  35 us
    ppermute x9, starting transfers between devices, to_col(): lax.ppermute(v, 'col', [(col_at(zl, y), col_at(zl ^ flip, y + k)) for zl...  24.4 us
    ppermute x9, starting transfers between devices, to_z(): return lax.ppermute(v, 'row', row_pairs(lambda z, x, c: (z + k, x, c)))  17.9 us
    ppermute x9, starting transfers between devices, to_y(): lax.ppermute(v, 'col', [(col_at(zl, y), col_at(zl, y + k)) for zl in rang...  14.3 us
    ppermute x9, starting transfers between devices, to_x(): return lax.ppermute(v, 'row', row_pairs(lambda z, x, c: (z, x + k, c)))  13.2 us
    ppermute x9, waiting for transfers between devices, to_y(): lax.ppermute(v, 'col', [(col_at(zl, y), col_at(zl, y + k)) for zl in rang...  12.3 us
    pallas_call x1, Pallas kernels, factor_and_basis(): pl.pallas_call(factor_kernel, out_shape=(jax.ShapeDtypeStruct((edge, size...  11.2 us
    ppermute x9, waiting for transfers between devices, to_x(): return lax.ppermute(v, 'row', row_pairs(lambda z, x, c: (z, x + k, c)))  10.9 us
  transfers between devices with their start and end apart: 46, of which 23 were waited for; matrix products, arithmetic and copies ran while one was open for 2% of the time, Pallas kernels for 4%

profile of v1, /device:TPU:70, one launch (start us, length us, event | category | flops | bytes accessed | tf_op | source)
XLA Modules:
  0.0 160.4 jit_solution(12315316003277909058)
XLA Ops:
  0.6 2.0 %collective-permute-start.17 = (bf16[128,256]{1,0:T(8,128)(2,1)}, bf16[128,256]{1,0:T(8,128)(2,1)S(1)}, u32[]{:S(2)}, u32[]{:S(2)}) collective-permute-start(bf16[128,256]{1,0:T(8,128)(2,1)} %param.9), channel_id=1, source_target_pairs={{0,4},{1,5},{2,6},{3,7},{4,0},{5,1},{6,2},{7,3},{8,12},{9,13},{10,... | collective-permute-start | bytes 196616 | tf_op jit(solution)/shard_map/ppermute | solution.py:47
  3.5 1.1 collective-permute-start.1
  4.6 2.1 %collective-permute-start.2 = (bf16[128,256]{1,0:T(8,128)(2,1)}, bf16[128,256]{1,0:T(8,128)(2,1)S(1)}, u32[]{:S(2)}, u32[]{:S(2)}) collective-permute-start(bf16[128,256]{1,0:T(8,128)(2,1)} %param.9), channel_id=1, source_target_pairs={{0,16},{8,24},{16,32},{24,40},{32,48},{40,56},{48,0},{56,8},{64,80... | collective-permute-start | bytes 196616 | tf_op jit(solution)/shard_map/ppermute | solution.py:35
  7.4 0.9 pad_maximum_fusion.1.refs_0_
  8.3 3.1 %collective-permute-start.18 = (bf16[2,128,256]{2,1,0:T(8,128)(2,1)S(1)}, bf16[2,128,256]{2,1,0:T(8,128)(2,1)S(1)}, u32[]{:S(2)}, u32[]{:S(2)}) collective-permute-start(bf16[2,128,256]{2,1,0:T(8,128)(2,1)S(1)} %pad_maximum_fusion.1.refs_0_), channel_id=1, source_target_pairs={{0,3},{1,0},{2,1},{3,2},{4,7},{5,4},{6,5},{7,6},{8,11},{9,8},{10,9... | collective-permute-start | bytes 393224 | tf_op jit(solution)/shard_map/ppermute | solution.py:43
  12.0 1.0 collective-permute-start.20
  13.0 0.9 pad_maximum_fusion.refs_0_
  14.7 1.3 collective-permute-done.18.refs_1_
  15.9 2.2 %collective-permute-done.19.refs_2_ = bf16[2,128,256]{2,1,0:T(8,128)(2,1)S(1)} collective-permute-done((bf16[2,128,256]{2,1,0:T(8,128)(2,1)S(1)}, bf16[2,128,256]{2,1,0:T(8,128)(2,1)S(1)}, u32[]{:S(2)}, u32[]{:S(2)}) %collective-permute-start.19) | collective-permute-done | bytes 131104 | tf_op jit(solution)/shard_map/ppermute | solution.py:43
  18.1 1.4 collective-permute-done.20.refs_3_
  19.5 3.1 %shard_map.69 = (f32[4,128,256]{2,1,0:T(8,128)S(1)}, f32[4,128,256]{2,1,0:T(8,128)S(1)}, f32[4,128,256]{2,1,0:T(8,128)S(1)}, f32[4,128,256]{2,1,0:T(8,128)S(1)},...) custom-call(s32[4,64]{1,0:T(4,128)S(1)} %pad_add_fusion.table, ...), custom_call_target="tpu_custom_call" | custom-call | flops 536870912 | bytes 6815744 | tf_op jit(solution)/shard_map/pallas_call | solution.py:163
  23.2 3.9 %collective-permute-start.4 = (bf16[4,128,256]{2,1,0:T(8,128)(2,1)S(1)}, bf16[4,128,256]{2,1,0:T(8,128)(2,1)S(1)}, u32[]{:S(2)}, u32[]{:S(2)}) collective-permute-start(bf16[4,128,256]{2,1,0:T(8,128)(2,1)S(1)} %pad_maximum_fusion.refs_0_), channel_id=1, source_target_pairs={{0,128},{8,136},{16,144},{24,152},{32,160},{40,168},{48,176},{56,1... | collective-permute-start | bytes 786440 | tf_op jit(solution)/shard_map/ppermute | solution.py:31
  27.7 1.1 collective-permute-start.5
  28.8 13.2 %collective-permute-done.4.refs_2_ = bf16[4,128,256]{2,1,0:T(8,128)(2,1)S(1)} collective-permute-done((bf16[4,128,256]{2,1,0:T(8,128)(2,1)S(1)}, bf16[4,128,256]{2,1,0:T(8,128)(2,1)S(1)}, u32[]{:S(2)}, u32[]{:S(2)}) %collective-permute-start.4) | collective-permute-done | bytes 262176 | tf_op jit(solution)/shard_map/ppermute | solution.py:31
  42.0 4.9 %collective-permute-done.5.refs_3_ = bf16[4,128,256]{2,1,0:T(8,128)(2,1)S(1)} collective-permute-done((bf16[4,128,256]{2,1,0:T(8,128)(2,1)S(1)}, bf16[4,128,256]{2,1,0:T(8,128)(2,1)S(1)}, u32[]{:S(2)}, u32[]{:S(2)}) %collective-permute-start.5) | collective-permute-done | bytes 262176 | tf_op jit(solution)/shard_map/ppermute | solution.py:31
  47.6 2.1 %collective-permute-start.23 = (f32[4,128,256]{2,1,0:T(8,128)S(1)}, f32[4,128,256]{2,1,0:T(8,128)S(1)}, u32[]{:S(2)}, u32[]{:S(2)}) collective-permute-start(f32[4,128,256]{2,1,0:T(8,128)S(1)} %add.122), channel_id=1, source_target_pairs={{0,32},{8,40},{16,48},{24,56},{32,0},{40,8},{48,16},{56,24},{64,96... | collective-permute-start | bytes 1572872 | tf_op jit(solution)/shard_map/ppermute | solution.py:35
  49.9 3.3 %collective-permute-start.25 = (f32[4,128,256]{2,1,0:T(8,128)S(1)}, f32[4,128,256]{2,1,0:T(8,128)S(1)}, u32[]{:S(2)}, u32[]{:S(2)}) collective-permute-start(f32[4,128,256]{2,1,0:T(8,128)S(1)} %add.124), channel_id=1, source_target_pairs={{0,16},{8,24},{16,32},{24,40},{32,48},{40,56},{48,0},{56,8},{64,80... | collective-permute-start | bytes 1572872 | tf_op jit(solution)/shard_map/ppermute | solution.py:35
  53.2 1.5 collective-permute-done.9.refs_7_
  54.7 2.6 %shard_map.68 = (f32[1,128,256]{2,1,0:T(8,128)S(1)}, f32[1,128,256]{2,1,0:T(8,128)S(1)}, f32[1,128,256]{2,1,0:T(8,128)S(1)}, f32[1,128,256]{2,1,0:T(8,128)S(1)},...) custom-call(s32[4,64]{1,0:T(4,128)S(1)} %pad_add_fusion.table, ...), custom_call_target="tpu_custom_call" | custom-call | flops 536870912 | bytes 5242880 | tf_op jit(solution)/shard_map/pallas_call | solution.py:163
  57.5 7.7 %collective-permute-start.11 = (f32[1,128,256]{2,1,0:T(8,128)S(1)}, f32[1,128,256]{2,1,0:T(8,128)S(1)}, u32[]{:S(2)}, u32[]{:S(2)}) collective-permute-start(f32[1,128,256]{2,1,0:T(8,128)S(1)} %get-tuple-element.20), channel_id=1, source_target_pairs={{0,4},{1,5},{2,6},{3,7},{4,0},{5,1},{6,2},{7,3},{8,12},{9,13},{10,... | collective-permute-start | bytes 393224 | tf_op jit(solution)/shard_map/ppermute | solution.py:47
  65.2 3.8 %collective-permute-start.12 = (f32[1,128,256]{2,1,0:T(8,128)S(1)}, f32[1,128,256]{2,1,0:T(8,128)S(1)}, u32[]{:S(2)}, u32[]{:S(2)}) collective-permute-start(f32[1,128,256]{2,1,0:T(8,128)S(1)} %get-tuple-element.21), channel_id=1, source_target_pairs={{0,5},{1,6},{2,7},{3,4},{4,1},{5,2},{6,3},{7,0},{8,13},{9,14},{10,... | collective-permute-start | bytes 393224 | tf_op jit(solution)/shard_map/ppermute | solution.py:47
  69.0 5.8 %collective-permute-done.27 = f32[4,128,256]{2,1,0:T(8,128)S(1)} collective-permute-done((f32[4,128,256]{2,1,0:T(8,128)S(1)}, f32[4,128,256]{2,1,0:T(8,128)S(1)}, u32[]{:S(2)}, u32[]{:S(2)}) %collective-permute-start.27) | collective-permute-done | bytes 524320 | tf_op jit(solution)/shard_map/ppermute | solution.py:35
  74.8 1.8 %collective-permute-start.13 = (f32[1,128,256]{2,1,0:T(8,128)S(1)}, f32[1,128,256]{2,1,0:T(8,128)S(1)}, u32[]{:S(2)}, u32[]{:S(2)}) collective-permute-start(f32[1,128,256]{2,1,0:T(8,128)S(1)} %get-tuple-element.22), channel_id=1, source_target_pairs={{0,2},{1,3},{2,0},{3,1},{4,6},{5,7},{6,4},{7,5},{8,10},{9,11},{10,... | collective-permute-start | bytes 393224 | tf_op jit(solution)/shard_map/ppermute | solution.py:47
  76.6 1.4 collective-permute-start.14
  78.2 6.8 %collective-permute-start.15 = (f32[1,128,256]{2,1,0:T(8,128)S(1)}, f32[1,128,256]{2,1,0:T(8,128)S(1)}, u32[]{:S(2)}, u32[]{:S(2)}) collective-permute-start(f32[1,128,256]{2,1,0:T(8,128)S(1)} %get-tuple-element.24), channel_id=1, source_target_pairs={{0,6},{1,7},{2,4},{3,5},{4,2},{5,3},{6,0},{7,1},{8,14},{9,15},{10,... | collective-permute-start | bytes 393224 | tf_op jit(solution)/shard_map/ppermute | solution.py:47
  85.7 3.5 %collective-permute-start.28 = (f32[128,256]{1,0:T(8,128)S(1)}, f32[128,256]{1,0:T(8,128)S(1)}, u32[]{:S(2)}, u32[]{:S(2)}) collective-permute-start(f32[128,256]{1,0:T(8,128)S(1)} %get-tuple-element.36), channel_id=1, source_target_pairs={{0,128},{8,136},{16,144},{24,152},{32,160},{40,168},{48,176},{56,1... | collective-permute-start | bytes 393224 | tf_op jit(solution)/shard_map/ppermute | solution.py:31
  89.2 1.6 collective-permute-start.29
  90.8 1.7 %collective-permute-start.30 = (f32[128,256]{1,0:T(8,128)S(1)}, f32[128,256]{1,0:T(8,128)S(1)}, u32[]{:S(2)}, u32[]{:S(2)}) collective-permute-start(f32[128,256]{1,0:T(8,128)S(1)} %get-tuple-element.34), channel_id=1, source_target_pairs={{0,192},{8,200},{16,208},{24,216},{32,224},{40,232},{48,240},{56,2... | collective-permute-start | bytes 393224 | tf_op jit(solution)/shard_map/ppermute | solution.py:31
  93.2 11.0 %collective-permute-done.28 = f32[128,256]{1,0:T(8,128)S(1)} collective-permute-done((f32[128,256]{1,0:T(8,128)S(1)}, f32[128,256]{1,0:T(8,128)S(1)}, u32[]{:S(2)}, u32[]{:S(2)}) %collective-permute-start.28) | collective-permute-done | bytes 131104 | tf_op jit(solution)/shard_map/ppermute | solution.py:31
  104.9 1.3 collective-permute-done.31
  106.3 2.1 %collective-permute-start.32 = (f32[32,256]{1,0:T(8,128)S(1)}, f32[32,256]{1,0:T(8,128)S(1)}, u32[]{:S(2)}, u32[]{:S(2)}) collective-permute-start(f32[32,256]{1,0:T(8,128)S(1)} %get-tuple-element.37), channel_id=1, source_target_pairs={{0,2},{1,3},{2,0},{3,1},{4,6},{5,7},{6,4},{7,5},{8,10},{9,11},{10,... | collective-permute-start | bytes 98312 | tf_op jit(solution)/shard_map/ppermute | solution.py:43
  108.3 3.2 %collective-permute-start.34 = (f32[32,256]{1,0:T(8,128)S(1)}, f32[32,256]{1,0:T(8,128)S(1)}, u32[]{:S(2)}, u32[]{:S(2)}) collective-permute-start(f32[32,256]{1,0:T(8,128)S(1)} %get-tuple-element.38), channel_id=1, source_target_pairs={{0,3},{1,0},{2,1},{3,2},{4,7},{5,4},{6,5},{7,6},{8,11},{9,8},{10,9... | collective-permute-start | bytes 98312 | tf_op jit(solution)/shard_map/ppermute | solution.py:43
  111.8 1.7 %collective-permute-done.33 = f32[32,256]{1,0:T(8,128)S(1)} collective-permute-done((f32[32,256]{1,0:T(8,128)S(1)}, f32[32,256]{1,0:T(8,128)S(1)}, u32[]{:S(2)}, u32[]{:S(2)}) %collective-permute-start.33) | collective-permute-done | bytes 32800 | tf_op jit(solution)/shard_map/ppermute | solution.py:43
  113.5 1.3 collective-permute-start.35
  114.7 2.5 %collective-permute-start.36 = (f32[32,256]{1,0:T(8,128)S(1)}, f32[32,256]{1,0:T(8,128)S(1)}, u32[]{:S(2)}, u32[]{:S(2)}) collective-permute-start(f32[32,256]{1,0:T(8,128)S(1)} %add_add_fusion.3), channel_id=1, source_target_pairs={{0,16},{8,24},{16,32},{24,40},{32,48},{40,56},{48,0},{56,8},{64,80... | collective-permute-start | bytes 98312 | tf_op jit(solution)/shard_map/ppermute | solution.py:35
  117.2 1.8 %collective-permute-done.35 = f32[32,256]{1,0:T(8,128)S(1)} collective-permute-done((f32[32,256]{1,0:T(8,128)S(1)}, f32[32,256]{1,0:T(8,128)S(1)}, u32[]{:S(2)}, u32[]{:S(2)}) %collective-permute-start.35) | collective-permute-done | bytes 32800 | tf_op jit(solution)/shard_map/ppermute | solution.py:35
  119.0 3.4 %collective-permute-done.37 = f32[32,256]{1,0:T(8,128)S(1)} collective-permute-done((f32[32,256]{1,0:T(8,128)S(1)}, f32[32,256]{1,0:T(8,128)S(1)}, u32[]{:S(2)}, u32[]{:S(2)}) %collective-permute-start.37) | collective-permute-done | bytes 32800 | tf_op jit(solution)/shard_map/ppermute | solution.py:35
  122.5 4.1 %collective-permute-done.38 = f32[32,256]{1,0:T(8,128)S(1)} collective-permute-done((f32[32,256]{1,0:T(8,128)S(1)}, f32[32,256]{1,0:T(8,128)S(1)}, u32[]{:S(2)}, u32[]{:S(2)}) %collective-permute-start.38) | collective-permute-done | bytes 32800 | tf_op jit(solution)/shard_map/ppermute | solution.py:47
  126.5 3.2 %collective-permute-start.39 = (f32[32,256]{1,0:T(8,128)S(1)}, f32[32,256]{1,0:T(8,128)S(1)}, u32[]{:S(2)}, u32[]{:S(2)}) collective-permute-start(f32[32,256]{1,0:T(8,128)S(1)} %add.148), channel_id=1, source_target_pairs={{0,128},{8,136},{16,144},{24,152},{32,160},{40,168},{48,176},{56,1... | collective-permute-start | bytes 98312 | tf_op jit(solution)/shard_map/ppermute | solution.py:31
  129.7 2.2 %collective-permute-start.40 = (f32[32,256]{1,0:T(8,128)S(1)}, f32[32,256]{1,0:T(8,128)S(1)}, u32[]{:S(2)}, u32[]{:S(2)}) collective-permute-start(f32[32,256]{1,0:T(8,128)S(1)} %add.148), channel_id=1, source_target_pairs={{0,64},{8,72},{16,80},{24,88},{32,96},{40,104},{48,112},{56,120},{... | collective-permute-start | bytes 98312 | tf_op jit(solution)/shard_map/ppermute | solution.py:31
  132.7 1.7 %collective-permute-done.39 = f32[32,256]{1,0:T(8,128)S(1)} collective-permute-done((f32[32,256]{1,0:T(8,128)S(1)}, f32[32,256]{1,0:T(8,128)S(1)}, u32[]{:S(2)}, u32[]{:S(2)}) %collective-permute-start.39) | collective-permute-done | bytes 32800 | tf_op jit(solution)/shard_map/ppermute | solution.py:31
  134.7 3.3 %collective-permute-done.41 = f32[32,256]{1,0:T(8,128)S(1)} collective-permute-done((f32[32,256]{1,0:T(8,128)S(1)}, f32[32,256]{1,0:T(8,128)S(1)}, u32[]{:S(2)}, u32[]{:S(2)}) %collective-permute-start.41) | collective-permute-done | bytes 32800 | tf_op jit(solution)/shard_map/ppermute | solution.py:31
  138.1 1.2 collective-permute-done.42
  139.3 3.4 %collective-permute-start.43 = (f32[2,32,256]{2,1,0:T(8,128)S(1)}, f32[2,32,256]{2,1,0:T(8,128)S(1)}, u32[]{:S(2)}, u32[]{:S(2)}) collective-permute-start(f32[2,32,256]{2,1,0:T(8,128)S(1)} %pad_maximum_fusion.2.piece0), channel_id=1, source_target_pairs={{0,3},{1,0},{2,1},{3,2},{4,7},{5,4},{6,5},{7,6},{8,11},{9,8},{10,9... | collective-permute-start | bytes 196616 | tf_op jit(solution)/shard_map/ppermute | solution.py:43
  142.7 1.0 collective-permute-start.45
  143.6 2.2 %collective-permute-done.43.piece1 = f32[2,32,256]{2,1,0:T(8,128)S(1)} collective-permute-done((f32[2,32,256]{2,1,0:T(8,128)S(1)}, f32[2,32,256]{2,1,0:T(8,128)S(1)}, u32[]{:S(2)}, u32[]{:S(2)}) %collective-permute-start.43) | collective-permute-done | bytes 65568 | tf_op jit(solution)/shard_map/ppermute | solution.py:43
  145.8 3.0 %collective-permute-done.44.piece2 = f32[2,32,256]{2,1,0:T(8,128)S(1)} collective-permute-done((f32[2,32,256]{2,1,0:T(8,128)S(1)}, f32[2,32,256]{2,1,0:T(8,128)S(1)}, u32[]{:S(2)}, u32[]{:S(2)}) %collective-permute-start.44) | collective-permute-done | bytes 65568 | tf_op jit(solution)/shard_map/ppermute | solution.py:43
  149.2 11.2 %factor.1 = (f32[128,256]{1,0:T(8,128)}, f32[256,256]{1,0:T(8,128)}) custom-call(s32[4,64]{1,0:T(4,128)S(1)} %pad_add_fusion.table, f32[2,32,256]{2,1,0:T(8,128)S(1)} %pad_maximum_fusion.2.piece0, f32[2,32,256]{2,1,0:T(8,128)S(1)} %collective-permute-done.43.piece1, f32[2,32,256]{2,1,0:T(8,128)S(1)} %collective-permute-done.44.piece2, ...), custom_call_target="tpu_custom_call" | custom-call | tf_op jit(solution)/shard_map/factor/pallas_call | solution.py:276
  (67 shorter events, 8.7 us)
Async XLA Ops:
  0.6 6.8 %collective-permute-start.17 = (bf16[128,256]{1,0:T(8,128)(2,1)}, bf16[128,256]{1,0:T(8,128)(2,1)S(1)}, u32[]{:S(2)}, u32[]{:S(2)}) collective-permute-start(bf16[128,256]{1,0:T(8,128)(2,1)} %param.9), channel_id=1, source_target_pairs={{0,4},{1,5},{2,6},{3,7},{4,0},{5,1},{6,2},{7,3},{8,12},{9,13},{10,... | collective-permute-start | bytes 196616 | tf_op jit(solution)/shard_map/ppermute | solution.py:47
  2.6 9.4 %collective-permute-start = (bf16[128,256]{1,0:T(8,128)(2,1)}, bf16[128,256]{1,0:T(8,128)(2,1)S(1)}, u32[]{:S(2)}, u32[]{:S(2)}) collective-permute-start(bf16[128,256]{1,0:T(8,128)(2,1)} %param.9), channel_id=1, source_target_pairs={{0,48},{8,56},{16,0},{24,8},{32,16},{40,24},{48,32},{56,40},{64,11... | collective-permute-start | bytes 196616 | tf_op jit(solution)/shard_map/ppermute | solution.py:35
  3.5 9.5 %collective-permute-start.1 = (bf16[128,256]{1,0:T(8,128)(2,1)}, bf16[128,256]{1,0:T(8,128)(2,1)S(1)}, u32[]{:S(2)}, u32[]{:S(2)}) collective-permute-start(bf16[128,256]{1,0:T(8,128)(2,1)} %param.9), channel_id=1, source_target_pairs={{0,32},{8,40},{16,48},{24,56},{32,0},{40,8},{48,16},{56,24},{64,96... | collective-permute-start | bytes 196616 | tf_op jit(solution)/shard_map/ppermute | solution.py:35
  4.6 8.4 %collective-permute-start.2 = (bf16[128,256]{1,0:T(8,128)(2,1)}, bf16[128,256]{1,0:T(8,128)(2,1)S(1)}, u32[]{:S(2)}, u32[]{:S(2)}) collective-permute-start(bf16[128,256]{1,0:T(8,128)(2,1)} %param.9), channel_id=1, source_target_pairs={{0,16},{8,24},{16,32},{24,40},{32,48},{40,56},{48,0},{56,8},{64,80... | collective-permute-start | bytes 196616 | tf_op jit(solution)/shard_map/ppermute | solution.py:35
  8.3 7.7 %collective-permute-start.18 = (bf16[2,128,256]{2,1,0:T(8,128)(2,1)S(1)}, bf16[2,128,256]{2,1,0:T(8,128)(2,1)S(1)}, u32[]{:S(2)}, u32[]{:S(2)}) collective-permute-start(bf16[2,128,256]{2,1,0:T(8,128)(2,1)S(1)} %pad_maximum_fusion.1.refs_0_), channel_id=1, source_target_pairs={{0,3},{1,0},{2,1},{3,2},{4,7},{5,4},{6,5},{7,6},{8,11},{9,8},{10,9... | collective-permute-start | bytes 393224 | tf_op jit(solution)/shard_map/ppermute | solution.py:43
  11.4 6.7 %collective-permute-start.19 = (bf16[2,128,256]{2,1,0:T(8,128)(2,1)S(1)}, bf16[2,128,256]{2,1,0:T(8,128)(2,1)S(1)}, u32[]{:S(2)}, u32[]{:S(2)}) collective-permute-start(bf16[2,128,256]{2,1,0:T(8,128)(2,1)S(1)} %pad_maximum_fusion.1.refs_0_), channel_id=1, source_target_pairs={{0,2},{1,3},{2,0},{3,1},{4,6},{5,7},{6,4},{7,5},{8,10},{9,11},{10,... | collective-permute-start | bytes 393224 | tf_op jit(solution)/shard_map/ppermute | solution.py:43
  12.0 7.5 %collective-permute-start.20 = (bf16[2,128,256]{2,1,0:T(8,128)(2,1)S(1)}, bf16[2,128,256]{2,1,0:T(8,128)(2,1)S(1)}, u32[]{:S(2)}, u32[]{:S(2)}) collective-permute-start(bf16[2,128,256]{2,1,0:T(8,128)(2,1)S(1)} %pad_maximum_fusion.1.refs_0_), channel_id=1, source_target_pairs={{0,1},{1,2},{2,3},{3,0},{4,5},{5,6},{6,7},{7,4},{8,9},{9,10},{10,1... | collective-permute-start | bytes 393224 | tf_op jit(solution)/shard_map/ppermute | solution.py:43
  13.8 13.9 %collective-permute-start.3 = (bf16[4,128,256]{2,1,0:T(8,128)(2,1)S(1)}, bf16[4,128,256]{2,1,0:T(8,128)(2,1)S(1)}, u32[]{:S(2)}, u32[]{:S(2)}) collective-permute-start(bf16[4,128,256]{2,1,0:T(8,128)(2,1)S(1)} %pad_maximum_fusion.refs_0_), channel_id=1, source_target_pairs={{0,192},{8,200},{16,208},{24,216},{32,224},{40,232},{48,240},{56,2... | collective-permute-start | bytes 786440 | tf_op jit(solution)/shard_map/ppermute | solution.py:31
  22.6 24.3 %collective-permute-start.22 = (f32[4,128,256]{2,1,0:T(8,128)S(1)}, f32[4,128,256]{2,1,0:T(8,128)S(1)}, u32[]{:S(2)}, u32[]{:S(2)}) collective-permute-start(f32[4,128,256]{2,1,0:T(8,128)S(1)} %get-tuple-element.29), channel_id=1, source_target_pairs={{0,8},{8,0},{16,24},{24,16},{32,40},{40,32},{48,56},{56,48},{64,72... | collective-permute-start | bytes 1572872 | tf_op jit(solution)/shard_map/ppermute | solution.py:39
  22.7 24.8 %collective-permute-start.26 = (f32[4,128,256]{2,1,0:T(8,128)S(1)}, f32[4,128,256]{2,1,0:T(8,128)S(1)}, u32[]{:S(2)}, u32[]{:S(2)}) collective-permute-start(f32[4,128,256]{2,1,0:T(8,128)S(1)} %get-tuple-element.33), channel_id=1, source_target_pairs={{0,8},{8,0},{16,24},{24,16},{32,40},{40,32},{48,56},{56,48},{64,72... | collective-permute-start | bytes 1572872 | tf_op jit(solution)/shard_map/ppermute | solution.py:39
  23.2 18.8 %collective-permute-start.4 = (bf16[4,128,256]{2,1,0:T(8,128)(2,1)S(1)}, bf16[4,128,256]{2,1,0:T(8,128)(2,1)S(1)}, u32[]{:S(2)}, u32[]{:S(2)}) collective-permute-start(bf16[4,128,256]{2,1,0:T(8,128)(2,1)S(1)} %pad_maximum_fusion.refs_0_), channel_id=1, source_target_pairs={{0,128},{8,136},{16,144},{24,152},{32,160},{40,168},{48,176},{56,1... | collective-permute-start | bytes 786440 | tf_op jit(solution)/shard_map/ppermute | solution.py:31
  27.1 22.7 %collective-permute-start.24 = (f32[4,128,256]{2,1,0:T(8,128)S(1)}, f32[4,128,256]{2,1,0:T(8,128)S(1)}, u32[]{:S(2)}, u32[]{:S(2)}) collective-permute-start(f32[4,128,256]{2,1,0:T(8,128)S(1)} %get-tuple-element.31), channel_id=1, source_target_pairs={{0,8},{8,0},{16,24},{24,16},{32,40},{40,32},{48,56},{56,48},{64,72... | collective-permute-start | bytes 1572872 | tf_op jit(solution)/shard_map/ppermute | solution.py:39
  27.7 19.1 %collective-permute-start.5 = (bf16[4,128,256]{2,1,0:T(8,128)(2,1)S(1)}, bf16[4,128,256]{2,1,0:T(8,128)(2,1)S(1)}, u32[]{:S(2)}, u32[]{:S(2)}) collective-permute-start(bf16[4,128,256]{2,1,0:T(8,128)(2,1)S(1)} %pad_maximum_fusion.refs_0_), channel_id=1, source_target_pairs={{0,64},{8,72},{16,80},{24,88},{32,96},{40,104},{48,112},{56,120},{... | collective-permute-start | bytes 786440 | tf_op jit(solution)/shard_map/ppermute | solution.py:31
  42.0 5.7 %collective-permute-start.6 = (bf16[4,128,256]{2,1,0:T(8,128)(2,1)S(1)}, bf16[4,128,256]{2,1,0:T(8,128)(2,1)S(1)}, u32[]{:S(2)}, u32[]{:S(2)}) collective-permute-start(bf16[4,128,256]{2,1,0:T(8,128)(2,1)S(1)} %pad_maximum_fusion.refs_0_), channel_id=1, source_target_pairs={{0,8},{8,0},{16,24},{24,16},{32,40},{40,32},{48,56},{56,48},{64,72... | collective-permute-start | bytes 786440 | tf_op jit(solution)/shard_map/ppermute | solution.py:39
  46.9 3.0 %collective-permute-start.7 = (bf16[4,128,256]{2,1,0:T(8,128)(2,1)S(1)}, bf16[4,128,256]{2,1,0:T(8,128)(2,1)S(1)}, u32[]{:S(2)}, u32[]{:S(2)}) collective-permute-start(bf16[4,128,256]{2,1,0:T(8,128)(2,1)S(1)} %collective-permute-done.3.refs_1_), channel_id=1, source_target_pairs={{0,8},{8,0},{16,24},{24,16},{32,40},{40,32},{48,56},{56,48},{64,72... | collective-permute-start | bytes 786440 | tf_op jit(solution)/shard_map/ppermute | solution.py:39
  46.9 6.3 %collective-permute-start.8 = (bf16[4,128,256]{2,1,0:T(8,128)(2,1)S(1)}, bf16[4,128,256]{2,1,0:T(8,128)(2,1)S(1)}, u32[]{:S(2)}, u32[]{:S(2)}) collective-permute-start(bf16[4,128,256]{2,1,0:T(8,128)(2,1)S(1)} %collective-permute-done.4.refs_2_), channel_id=1, source_target_pairs={{0,8},{8,0},{16,24},{24,16},{32,40},{40,32},{48,56},{56,48},{64,72... | collective-permute-start | bytes 786440 | tf_op jit(solution)/shard_map/ppermute | solution.py:39
  47.5 10.0 %collective-permute-start.21 = (f32[4,128,256]{2,1,0:T(8,128)S(1)}, f32[4,128,256]{2,1,0:T(8,128)S(1)}, u32[]{:S(2)}, u32[]{:S(2)}) collective-permute-start(f32[4,128,256]{2,1,0:T(8,128)S(1)} %get-tuple-element.27), channel_id=1, source_target_pairs={{0,8},{8,0},{16,24},{24,16},{32,40},{40,32},{48,56},{56,48},{64,72... | collective-permute-start | bytes 1572872 | tf_op jit(solution)/shard_map/ppermute | solution.py:39
  47.6 17.5 %collective-permute-start.23 = (f32[4,128,256]{2,1,0:T(8,128)S(1)}, f32[4,128,256]{2,1,0:T(8,128)S(1)}, u32[]{:S(2)}, u32[]{:S(2)}) collective-permute-start(f32[4,128,256]{2,1,0:T(8,128)S(1)} %add.122), channel_id=1, source_target_pairs={{0,32},{8,40},{16,48},{24,56},{32,0},{40,8},{48,16},{56,24},{64,96... | collective-permute-start | bytes 1572872 | tf_op jit(solution)/shard_map/ppermute | solution.py:35
  49.8 25.0 %collective-permute-start.27 = (f32[4,128,256]{2,1,0:T(8,128)S(1)}, f32[4,128,256]{2,1,0:T(8,128)S(1)}, u32[]{:S(2)}, u32[]{:S(2)}) collective-permute-start(f32[4,128,256]{2,1,0:T(8,128)S(1)} %add.125), channel_id=1, source_target_pairs={{0,48},{8,56},{16,0},{24,8},{32,16},{40,24},{48,32},{56,40},{64,11... | collective-permute-start | bytes 1572872 | tf_op jit(solution)/shard_map/ppermute | solution.py:35
  49.9 26.7 %collective-permute-start.25 = (f32[4,128,256]{2,1,0:T(8,128)S(1)}, f32[4,128,256]{2,1,0:T(8,128)S(1)}, u32[]{:S(2)}, u32[]{:S(2)}) collective-permute-start(f32[4,128,256]{2,1,0:T(8,128)S(1)} %add.124), channel_id=1, source_target_pairs={{0,16},{8,24},{16,32},{24,40},{32,48},{40,56},{48,0},{56,8},{64,80... | collective-permute-start | bytes 1572872 | tf_op jit(solution)/shard_map/ppermute | solution.py:35
  53.2 1.5 collective-permute-start.9
  57.4 20.8 %collective-permute-start.10 = (f32[1,128,256]{2,1,0:T(8,128)S(1)}, f32[1,128,256]{2,1,0:T(8,128)S(1)}, u32[]{:S(2)}, u32[]{:S(2)}) collective-permute-start(f32[1,128,256]{2,1,0:T(8,128)S(1)} %get-tuple-element.19), channel_id=1, source_target_pairs={{0,1},{1,2},{2,3},{3,0},{4,5},{5,6},{6,7},{7,4},{8,9},{9,10},{10,1... | collective-permute-start | bytes 393224 | tf_op jit(solution)/shard_map/ppermute | solution.py:47
  57.5 27.6 %collective-permute-start.11 = (f32[1,128,256]{2,1,0:T(8,128)S(1)}, f32[1,128,256]{2,1,0:T(8,128)S(1)}, u32[]{:S(2)}, u32[]{:S(2)}) collective-permute-start(f32[1,128,256]{2,1,0:T(8,128)S(1)} %get-tuple-element.20), channel_id=1, source_target_pairs={{0,4},{1,5},{2,6},{3,7},{4,0},{5,1},{6,2},{7,3},{8,12},{9,13},{10,... | collective-permute-start | bytes 393224 | tf_op jit(solution)/shard_map/ppermute | solution.py:47
  65.2 20.5 %collective-permute-start.12 = (f32[1,128,256]{2,1,0:T(8,128)S(1)}, f32[1,128,256]{2,1,0:T(8,128)S(1)}, u32[]{:S(2)}, u32[]{:S(2)}) collective-permute-start(f32[1,128,256]{2,1,0:T(8,128)S(1)} %get-tuple-element.21), channel_id=1, source_target_pairs={{0,5},{1,6},{2,7},{3,4},{4,1},{5,2},{6,3},{7,0},{8,13},{9,14},{10,... | collective-permute-start | bytes 393224 | tf_op jit(solution)/shard_map/ppermute | solution.py:47
  74.8 14.4 %collective-permute-start.13 = (f32[1,128,256]{2,1,0:T(8,128)S(1)}, f32[1,128,256]{2,1,0:T(8,128)S(1)}, u32[]{:S(2)}, u32[]{:S(2)}) collective-permute-start(f32[1,128,256]{2,1,0:T(8,128)S(1)} %get-tuple-element.22), channel_id=1, source_target_pairs={{0,2},{1,3},{2,0},{3,1},{4,6},{5,7},{6,4},{7,5},{8,10},{9,11},{10,... | collective-permute-start | bytes 393224 | tf_op jit(solution)/shard_map/ppermute | solution.py:47
  76.6 14.2 %collective-permute-start.14 = (f32[1,128,256]{2,1,0:T(8,128)S(1)}, f32[1,128,256]{2,1,0:T(8,128)S(1)}, u32[]{:S(2)}, u32[]{:S(2)}) collective-permute-start(f32[1,128,256]{2,1,0:T(8,128)S(1)} %get-tuple-element.23), channel_id=1, source_target_pairs={{0,3},{1,0},{2,1},{3,2},{4,7},{5,4},{6,5},{7,6},{8,11},{9,8},{10,9... | collective-permute-start | bytes 393224 | tf_op jit(solution)/shard_map/ppermute | solution.py:47
  78.2 14.2 %collective-permute-start.15 = (f32[1,128,256]{2,1,0:T(8,128)S(1)}, f32[1,128,256]{2,1,0:T(8,128)S(1)}, u32[]{:S(2)}, u32[]{:S(2)}) collective-permute-start(f32[1,128,256]{2,1,0:T(8,128)S(1)} %get-tuple-element.24), channel_id=1, source_target_pairs={{0,6},{1,7},{2,4},{3,5},{4,2},{5,3},{6,0},{7,1},{8,14},{9,15},{10,... | collective-permute-start | bytes 393224 | tf_op jit(solution)/shard_map/ppermute | solution.py:47
  85.1 8.1 %collective-permute-start.16 = (f32[1,128,256]{2,1,0:T(8,128)S(1)}, f32[1,128,256]{2,1,0:T(8,128)S(1)}, u32[]{:S(2)}, u32[]{:S(2)}) collective-permute-start(f32[1,128,256]{2,1,0:T(8,128)S(1)} %get-tuple-element.25), channel_id=1, source_target_pairs={{0,7},{1,4},{2,5},{3,6},{4,3},{5,0},{6,1},{7,2},{8,15},{9,12},{10,... | collective-permute-start | bytes 393224 | tf_op jit(solution)/shard_map/ppermute | solution.py:47
  85.7 18.5 %collective-permute-start.28 = (f32[128,256]{1,0:T(8,128)S(1)}, f32[128,256]{1,0:T(8,128)S(1)}, u32[]{:S(2)}, u32[]{:S(2)}) collective-permute-start(f32[128,256]{1,0:T(8,128)S(1)} %get-tuple-element.36), channel_id=1, source_target_pairs={{0,128},{8,136},{16,144},{24,152},{32,160},{40,168},{48,176},{56,1... | collective-permute-start | bytes 393224 | tf_op jit(solution)/shard_map/ppermute | solution.py:31
  89.2 15.0 %collective-permute-start.29 = (f32[128,256]{1,0:T(8,128)S(1)}, f32[128,256]{1,0:T(8,128)S(1)}, u32[]{:S(2)}, u32[]{:S(2)}) collective-permute-start(f32[128,256]{1,0:T(8,128)S(1)} %get-tuple-element.35), channel_id=1, source_target_pairs={{0,64},{8,72},{16,80},{24,88},{32,96},{40,104},{48,112},{56,120},{... | collective-permute-start | bytes 393224 | tf_op jit(solution)/shard_map/ppermute | solution.py:31
  90.8 13.5 %collective-permute-start.30 = (f32[128,256]{1,0:T(8,128)S(1)}, f32[128,256]{1,0:T(8,128)S(1)}, u32[]{:S(2)}, u32[]{:S(2)}) collective-permute-start(f32[128,256]{1,0:T(8,128)S(1)} %get-tuple-element.34), channel_id=1, source_target_pairs={{0,192},{8,200},{16,208},{24,216},{32,224},{40,232},{48,240},{56,2... | collective-permute-start | bytes 393224 | tf_op jit(solution)/shard_map/ppermute | solution.py:31
  104.8 1.4 collective-permute-start.31
  106.3 5.5 %collective-permute-start.32 = (f32[32,256]{1,0:T(8,128)S(1)}, f32[32,256]{1,0:T(8,128)S(1)}, u32[]{:S(2)}, u32[]{:S(2)}) collective-permute-start(f32[32,256]{1,0:T(8,128)S(1)} %get-tuple-element.37), channel_id=1, source_target_pairs={{0,2},{1,3},{2,0},{3,1},{4,6},{5,7},{6,4},{7,5},{8,10},{9,11},{10,... | collective-permute-start | bytes 98312 | tf_op jit(solution)/shard_map/ppermute | solution.py:43
  108.3 5.1 %collective-permute-start.33 = (f32[32,256]{1,0:T(8,128)S(1)}, f32[32,256]{1,0:T(8,128)S(1)}, u32[]{:S(2)}, u32[]{:S(2)}) collective-permute-start(f32[32,256]{1,0:T(8,128)S(1)} %get-tuple-element.39), channel_id=1, source_target_pairs={{0,1},{1,2},{2,3},{3,0},{4,5},{5,6},{6,7},{7,4},{8,9},{9,10},{10,1... | collective-permute-start | bytes 98312 | tf_op jit(solution)/shard_map/ppermute | solution.py:43
  108.3 5.1 %collective-permute-start.34 = (f32[32,256]{1,0:T(8,128)S(1)}, f32[32,256]{1,0:T(8,128)S(1)}, u32[]{:S(2)}, u32[]{:S(2)}) collective-permute-start(f32[32,256]{1,0:T(8,128)S(1)} %get-tuple-element.38), channel_id=1, source_target_pairs={{0,3},{1,0},{2,1},{3,2},{4,7},{5,4},{6,5},{7,6},{8,11},{9,8},{10,9... | collective-permute-start | bytes 98312 | tf_op jit(solution)/shard_map/ppermute | solution.py:43
  113.5 5.5 %collective-permute-start.35 = (f32[32,256]{1,0:T(8,128)S(1)}, f32[32,256]{1,0:T(8,128)S(1)}, u32[]{:S(2)}, u32[]{:S(2)}) collective-permute-start(f32[32,256]{1,0:T(8,128)S(1)} %add_add_fusion.3), channel_id=1, source_target_pairs={{0,32},{8,40},{16,48},{24,56},{32,0},{40,8},{48,16},{56,24},{64,96... | collective-permute-start | bytes 98312 | tf_op jit(solution)/shard_map/ppermute | solution.py:35
  114.7 4.2 %collective-permute-start.36 = (f32[32,256]{1,0:T(8,128)S(1)}, f32[32,256]{1,0:T(8,128)S(1)}, u32[]{:S(2)}, u32[]{:S(2)}) collective-permute-start(f32[32,256]{1,0:T(8,128)S(1)} %add_add_fusion.3), channel_id=1, source_target_pairs={{0,16},{8,24},{16,32},{24,40},{32,48},{40,56},{48,0},{56,8},{64,80... | collective-permute-start | bytes 98312 | tf_op jit(solution)/shard_map/ppermute | solution.py:35
  117.2 5.1 %collective-permute-start.37 = (f32[32,256]{1,0:T(8,128)S(1)}, f32[32,256]{1,0:T(8,128)S(1)}, u32[]{:S(2)}, u32[]{:S(2)}) collective-permute-start(f32[32,256]{1,0:T(8,128)S(1)} %add_add_fusion.3), channel_id=1, source_target_pairs={{0,48},{8,56},{16,0},{24,8},{32,16},{40,24},{48,32},{56,40},{64,11... | collective-permute-start | bytes 98312 | tf_op jit(solution)/shard_map/ppermute | solution.py:35
  122.3 4.2 %collective-permute-start.38 = (f32[32,256]{1,0:T(8,128)S(1)}, f32[32,256]{1,0:T(8,128)S(1)}, u32[]{:S(2)}, u32[]{:S(2)}) collective-permute-start(f32[32,256]{1,0:T(8,128)S(1)} %add_add_fusion.2), channel_id=1, source_target_pairs={{0,4},{1,5},{2,6},{3,7},{4,0},{5,1},{6,2},{7,3},{8,12},{9,13},{10,... | collective-permute-start | bytes 98312 | tf_op jit(solution)/shard_map/ppermute | solution.py:47
  126.5 7.8 %collective-permute-start.39 = (f32[32,256]{1,0:T(8,128)S(1)}, f32[32,256]{1,0:T(8,128)S(1)}, u32[]{:S(2)}, u32[]{:S(2)}) collective-permute-start(f32[32,256]{1,0:T(8,128)S(1)} %add.148), channel_id=1, source_target_pairs={{0,128},{8,136},{16,144},{24,152},{32,160},{40,168},{48,176},{56,1... | collective-permute-start | bytes 98312 | tf_op jit(solution)/shard_map/ppermute | solution.py:31
  129.7 5.0 %collective-permute-start.40 = (f32[32,256]{1,0:T(8,128)S(1)}, f32[32,256]{1,0:T(8,128)S(1)}, u32[]{:S(2)}, u32[]{:S(2)}) collective-permute-start(f32[32,256]{1,0:T(8,128)S(1)} %add.148), channel_id=1, source_target_pairs={{0,64},{8,72},{16,80},{24,88},{32,96},{40,104},{48,112},{56,120},{... | collective-permute-start | bytes 98312 | tf_op jit(solution)/shard_map/ppermute | solution.py:31
  131.9 6.1 %collective-permute-start.41 = (f32[32,256]{1,0:T(8,128)S(1)}, f32[32,256]{1,0:T(8,128)S(1)}, u32[]{:S(2)}, u32[]{:S(2)}) collective-permute-start(f32[32,256]{1,0:T(8,128)S(1)} %add.148), channel_id=1, source_target_pairs={{0,192},{8,200},{16,208},{24,216},{32,224},{40,232},{48,240},{56,2... | collective-permute-start | bytes 98312 | tf_op jit(solution)/shard_map/ppermute | solution.py:31
  138.0 1.3 collective-permute-start.42
  139.3 6.5 %collective-permute-start.43 = (f32[2,32,256]{2,1,0:T(8,128)S(1)}, f32[2,32,256]{2,1,0:T(8,128)S(1)}, u32[]{:S(2)}, u32[]{:S(2)}) collective-permute-start(f32[2,32,256]{2,1,0:T(8,128)S(1)} %pad_maximum_fusion.2.piece0), channel_id=1, source_target_pairs={{0,3},{1,0},{2,1},{3,2},{4,7},{5,4},{6,5},{7,6},{8,11},{9,8},{10,9... | collective-permute-start | bytes 196616 | tf_op jit(solution)/shard_map/ppermute | solution.py:43
  142.7 6.1 %collective-permute-start.44 = (f32[2,32,256]{2,1,0:T(8,128)S(1)}, f32[2,32,256]{2,1,0:T(8,128)S(1)}, u32[]{:S(2)}, u32[]{:S(2)}) collective-permute-start(f32[2,32,256]{2,1,0:T(8,128)S(1)} %pad_maximum_fusion.2.piece0), channel_id=1, source_target_pairs={{0,2},{1,3},{2,0},{3,1},{4,6},{5,7},{6,4},{7,5},{8,10},{9,11},{10,... | collective-permute-start | bytes 196616 | tf_op jit(solution)/shard_map/ppermute | solution.py:43
  142.7 6.5 %collective-permute-start.45 = (f32[2,32,256]{2,1,0:T(8,128)S(1)}, f32[2,32,256]{2,1,0:T(8,128)S(1)}, u32[]{:S(2)}, u32[]{:S(2)}) collective-permute-start(f32[2,32,256]{2,1,0:T(8,128)S(1)} %pad_maximum_fusion.2.piece0), channel_id=1, source_target_pairs={{0,1},{1,2},{2,3},{3,0},{4,5},{5,6},{6,7},{7,4},{8,9},{9,10},{10,1... | collective-permute-start | bytes 196616 | tf_op jit(solution)/shard_map/ppermute | solution.py:43

commit v2 on v1

--- a/solution.py
+++ b/solution.py
@@ -43,14 +43,8 @@
     return lax.ppermute(v, "col", [(col_at(zl, y), col_at(zl, y + k)) for zl in range(N_ZL) for y in range(N_Y)])
 
 
-def to_col(v, k, flip):
-    return lax.ppermute(
-        v, "col", [(col_at(zl, y), col_at(zl ^ flip, y + k)) for zl in range(N_ZL) for y in range(N_Y)]
-    )
-
-
 def to_zl(v):
-    return to_col(v, 0, 1)
+    return lax.ppermute(v, "col", [(col_at(zl, y), col_at(1 - zl, y)) for zl in range(N_ZL) for y in range(N_Y)])
 
 
 def ring_sum(parts):
@@ -118,7 +112,7 @@
 def col_spot(table, cp):
     r = table[3, 0]
     zk, xk, cx = ((cp >> 3) - (r >> 3)) & 3, ((cp >> 1) - (r >> 1)) & 3, (cp ^ r) & 1
-    return cx * N_X * N_ZH, xk, zk
+    return cx * N_X * N_ZH + xk * N_ZH + zk
 
 
 def mirror_kernel(table, blocks, *refs):
@@ -130,8 +124,7 @@
             vectors[k * N_ZL : (k + 1) * N_ZL] = piece[...]
 
     def add(tile, rp, cp):
-        base, xk, zk = col_spot(table, cp)
-        acc[base + xk * N_ZH + zk] += lax.dot_general(
+        acc[col_spot(table, cp)] += lax.dot_general(
             tile, vectors[row_spot(table, rp)], (((0,), (0,)), ((), ())), preferred_element_type=F32
         )
 
@@ -140,17 +133,16 @@
 
 
 def direct_kernel(table, blocks, *refs):
-    n = N_CORE * N_ZH
+    n = N_CORE * N_X
     pieces, outs, (vectors, acc, tiles, sems) = refs[:n], refs[n:-4], refs[-4:]
 
     def prepare():
         clear(acc)
         for k, piece in enumerate(pieces):
-            vectors[k * N_X : (k + 1) * N_X] = piece[...]
+            vectors[k * N_ZH : (k + 1) * N_ZH] = piece[...]
 
     def add(tile, rp, cp):
-        base, xk, zk = col_spot(table, cp)
-        acc[row_spot(table, rp)] += jnp.dot(tile, vectors[base + zk * N_X + xk], preferred_element_type=F32)
+        acc[row_spot(table, rp)] += jnp.dot(tile, vectors[col_spot(table, cp)], preferred_element_type=F32)
 
     slot_loop(table, blocks, tiles, sems, prepare, add)
     hand_out(acc, outs)
@@ -309,20 +301,18 @@
         [block_rows, block_cols, jnp.broadcast_to(counts, (1, slots)), jnp.where(at == 0, r, c)], 0
     )
     first = jnp.stack([trials, to_zl(trials)])
-    xs = jnp.stack([trials] + [to_x(trials, -k) for k in range(1, N_X)])
+    zs = jnp.stack([trials] + [to_z(trials, -k) for k in range(1, N_ZH)])
     row_pieces = [first] + [to_y(first, -k) for k in range(1, N_Y)]
-    col_pieces = [xs] + [to_z(xs, -k) for k in range(1, N_ZH)]
+    col_pieces = [zs] + [to_x(zs, -k) for k in range(1, N_X)]
     outs = products_of(mirror_kernel, table, blocks[0], row_pieces, N_CORE * N_X, N_ZH)
     keep, send = outs[:N_X], outs[N_X:]
     col_pieces = col_pieces + [to_core(v) for v in col_pieces]
-    row_outs = products_of(direct_kernel, table, blocks[0], col_pieces, N_COL, 1)
+    row_outs = products_of(direct_kernel, table, blocks[0], col_pieces, N_Y, N_ZL)
     theirs = {k: to_core(send[k]) for k in (1, 3, 2, 0)}
     sent = {k: to_x(keep[k] + theirs[k], k) for k in (1, 3, 2)}
     got = ring_sum([keep[0] + theirs[0]] + [sent[k] for k in range(1, N_X)])
-    got_rows = [row_outs[0]]
-    for n in range(1, N_COL):
-        got_rows.append(to_col(row_outs[n], n // N_ZL, n % N_ZL))
-    row_sum = (ring_sum(got_rows[:4]) + ring_sum(got_rows[4:]))[0]
+    rows = ring_sum([row_outs[0]] + [to_y(row_outs[k], k) for k in range(1, N_Y)])
+    row_sum = rows[0] + to_zl(rows[1])
     col_sum = ring_sum([got[0]] + [to_z(got[k], k) for k in range(1, N_ZH)])
     products = row_sum + col_sum
     return factor_and_basis(table, gram_pieces(products, r, c), products)

time: 161 us -> 155 us (0.963)
  the two profiles are of different devices: /device:TPU:70 before, /device:TPU:2 now
where the time goes in v2:
time: 155 us; the launch traced here: 153 us
  starting transfers between devices  74 us (48%)
  waiting for transfers between devices  54.6 us (35%)
  Pallas kernels  19 us (12%)
  other arithmetic  3.06 us (2%)
    ppermute x12, starting transfers between devices, to_y(): lax.ppermute(v, 'col', [(col_at(zl, y), col_at(zl, y + k)) for zl in rang...  26.5 us
    ppermute x9, starting transfers between devices, to_z(): return lax.ppermute(v, 'row', row_pairs(lambda z, x, c: (z + k, x, c)))  24.4 us
    ppermute x9, waiting for transfers between devices, to_x(): return lax.ppermute(v, 'row', row_pairs(lambda z, x, c: (z, x + k, c)))  22.8 us
    ppermute x9, starting transfers between devices, to_x(): return lax.ppermute(v, 'row', row_pairs(lambda z, x, c: (z, x + k, c)))  18 us
    ppermute x9, waiting for transfers between devices, to_z(): return lax.ppermute(v, 'row', row_pairs(lambda z, x, c: (z + k, x, c)))  13.1 us
    ppermute x12, waiting for transfers between devices, to_y(): lax.ppermute(v, 'col', [(col_at(zl, y), col_at(zl, y + k)) for zl in rang...  12.2 us
    pallas_call x1, Pallas kernels, factor_and_basis(): pl.pallas_call(factor_kernel, out_shape=(jax.ShapeDtypeStruct((edge, size...  11.2 us
    pallas_call x2, Pallas kernels, products_of(): pl.pallas_call(kernel, out_shape=(jax.ShapeDtypeStruct((out_blocks, edge,...  7.81 us
  transfers between devices with their start and end apart: 43, of which 20 were waited for; matrix products, arithmetic and copies ran while one was open for 2% of the time, Pallas kernels for 5%

profile of v2, /device:TPU:2, one launch (start us, length us, event | category | flops | bytes accessed | tf_op | source)
XLA Modules:
  0.0 152.7 jit_solution(14222096610355866235)
XLA Ops:
  0.6 2.0 %collective-permute-start.14 = (bf16[128,256]{1,0:T(8,128)(2,1)}, bf16[128,256]{1,0:T(8,128)(2,1)S(1)}, u32[]{:S(2)}, u32[]{:S(2)}) collective-permute-start(bf16[128,256]{1,0:T(8,128)(2,1)} %param.9), channel_id=1, source_target_pairs={{0,4},{1,5},{2,6},{3,7},{4,0},{5,1},{6,2},{7,3},{8,12},{9,13},{10,... | collective-permute-start | bytes 196616 | tf_op jit(solution)/shard_map/ppermute | solution.py:47
  2.6 3.3 %collective-permute-start.2 = (bf16[128,256]{1,0:T(8,128)(2,1)}, bf16[128,256]{1,0:T(8,128)(2,1)S(1)}, u32[]{:S(2)}, u32[]{:S(2)}) collective-permute-start(bf16[128,256]{1,0:T(8,128)(2,1)} %param.9), channel_id=1, source_target_pairs={{0,64},{8,72},{16,80},{24,88},{32,96},{40,104},{48,112},{56,120},{... | collective-permute-start | bytes 196616 | tf_op jit(solution)/shard_map/ppermute | solution.py:31
  5.9 4.5 %collective-permute-start.1 = (bf16[128,256]{1,0:T(8,128)(2,1)}, bf16[128,256]{1,0:T(8,128)(2,1)S(1)}, u32[]{:S(2)}, u32[]{:S(2)}) collective-permute-start(bf16[128,256]{1,0:T(8,128)(2,1)} %param.9), channel_id=1, source_target_pairs={{0,128},{8,136},{16,144},{24,152},{32,160},{40,168},{48,176},{56,1... | collective-permute-start | bytes 196616 | tf_op jit(solution)/shard_map/ppermute | solution.py:31
  10.4 2.7 %collective-permute-start = (bf16[128,256]{1,0:T(8,128)(2,1)}, bf16[128,256]{1,0:T(8,128)(2,1)S(1)}, u32[]{:S(2)}, u32[]{:S(2)}) collective-permute-start(bf16[128,256]{1,0:T(8,128)(2,1)} %param.9), channel_id=1, source_target_pairs={{0,192},{8,200},{16,208},{24,216},{32,224},{40,232},{48,240},{56,2... | collective-permute-start | bytes 196616 | tf_op jit(solution)/shard_map/ppermute | solution.py:31
  13.9 3.1 %collective-permute-start.15 = (bf16[2,128,256]{2,1,0:T(8,128)(2,1)S(1)}, bf16[2,128,256]{2,1,0:T(8,128)(2,1)S(1)}, u32[]{:S(2)}, u32[]{:S(2)}) collective-permute-start(bf16[2,128,256]{2,1,0:T(8,128)(2,1)S(1)} %pad_maximum_fusion.1.refs_0_), channel_id=1, source_target_pairs={{0,3},{1,0},{2,1},{3,2},{4,7},{5,4},{6,5},{7,6},{8,11},{9,8},{10,9... | collective-permute-start | bytes 393224 | tf_op jit(solution)/shard_map/ppermute | solution.py:43
  19.3 3.1 %collective-permute-start.16 = (bf16[2,128,256]{2,1,0:T(8,128)(2,1)S(1)}, bf16[2,128,256]{2,1,0:T(8,128)(2,1)S(1)}, u32[]{:S(2)}, u32[]{:S(2)}) collective-permute-start(bf16[2,128,256]{2,1,0:T(8,128)(2,1)S(1)} %pad_maximum_fusion.1.refs_0_), channel_id=1, source_target_pairs={{0,2},{1,3},{2,0},{3,1},{4,6},{5,7},{6,4},{7,5},{8,10},{9,11},{10,... | collective-permute-start | bytes 393224 | tf_op jit(solution)/shard_map/ppermute | solution.py:43
  23.0 2.4 %collective-permute-start.4 = (bf16[4,128,256]{2,1,0:T(8,128)(2,1)S(1)}, bf16[4,128,256]{2,1,0:T(8,128)(2,1)S(1)}, u32[]{:S(2)}, u32[]{:S(2)}) collective-permute-start(bf16[4,128,256]{2,1,0:T(8,128)(2,1)S(1)} %pad_maximum_fusion.refs_0_), channel_id=1, source_target_pairs={{0,32},{8,40},{16,48},{24,56},{32,0},{40,8},{48,16},{56,24},{64,96... | collective-permute-start | bytes 786440 | tf_op jit(solution)/shard_map/ppermute | solution.py:35
  25.4 1.8 %collective-permute-start.5 = (bf16[4,128,256]{2,1,0:T(8,128)(2,1)S(1)}, bf16[4,128,256]{2,1,0:T(8,128)(2,1)S(1)}, u32[]{:S(2)}, u32[]{:S(2)}) collective-permute-start(bf16[4,128,256]{2,1,0:T(8,128)(2,1)S(1)} %pad_maximum_fusion.refs_0_), channel_id=1, source_target_pairs={{0,16},{8,24},{16,32},{24,40},{32,48},{40,56},{48,0},{56,8},{64,80... | collective-permute-start | bytes 786440 | tf_op jit(solution)/shard_map/ppermute | solution.py:35
  28.9 4.2 %shard_map.69 = (f32[4,128,256]{2,1,0:T(8,128)S(1)}, f32[4,128,256]{2,1,0:T(8,128)S(1)}, f32[4,128,256]{2,1,0:T(8,128)S(1)}, f32[4,128,256]{2,1,0:T(8,128)S(1)},...) custom-call(s32[4,64]{1,0:T(4,128)S(1)} %pad_add_fusion.table, ...), custom_call_target="tpu_custom_call" | custom-call | flops 536870912 | bytes 6815744 | tf_op jit(solution)/shard_map/pallas_call | solution.py:155
  33.7 3.3 %collective-permute-done.5.refs_3_ = bf16[4,128,256]{2,1,0:T(8,128)(2,1)S(1)} collective-permute-done((bf16[4,128,256]{2,1,0:T(8,128)(2,1)S(1)}, bf16[4,128,256]{2,1,0:T(8,128)(2,1)S(1)}, u32[]{:S(2)}, u32[]{:S(2)}) %collective-permute-start.5) | collective-permute-done | bytes 262176 | tf_op jit(solution)/shard_map/ppermute | solution.py:35
  38.6 3.6 %shard_map.68 = (f32[2,128,256]{2,1,0:T(8,128)S(1)}, f32[2,128,256]{2,1,0:T(8,128)S(1)}, f32[2,128,256]{2,1,0:T(8,128)S(1)}, f32[2,128,256]{2,1,0:T(8,128)S(1)}) custom-call(s32[4,64]{1,0:T(4,128)S(1)} %pad_add_fusion.table, bf16[64,128,128]{2,1,0:T(8,128)(2,1)} %bitcast.37, bf16[4,128,256]{2,1,0:T(8,128)(2,1)S(1)} %pad_maximum_fusion.refs_0_, ...), custom_call_target="tpu_custom_call" | custom-call | flops 536870912 | bytes 5242880 | tf_op jit(solution)/shard_map/pallas_call | solution.py:155
  42.2 1.0 collective-permute-start.11
  43.3 2.5 %collective-permute-start.12 = (f32[2,128,256]{2,1,0:T(8,128)S(1)}, f32[2,128,256]{2,1,0:T(8,128)S(1)}, u32[]{:S(2)}, u32[]{:S(2)}) collective-permute-start(f32[2,128,256]{2,1,0:T(8,128)S(1)} %get-tuple-element.17), channel_id=1, source_target_pairs={{0,3},{1,0},{2,1},{3,2},{4,7},{5,4},{6,5},{7,6},{8,11},{9,8},{10,9... | collective-permute-start | bytes 786440 | tf_op jit(solution)/shard_map/ppermute | solution.py:43
  45.7 1.1 collective-permute-start.10
  47.1 2.0 %collective-permute-start.22 = (f32[4,128,256]{2,1,0:T(8,128)S(1)}, f32[4,128,256]{2,1,0:T(8,128)S(1)}, u32[]{:S(2)}, u32[]{:S(2)}) collective-permute-start(f32[4,128,256]{2,1,0:T(8,128)S(1)} %add.112), channel_id=1, source_target_pairs={{0,16},{8,24},{16,32},{24,40},{32,48},{40,56},{48,0},{56,8},{64,80... | collective-permute-start | bytes 1572872 | tf_op jit(solution)/shard_map/ppermute | solution.py:35
  49.2 2.9 %collective-permute-done.11 = f32[2,128,256]{2,1,0:T(8,128)S(1)} collective-permute-done((f32[2,128,256]{2,1,0:T(8,128)S(1)}, f32[2,128,256]{2,1,0:T(8,128)S(1)}, u32[]{:S(2)}, u32[]{:S(2)}) %collective-permute-start.11) | collective-permute-done | bytes 262176 | tf_op jit(solution)/shard_map/ppermute | solution.py:43
  52.1 2.3 %collective-permute-start.24 = (f32[4,128,256]{2,1,0:T(8,128)S(1)}, f32[4,128,256]{2,1,0:T(8,128)S(1)}, u32[]{:S(2)}, u32[]{:S(2)}) collective-permute-start(f32[4,128,256]{2,1,0:T(8,128)S(1)} %add.113), channel_id=1, source_target_pairs={{0,48},{8,56},{16,0},{24,8},{32,16},{40,24},{48,32},{56,40},{64,11... | collective-permute-start | bytes 1572872 | tf_op jit(solution)/shard_map/ppermute | solution.py:35
  54.3 2.6 %collective-permute-done.12 = f32[2,128,256]{2,1,0:T(8,128)S(1)} collective-permute-done((f32[2,128,256]{2,1,0:T(8,128)S(1)}, f32[2,128,256]{2,1,0:T(8,128)S(1)}, u32[]{:S(2)}, u32[]{:S(2)}) %collective-permute-start.12) | collective-permute-done | bytes 262176 | tf_op jit(solution)/shard_map/ppermute | solution.py:43
  56.9 4.1 %collective-permute-start.20 = (f32[4,128,256]{2,1,0:T(8,128)S(1)}, f32[4,128,256]{2,1,0:T(8,128)S(1)}, u32[]{:S(2)}, u32[]{:S(2)}) collective-permute-start(f32[4,128,256]{2,1,0:T(8,128)S(1)} %add.110), channel_id=1, source_target_pairs={{0,32},{8,40},{16,48},{24,56},{32,0},{40,8},{48,16},{56,24},{64,96... | collective-permute-start | bytes 1572872 | tf_op jit(solution)/shard_map/ppermute | solution.py:35
  61.2 2.0 %collective-permute-done.22 = f32[4,128,256]{2,1,0:T(8,128)S(1)} collective-permute-done((f32[4,128,256]{2,1,0:T(8,128)S(1)}, f32[4,128,256]{2,1,0:T(8,128)S(1)}, u32[]{:S(2)}, u32[]{:S(2)}) %collective-permute-start.22) | collective-permute-done | bytes 524320 | tf_op jit(solution)/shard_map/ppermute | solution.py:35
  63.3 3.4 %collective-permute-done.24 = f32[4,128,256]{2,1,0:T(8,128)S(1)} collective-permute-done((f32[4,128,256]{2,1,0:T(8,128)S(1)}, f32[4,128,256]{2,1,0:T(8,128)S(1)}, u32[]{:S(2)}, u32[]{:S(2)}) %collective-permute-start.24) | collective-permute-done | bytes 524320 | tf_op jit(solution)/shard_map/ppermute | solution.py:35
  66.7 11.3 %collective-permute-done.20 = f32[4,128,256]{2,1,0:T(8,128)S(1)} collective-permute-done((f32[4,128,256]{2,1,0:T(8,128)S(1)}, f32[4,128,256]{2,1,0:T(8,128)S(1)}, u32[]{:S(2)}, u32[]{:S(2)}) %collective-permute-start.20) | collective-permute-done | bytes 524320 | tf_op jit(solution)/shard_map/ppermute | solution.py:35
  78.2 3.3 %collective-permute-start.25 = (f32[128,256]{1,0:T(8,128)S(1)}, f32[128,256]{1,0:T(8,128)S(1)}, u32[]{:S(2)}, u32[]{:S(2)}) collective-permute-start(f32[128,256]{1,0:T(8,128)S(1)} %get-tuple-element.28), channel_id=1, source_target_pairs={{0,128},{8,136},{16,144},{24,152},{32,160},{40,168},{48,176},{56,1... | collective-permute-start | bytes 393224 | tf_op jit(solution)/shard_map/ppermute | solution.py:31
  81.5 2.1 %collective-permute-start.26 = (f32[128,256]{1,0:T(8,128)S(1)}, f32[128,256]{1,0:T(8,128)S(1)}, u32[]{:S(2)}, u32[]{:S(2)}) collective-permute-start(f32[128,256]{1,0:T(8,128)S(1)} %get-tuple-element.27), channel_id=1, source_target_pairs={{0,64},{8,72},{16,80},{24,88},{32,96},{40,104},{48,112},{56,120},{... | collective-permute-start | bytes 393224 | tf_op jit(solution)/shard_map/ppermute | solution.py:31
  83.6 2.1 %collective-permute-start.27 = (f32[128,256]{1,0:T(8,128)S(1)}, f32[128,256]{1,0:T(8,128)S(1)}, u32[]{:S(2)}, u32[]{:S(2)}) collective-permute-start(f32[128,256]{1,0:T(8,128)S(1)} %get-tuple-element.26), channel_id=1, source_target_pairs={{0,192},{8,200},{16,208},{24,216},{32,224},{40,232},{48,240},{56,2... | collective-permute-start | bytes 393224 | tf_op jit(solution)/shard_map/ppermute | solution.py:31
  85.6 3.1 %collective-permute-done.25 = f32[128,256]{1,0:T(8,128)S(1)} collective-permute-done((f32[128,256]{1,0:T(8,128)S(1)}, f32[128,256]{1,0:T(8,128)S(1)}, u32[]{:S(2)}, u32[]{:S(2)}) %collective-permute-start.25) | collective-permute-done | bytes 131104 | tf_op jit(solution)/shard_map/ppermute | solution.py:31
  88.7 1.9 %collective-permute-done.26 = f32[128,256]{1,0:T(8,128)S(1)} collective-permute-done((f32[128,256]{1,0:T(8,128)S(1)}, f32[128,256]{1,0:T(8,128)S(1)}, u32[]{:S(2)}, u32[]{:S(2)}) %collective-permute-start.26) | collective-permute-done | bytes 131104 | tf_op jit(solution)/shard_map/ppermute | solution.py:31
  90.7 2.7 %collective-permute-done.27 = f32[128,256]{1,0:T(8,128)S(1)} collective-permute-done((f32[128,256]{1,0:T(8,128)S(1)}, f32[128,256]{1,0:T(8,128)S(1)}, u32[]{:S(2)}, u32[]{:S(2)}) %collective-permute-start.27) | collective-permute-done | bytes 131104 | tf_op jit(solution)/shard_map/ppermute | solution.py:31
  93.9 1.3 collective-permute-done.28
  95.3 5.7 %collective-permute-start.30 = (f32[32,256]{1,0:T(8,128)S(1)}, f32[32,256]{1,0:T(8,128)S(1)}, u32[]{:S(2)}, u32[]{:S(2)}) collective-permute-start(f32[32,256]{1,0:T(8,128)S(1)} %get-tuple-element.31), channel_id=1, source_target_pairs={{0,1},{1,2},{2,3},{3,0},{4,5},{5,6},{6,7},{7,4},{8,9},{9,10},{10,1... | collective-permute-start | bytes 98312 | tf_op jit(solution)/shard_map/ppermute | solution.py:43
  101.0 4.4 %collective-permute-start.29 = (f32[32,256]{1,0:T(8,128)S(1)}, f32[32,256]{1,0:T(8,128)S(1)}, u32[]{:S(2)}, u32[]{:S(2)}) collective-permute-start(f32[32,256]{1,0:T(8,128)S(1)} %get-tuple-element.29), channel_id=1, source_target_pairs={{0,2},{1,3},{2,0},{3,1},{4,6},{5,7},{6,4},{7,5},{8,10},{9,11},{10,... | collective-permute-start | bytes 98312 | tf_op jit(solution)/shard_map/ppermute | solution.py:43
  105.4 1.9 %collective-permute-done.29 = f32[32,256]{1,0:T(8,128)S(1)} collective-permute-done((f32[32,256]{1,0:T(8,128)S(1)}, f32[32,256]{1,0:T(8,128)S(1)}, u32[]{:S(2)}, u32[]{:S(2)}) %collective-permute-start.29) | collective-permute-done | bytes 32800 | tf_op jit(solution)/shard_map/ppermute | solution.py:43
  107.4 2.0 %collective-permute-start.34 = (f32[32,256]{1,0:T(8,128)S(1)}, f32[32,256]{1,0:T(8,128)S(1)}, u32[]{:S(2)}, u32[]{:S(2)}) collective-permute-start(f32[32,256]{1,0:T(8,128)S(1)} %add_add_fusion.4), channel_id=1, source_target_pairs={{0,48},{8,56},{16,0},{24,8},{32,16},{40,24},{48,32},{56,40},{64,11... | collective-permute-start | bytes 98312 | tf_op jit(solution)/shard_map/ppermute | solution.py:35
  109.4 2.7 %collective-permute-start.32 = (f32[32,256]{1,0:T(8,128)S(1)}, f32[32,256]{1,0:T(8,128)S(1)}, u32[]{:S(2)}, u32[]{:S(2)}) collective-permute-start(f32[32,256]{1,0:T(8,128)S(1)} %add_add_fusion.4), channel_id=1, source_target_pairs={{0,32},{8,40},{16,48},{24,56},{32,0},{40,8},{48,16},{56,24},{64,96... | collective-permute-start | bytes 98312 | tf_op jit(solution)/shard_map/ppermute | solution.py:35
  112.6 2.3 %collective-permute-done.32 = f32[32,256]{1,0:T(8,128)S(1)} collective-permute-done((f32[32,256]{1,0:T(8,128)S(1)}, f32[32,256]{1,0:T(8,128)S(1)}, u32[]{:S(2)}, u32[]{:S(2)}) %collective-permute-start.32) | collective-permute-done | bytes 32800 | tf_op jit(solution)/shard_map/ppermute | solution.py:35
  114.9 0.9 collective-permute-start.35
  115.8 3.1 %collective-permute-done.35 = f32[32,256]{1,0:T(8,128)S(1)} collective-permute-done((f32[32,256]{1,0:T(8,128)S(1)}, f32[32,256]{1,0:T(8,128)S(1)}, u32[]{:S(2)}, u32[]{:S(2)}) %collective-permute-start.35) | collective-permute-done | bytes 32800 | tf_op jit(solution)/shard_map/ppermute | solution.py:47
  118.9 1.0 collective-permute-start.37
  119.8 3.2 %collective-permute-start.38 = (f32[32,256]{1,0:T(8,128)S(1)}, f32[32,256]{1,0:T(8,128)S(1)}, u32[]{:S(2)}, u32[]{:S(2)}) collective-permute-start(f32[32,256]{1,0:T(8,128)S(1)} %add.136), channel_id=1, source_target_pairs={{0,192},{8,200},{16,208},{24,216},{32,224},{40,232},{48,240},{56,2... | collective-permute-start | bytes 98312 | tf_op jit(solution)/shard_map/ppermute | solution.py:31
  123.0 2.4 %collective-permute-start.36 = (f32[32,256]{1,0:T(8,128)S(1)}, f32[32,256]{1,0:T(8,128)S(1)}, u32[]{:S(2)}, u32[]{:S(2)}) collective-permute-start(f32[32,256]{1,0:T(8,128)S(1)} %add.136), channel_id=1, source_target_pairs={{0,128},{8,136},{16,144},{24,152},{32,160},{40,168},{48,176},{56,1... | collective-permute-start | bytes 98312 | tf_op jit(solution)/shard_map/ppermute | solution.py:31
  125.4 5.4 %collective-permute-done.36 = f32[32,256]{1,0:T(8,128)S(1)} collective-permute-done((f32[32,256]{1,0:T(8,128)S(1)}, f32[32,256]{1,0:T(8,128)S(1)}, u32[]{:S(2)}, u32[]{:S(2)}) %collective-permute-start.36) | collective-permute-done | bytes 32800 | tf_op jit(solution)/shard_map/ppermute | solution.py:31
  130.9 1.2 collective-permute-done.39
  132.1 2.2 %collective-permute-start.40 = (f32[2,32,256]{2,1,0:T(8,128)S(1)}, f32[2,32,256]{2,1,0:T(8,128)S(1)}, u32[]{:S(2)}, u32[]{:S(2)}) collective-permute-start(f32[2,32,256]{2,1,0:T(8,128)S(1)} %pad_maximum_fusion.2.piece0), channel_id=1, source_target_pairs={{0,3},{1,0},{2,1},{3,2},{4,7},{5,4},{6,5},{7,6},{8,11},{9,8},{10,9... | collective-permute-start | bytes 196616 | tf_op jit(solution)/shard_map/ppermute | solution.py:43
  134.3 1.5 collective-permute-start.41
  135.8 1.3 collective-permute-start.42
  137.1 3.4 %collective-permute-done.41.piece2 = f32[2,32,256]{2,1,0:T(8,128)S(1)} collective-permute-done((f32[2,32,256]{2,1,0:T(8,128)S(1)}, f32[2,32,256]{2,1,0:T(8,128)S(1)}, u32[]{:S(2)}, u32[]{:S(2)}) %collective-permute-start.41) | collective-permute-done | bytes 65568 | tf_op jit(solution)/shard_map/ppermute | solution.py:43
  140.5 1.0 collective-permute-done.42.piece3
  141.5 11.2 %factor.1 = (f32[128,256]{1,0:T(8,128)}, f32[256,256]{1,0:T(8,128)}) custom-call(s32[4,64]{1,0:T(4,128)S(1)} %pad_add_fusion.table, f32[2,32,256]{2,1,0:T(8,128)S(1)} %pad_maximum_fusion.2.piece0, f32[2,32,256]{2,1,0:T(8,128)S(1)} %collective-permute-done.40.piece1, f32[2,32,256]{2,1,0:T(8,128)S(1)} %collective-permute-done.41.piece2, ...), custom_call_target="tpu_custom_call" | custom-call | tf_op jit(solution)/shard_map/factor/pallas_call | solution.py:268
  (63 shorter events, 8.9 us)
Async XLA Ops:
  0.6 12.4 %collective-permute-start.14 = (bf16[128,256]{1,0:T(8,128)(2,1)}, bf16[128,256]{1,0:T(8,128)(2,1)S(1)}, u32[]{:S(2)}, u32[]{:S(2)}) collective-permute-start(bf16[128,256]{1,0:T(8,128)(2,1)} %param.9), channel_id=1, source_target_pairs={{0,4},{1,5},{2,6},{3,7},{4,0},{5,1},{6,2},{7,3},{8,12},{9,13},{10,... | collective-permute-start | bytes 196616 | tf_op jit(solution)/shard_map/ppermute | solution.py:47
  2.6 14.4 %collective-permute-start.2 = (bf16[128,256]{1,0:T(8,128)(2,1)}, bf16[128,256]{1,0:T(8,128)(2,1)S(1)}, u32[]{:S(2)}, u32[]{:S(2)}) collective-permute-start(bf16[128,256]{1,0:T(8,128)(2,1)} %param.9), channel_id=1, source_target_pairs={{0,64},{8,72},{16,80},{24,88},{32,96},{40,104},{48,112},{56,120},{... | collective-permute-start | bytes 196616 | tf_op jit(solution)/shard_map/ppermute | solution.py:31
  5.9 11.1 %collective-permute-start.1 = (bf16[128,256]{1,0:T(8,128)(2,1)}, bf16[128,256]{1,0:T(8,128)(2,1)S(1)}, u32[]{:S(2)}, u32[]{:S(2)}) collective-permute-start(bf16[128,256]{1,0:T(8,128)(2,1)} %param.9), channel_id=1, source_target_pairs={{0,128},{8,136},{16,144},{24,152},{32,160},{40,168},{48,176},{56,1... | collective-permute-start | bytes 196616 | tf_op jit(solution)/shard_map/ppermute | solution.py:31
  10.4 6.7 %collective-permute-start = (bf16[128,256]{1,0:T(8,128)(2,1)}, bf16[128,256]{1,0:T(8,128)(2,1)S(1)}, u32[]{:S(2)}, u32[]{:S(2)}) collective-permute-start(bf16[128,256]{1,0:T(8,128)(2,1)} %param.9), channel_id=1, source_target_pairs={{0,192},{8,200},{16,208},{24,216},{32,224},{40,232},{48,240},{56,2... | collective-permute-start | bytes 196616 | tf_op jit(solution)/shard_map/ppermute | solution.py:31
  13.9 11.5 %collective-permute-start.15 = (bf16[2,128,256]{2,1,0:T(8,128)(2,1)S(1)}, bf16[2,128,256]{2,1,0:T(8,128)(2,1)S(1)}, u32[]{:S(2)}, u32[]{:S(2)}) collective-permute-start(bf16[2,128,256]{2,1,0:T(8,128)(2,1)S(1)} %pad_maximum_fusion.1.refs_0_), channel_id=1, source_target_pairs={{0,3},{1,0},{2,1},{3,2},{4,7},{5,4},{6,5},{7,6},{8,11},{9,8},{10,9... | collective-permute-start | bytes 393224 | tf_op jit(solution)/shard_map/ppermute | solution.py:43
  17.9 10.1 %collective-permute-start.3 = (bf16[4,128,256]{2,1,0:T(8,128)(2,1)S(1)}, bf16[4,128,256]{2,1,0:T(8,128)(2,1)S(1)}, u32[]{:S(2)}, u32[]{:S(2)}) collective-permute-start(bf16[4,128,256]{2,1,0:T(8,128)(2,1)S(1)} %pad_maximum_fusion.refs_0_), channel_id=1, source_target_pairs={{0,48},{8,56},{16,0},{24,8},{32,16},{40,24},{48,32},{56,40},{64,11... | collective-permute-start | bytes 786440 | tf_op jit(solution)/shard_map/ppermute | solution.py:35
  19.3 8.7 %collective-permute-start.16 = (bf16[2,128,256]{2,1,0:T(8,128)(2,1)S(1)}, bf16[2,128,256]{2,1,0:T(8,128)(2,1)S(1)}, u32[]{:S(2)}, u32[]{:S(2)}) collective-permute-start(bf16[2,128,256]{2,1,0:T(8,128)(2,1)S(1)} %pad_maximum_fusion.1.refs_0_), channel_id=1, source_target_pairs={{0,2},{1,3},{2,0},{3,1},{4,6},{5,7},{6,4},{7,5},{8,10},{9,11},{10,... | collective-permute-start | bytes 393224 | tf_op jit(solution)/shard_map/ppermute | solution.py:43
  22.3 6.6 %collective-permute-start.17 = (bf16[2,128,256]{2,1,0:T(8,128)(2,1)S(1)}, bf16[2,128,256]{2,1,0:T(8,128)(2,1)S(1)}, u32[]{:S(2)}, u32[]{:S(2)}) collective-permute-start(bf16[2,128,256]{2,1,0:T(8,128)(2,1)S(1)} %pad_maximum_fusion.1.refs_0_), channel_id=1, source_target_pairs={{0,1},{1,2},{2,3},{3,0},{4,5},{5,6},{6,7},{7,4},{8,9},{9,10},{10,1... | collective-permute-start | bytes 393224 | tf_op jit(solution)/shard_map/ppermute | solution.py:43
  23.0 10.2 %collective-permute-start.4 = (bf16[4,128,256]{2,1,0:T(8,128)(2,1)S(1)}, bf16[4,128,256]{2,1,0:T(8,128)(2,1)S(1)}, u32[]{:S(2)}, u32[]{:S(2)}) collective-permute-start(bf16[4,128,256]{2,1,0:T(8,128)(2,1)S(1)} %pad_maximum_fusion.refs_0_), channel_id=1, source_target_pairs={{0,32},{8,40},{16,48},{24,56},{32,0},{40,8},{48,16},{56,24},{64,96... | collective-permute-start | bytes 786440 | tf_op jit(solution)/shard_map/ppermute | solution.py:35
  25.4 11.6 %collective-permute-start.5 = (bf16[4,128,256]{2,1,0:T(8,128)(2,1)S(1)}, bf16[4,128,256]{2,1,0:T(8,128)(2,1)S(1)}, u32[]{:S(2)}, u32[]{:S(2)}) collective-permute-start(bf16[4,128,256]{2,1,0:T(8,128)(2,1)S(1)} %pad_maximum_fusion.refs_0_), channel_id=1, source_target_pairs={{0,16},{8,24},{16,32},{24,40},{32,48},{40,56},{48,0},{56,8},{64,80... | collective-permute-start | bytes 786440 | tf_op jit(solution)/shard_map/ppermute | solution.py:35
  28.0 9.1 %collective-permute-start.6 = (bf16[4,128,256]{2,1,0:T(8,128)(2,1)S(1)}, bf16[4,128,256]{2,1,0:T(8,128)(2,1)S(1)}, u32[]{:S(2)}, u32[]{:S(2)}) collective-permute-start(bf16[4,128,256]{2,1,0:T(8,128)(2,1)S(1)} %pad_maximum_fusion.refs_0_), channel_id=1, source_target_pairs={{0,8},{8,0},{16,24},{24,16},{32,40},{40,32},{48,56},{56,48},{64,72... | collective-permute-start | bytes 786440 | tf_op jit(solution)/shard_map/ppermute | solution.py:39
  28.1 9.5 %collective-permute-start.7 = (bf16[4,128,256]{2,1,0:T(8,128)(2,1)S(1)}, bf16[4,128,256]{2,1,0:T(8,128)(2,1)S(1)}, u32[]{:S(2)}, u32[]{:S(2)}) collective-permute-start(bf16[4,128,256]{2,1,0:T(8,128)(2,1)S(1)} %collective-permute-done.3.refs_1_), channel_id=1, source_target_pairs={{0,8},{8,0},{16,24},{24,16},{32,40},{40,32},{48,56},{56,48},{64,72... | collective-permute-start | bytes 786440 | tf_op jit(solution)/shard_map/ppermute | solution.py:39
  33.1 12.6 %collective-permute-start.21 = (f32[4,128,256]{2,1,0:T(8,128)S(1)}, f32[4,128,256]{2,1,0:T(8,128)S(1)}, u32[]{:S(2)}, u32[]{:S(2)}) collective-permute-start(f32[4,128,256]{2,1,0:T(8,128)S(1)} %get-tuple-element.23), channel_id=1, source_target_pairs={{0,8},{8,0},{16,24},{24,16},{32,40},{40,32},{48,56},{56,48},{64,72... | collective-permute-start | bytes 1572872 | tf_op jit(solution)/shard_map/ppermute | solution.py:39
  33.2 4.4 %collective-permute-start.8 = (bf16[4,128,256]{2,1,0:T(8,128)(2,1)S(1)}, bf16[4,128,256]{2,1,0:T(8,128)(2,1)S(1)}, u32[]{:S(2)}, u32[]{:S(2)}) collective-permute-start(bf16[4,128,256]{2,1,0:T(8,128)(2,1)S(1)} %collective-permute-done.4.refs_2_), channel_id=1, source_target_pairs={{0,8},{8,0},{16,24},{24,16},{32,40},{40,32},{48,56},{56,48},{64,72... | collective-permute-start | bytes 786440 | tf_op jit(solution)/shard_map/ppermute | solution.py:39
  37.1 1.5 %collective-permute-start.9 = (bf16[4,128,256]{2,1,0:T(8,128)(2,1)S(1)}, bf16[4,128,256]{2,1,0:T(8,128)(2,1)S(1)}, u32[]{:S(2)}, u32[]{:S(2)}) collective-permute-start(bf16[4,128,256]{2,1,0:T(8,128)(2,1)S(1)} %collective-permute-done.5.refs_3_), channel_id=1, source_target_pairs={{0,8},{8,0},{16,24},{24,16},{32,40},{40,32},{48,56},{56,48},{64,72... | collective-permute-start | bytes 786440 | tf_op jit(solution)/shard_map/ppermute | solution.py:39
  37.1 9.9 %collective-permute-start.23 = (f32[4,128,256]{2,1,0:T(8,128)S(1)}, f32[4,128,256]{2,1,0:T(8,128)S(1)}, u32[]{:S(2)}, u32[]{:S(2)}) collective-permute-start(f32[4,128,256]{2,1,0:T(8,128)S(1)} %get-tuple-element.25), channel_id=1, source_target_pairs={{0,8},{8,0},{16,24},{24,16},{32,40},{40,32},{48,56},{56,48},{64,72... | collective-permute-start | bytes 1572872 | tf_op jit(solution)/shard_map/ppermute | solution.py:39
  37.6 9.5 %collective-permute-start.19 = (f32[4,128,256]{2,1,0:T(8,128)S(1)}, f32[4,128,256]{2,1,0:T(8,128)S(1)}, u32[]{:S(2)}, u32[]{:S(2)}) collective-permute-start(f32[4,128,256]{2,1,0:T(8,128)S(1)} %get-tuple-element.21), channel_id=1, source_target_pairs={{0,8},{8,0},{16,24},{24,16},{32,40},{40,32},{48,56},{56,48},{64,72... | collective-permute-start | bytes 1572872 | tf_op jit(solution)/shard_map/ppermute | solution.py:39
  42.2 9.8 %collective-permute-start.11 = (f32[2,128,256]{2,1,0:T(8,128)S(1)}, f32[2,128,256]{2,1,0:T(8,128)S(1)}, u32[]{:S(2)}, u32[]{:S(2)}) collective-permute-start(f32[2,128,256]{2,1,0:T(8,128)S(1)} %get-tuple-element.16), channel_id=1, source_target_pairs={{0,1},{1,2},{2,3},{3,0},{4,5},{5,6},{6,7},{7,4},{8,9},{9,10},{10,1... | collective-permute-start | bytes 786440 | tf_op jit(solution)/shard_map/ppermute | solution.py:43
  43.3 13.7 %collective-permute-start.12 = (f32[2,128,256]{2,1,0:T(8,128)S(1)}, f32[2,128,256]{2,1,0:T(8,128)S(1)}, u32[]{:S(2)}, u32[]{:S(2)}) collective-permute-start(f32[2,128,256]{2,1,0:T(8,128)S(1)} %get-tuple-element.17), channel_id=1, source_target_pairs={{0,3},{1,0},{2,1},{3,2},{4,7},{5,4},{6,5},{7,6},{8,11},{9,8},{10,9... | collective-permute-start | bytes 786440 | tf_op jit(solution)/shard_map/ppermute | solution.py:43
  45.7 15.3 %collective-permute-start.10 = (f32[2,128,256]{2,1,0:T(8,128)S(1)}, f32[2,128,256]{2,1,0:T(8,128)S(1)}, u32[]{:S(2)}, u32[]{:S(2)}) collective-permute-start(f32[2,128,256]{2,1,0:T(8,128)S(1)} %get-tuple-element.15), channel_id=1, source_target_pairs={{0,2},{1,3},{2,0},{3,1},{4,6},{5,7},{6,4},{7,5},{8,10},{9,11},{10,... | collective-permute-start | bytes 786440 | tf_op jit(solution)/shard_map/ppermute | solution.py:43
  46.9 14.3 %collective-permute-start.18 = (f32[4,128,256]{2,1,0:T(8,128)S(1)}, f32[4,128,256]{2,1,0:T(8,128)S(1)}, u32[]{:S(2)}, u32[]{:S(2)}) collective-permute-start(f32[4,128,256]{2,1,0:T(8,128)S(1)} %get-tuple-element.19), channel_id=1, source_target_pairs={{0,8},{8,0},{16,24},{24,16},{32,40},{40,32},{48,56},{56,48},{64,72... | collective-permute-start | bytes 1572872 | tf_op jit(solution)/shard_map/ppermute | solution.py:39
  47.1 16.1 %collective-permute-start.22 = (f32[4,128,256]{2,1,0:T(8,128)S(1)}, f32[4,128,256]{2,1,0:T(8,128)S(1)}, u32[]{:S(2)}, u32[]{:S(2)}) collective-permute-start(f32[4,128,256]{2,1,0:T(8,128)S(1)} %add.112), channel_id=1, source_target_pairs={{0,16},{8,24},{16,32},{24,40},{32,48},{40,56},{48,0},{56,8},{64,80... | collective-permute-start | bytes 1572872 | tf_op jit(solution)/shard_map/ppermute | solution.py:35
  52.1 14.6 %collective-permute-start.24 = (f32[4,128,256]{2,1,0:T(8,128)S(1)}, f32[4,128,256]{2,1,0:T(8,128)S(1)}, u32[]{:S(2)}, u32[]{:S(2)}) collective-permute-start(f32[4,128,256]{2,1,0:T(8,128)S(1)} %add.113), channel_id=1, source_target_pairs={{0,48},{8,56},{16,0},{24,8},{32,16},{40,24},{48,32},{56,40},{64,11... | collective-permute-start | bytes 1572872 | tf_op jit(solution)/shard_map/ppermute | solution.py:35
  56.9 21.0 %collective-permute-start.20 = (f32[4,128,256]{2,1,0:T(8,128)S(1)}, f32[4,128,256]{2,1,0:T(8,128)S(1)}, u32[]{:S(2)}, u32[]{:S(2)}) collective-permute-start(f32[4,128,256]{2,1,0:T(8,128)S(1)} %add.110), channel_id=1, source_target_pairs={{0,32},{8,40},{16,48},{24,56},{32,0},{40,8},{48,16},{56,24},{64,96... | collective-permute-start | bytes 1572872 | tf_op jit(solution)/shard_map/ppermute | solution.py:35
  61.1 24.5 %collective-permute-start.13 = (f32[128,256]{1,0:T(8,128)S(1)}, f32[128,256]{1,0:T(8,128)S(1)}, u32[]{:S(2)}, u32[]{:S(2)}) collective-permute-start(f32[128,256]{1,0:T(8,128)S(1)} %slice_bitcast_fusion.4), channel_id=1, source_target_pairs={{0,4},{1,5},{2,6},{3,7},{4,0},{5,1},{6,2},{7,3},{8,12},{9,13},{10,... | collective-permute-start | bytes 393224 | tf_op jit(solution)/shard_map/ppermute | solution.py:47
  78.2 10.5 %collective-permute-start.25 = (f32[128,256]{1,0:T(8,128)S(1)}, f32[128,256]{1,0:T(8,128)S(1)}, u32[]{:S(2)}, u32[]{:S(2)}) collective-permute-start(f32[128,256]{1,0:T(8,128)S(1)} %get-tuple-element.28), channel_id=1, source_target_pairs={{0,128},{8,136},{16,144},{24,152},{32,160},{40,168},{48,176},{56,1... | collective-permute-start | bytes 393224 | tf_op jit(solution)/shard_map/ppermute | solution.py:31
  81.5 9.1 %collective-permute-start.26 = (f32[128,256]{1,0:T(8,128)S(1)}, f32[128,256]{1,0:T(8,128)S(1)}, u32[]{:S(2)}, u32[]{:S(2)}) collective-permute-start(f32[128,256]{1,0:T(8,128)S(1)} %get-tuple-element.27), channel_id=1, source_target_pairs={{0,64},{8,72},{16,80},{24,88},{32,96},{40,104},{48,112},{56,120},{... | collective-permute-start | bytes 393224 | tf_op jit(solution)/shard_map/ppermute | solution.py:31
  83.6 9.7 %collective-permute-start.27 = (f32[128,256]{1,0:T(8,128)S(1)}, f32[128,256]{1,0:T(8,128)S(1)}, u32[]{:S(2)}, u32[]{:S(2)}) collective-permute-start(f32[128,256]{1,0:T(8,128)S(1)} %get-tuple-element.26), channel_id=1, source_target_pairs={{0,192},{8,200},{16,208},{24,216},{32,224},{40,232},{48,240},{56,2... | collective-permute-start | bytes 393224 | tf_op jit(solution)/shard_map/ppermute | solution.py:31
  93.8 1.4 collective-permute-start.28
  95.3 10.1 %collective-permute-start.30 = (f32[32,256]{1,0:T(8,128)S(1)}, f32[32,256]{1,0:T(8,128)S(1)}, u32[]{:S(2)}, u32[]{:S(2)}) collective-permute-start(f32[32,256]{1,0:T(8,128)S(1)} %get-tuple-element.31), channel_id=1, source_target_pairs={{0,1},{1,2},{2,3},{3,0},{4,5},{5,6},{6,7},{7,4},{8,9},{9,10},{10,1... | collective-permute-start | bytes 98312 | tf_op jit(solution)/shard_map/ppermute | solution.py:43
  101.0 4.4 %collective-permute-start.31 = (f32[32,256]{1,0:T(8,128)S(1)}, f32[32,256]{1,0:T(8,128)S(1)}, u32[]{:S(2)}, u32[]{:S(2)}) collective-permute-start(f32[32,256]{1,0:T(8,128)S(1)} %get-tuple-element.30), channel_id=1, source_target_pairs={{0,3},{1,0},{2,1},{3,2},{4,7},{5,4},{6,5},{7,6},{8,11},{9,8},{10,9... | collective-permute-start | bytes 98312 | tf_op jit(solution)/shard_map/ppermute | solution.py:43
  101.0 6.3 %collective-permute-start.29 = (f32[32,256]{1,0:T(8,128)S(1)}, f32[32,256]{1,0:T(8,128)S(1)}, u32[]{:S(2)}, u32[]{:S(2)}) collective-permute-start(f32[32,256]{1,0:T(8,128)S(1)} %get-tuple-element.29), channel_id=1, source_target_pairs={{0,2},{1,3},{2,0},{3,1},{4,6},{5,7},{6,4},{7,5},{8,10},{9,11},{10,... | collective-permute-start | bytes 98312 | tf_op jit(solution)/shard_map/ppermute | solution.py:43
  107.3 4.8 %collective-permute-start.33 = (f32[32,256]{1,0:T(8,128)S(1)}, f32[32,256]{1,0:T(8,128)S(1)}, u32[]{:S(2)}, u32[]{:S(2)}) collective-permute-start(f32[32,256]{1,0:T(8,128)S(1)} %add_add_fusion.4), channel_id=1, source_target_pairs={{0,16},{8,24},{16,32},{24,40},{32,48},{40,56},{48,0},{56,8},{64,80... | collective-permute-start | bytes 98312 | tf_op jit(solution)/shard_map/ppermute | solution.py:35
  107.4 5.1 %collective-permute-start.34 = (f32[32,256]{1,0:T(8,128)S(1)}, f32[32,256]{1,0:T(8,128)S(1)}, u32[]{:S(2)}, u32[]{:S(2)}) collective-permute-start(f32[32,256]{1,0:T(8,128)S(1)} %add_add_fusion.4), channel_id=1, source_target_pairs={{0,48},{8,56},{16,0},{24,8},{32,16},{40,24},{48,32},{56,40},{64,11... | collective-permute-start | bytes 98312 | tf_op jit(solution)/shard_map/ppermute | solution.py:35
  109.4 5.4 %collective-permute-start.32 = (f32[32,256]{1,0:T(8,128)S(1)}, f32[32,256]{1,0:T(8,128)S(1)}, u32[]{:S(2)}, u32[]{:S(2)}) collective-permute-start(f32[32,256]{1,0:T(8,128)S(1)} %add_add_fusion.4), channel_id=1, source_target_pairs={{0,32},{8,40},{16,48},{24,56},{32,0},{40,8},{48,16},{56,24},{64,96... | collective-permute-start | bytes 98312 | tf_op jit(solution)/shard_map/ppermute | solution.py:35
  114.9 4.0 %collective-permute-start.35 = (f32[32,256]{1,0:T(8,128)S(1)}, f32[32,256]{1,0:T(8,128)S(1)}, u32[]{:S(2)}, u32[]{:S(2)}) collective-permute-start(f32[32,256]{1,0:T(8,128)S(1)} %add_add_fusion.3), channel_id=1, source_target_pairs={{0,4},{1,5},{2,6},{3,7},{4,0},{5,1},{6,2},{7,3},{8,12},{9,13},{10,... | collective-permute-start | bytes 98312 | tf_op jit(solution)/shard_map/ppermute | solution.py:47
  118.9 6.6 %collective-permute-start.37 = (f32[32,256]{1,0:T(8,128)S(1)}, f32[32,256]{1,0:T(8,128)S(1)}, u32[]{:S(2)}, u32[]{:S(2)}) collective-permute-start(f32[32,256]{1,0:T(8,128)S(1)} %add.136), channel_id=1, source_target_pairs={{0,64},{8,72},{16,80},{24,88},{32,96},{40,104},{48,112},{56,120},{... | collective-permute-start | bytes 98312 | tf_op jit(solution)/shard_map/ppermute | solution.py:31
  119.8 5.6 %collective-permute-start.38 = (f32[32,256]{1,0:T(8,128)S(1)}, f32[32,256]{1,0:T(8,128)S(1)}, u32[]{:S(2)}, u32[]{:S(2)}) collective-permute-start(f32[32,256]{1,0:T(8,128)S(1)} %add.136), channel_id=1, source_target_pairs={{0,192},{8,200},{16,208},{24,216},{32,224},{40,232},{48,240},{56,2... | collective-permute-start | bytes 98312 | tf_op jit(solution)/shard_map/ppermute | solution.py:31
  123.0 7.8 %collective-permute-start.36 = (f32[32,256]{1,0:T(8,128)S(1)}, f32[32,256]{1,0:T(8,128)S(1)}, u32[]{:S(2)}, u32[]{:S(2)}) collective-permute-start(f32[32,256]{1,0:T(8,128)S(1)} %add.136), channel_id=1, source_target_pairs={{0,128},{8,136},{16,144},{24,152},{32,160},{40,168},{48,176},{56,1... | collective-permute-start | bytes 98312 | tf_op jit(solution)/shard_map/ppermute | solution.py:31
  130.8 1.3 collective-permute-start.39
  132.1 5.0 %collective-permute-start.40 = (f32[2,32,256]{2,1,0:T(8,128)S(1)}, f32[2,32,256]{2,1,0:T(8,128)S(1)}, u32[]{:S(2)}, u32[]{:S(2)}) collective-permute-start(f32[2,32,256]{2,1,0:T(8,128)S(1)} %pad_maximum_fusion.2.piece0), channel_id=1, source_target_pairs={{0,3},{1,0},{2,1},{3,2},{4,7},{5,4},{6,5},{7,6},{8,11},{9,8},{10,9... | collective-permute-start | bytes 196616 | tf_op jit(solution)/shard_map/ppermute | solution.py:43
  134.3 6.2 %collective-permute-start.41 = (f32[2,32,256]{2,1,0:T(8,128)S(1)}, f32[2,32,256]{2,1,0:T(8,128)S(1)}, u32[]{:S(2)}, u32[]{:S(2)}) collective-permute-start(f32[2,32,256]{2,1,0:T(8,128)S(1)} %pad_maximum_fusion.2.piece0), channel_id=1, source_target_pairs={{0,2},{1,3},{2,0},{3,1},{4,6},{5,7},{6,4},{7,5},{8,10},{9,11},{10,... | collective-permute-start | bytes 196616 | tf_op jit(solution)/shard_map/ppermute | solution.py:43
  135.8 5.7 %collective-permute-start.42 = (f32[2,32,256]{2,1,0:T(8,128)S(1)}, f32[2,32,256]{2,1,0:T(8,128)S(1)}, u32[]{:S(2)}, u32[]{:S(2)}) collective-permute-start(f32[2,32,256]{2,1,0:T(8,128)S(1)} %pad_maximum_fusion.2.piece0), channel_id=1, source_target_pairs={{0,1},{1,2},{2,3},{3,0},{4,5},{5,6},{6,7},{7,4},{8,9},{9,10},{10,1... | collective-permute-start | bytes 196616 | tf_op jit(solution)/shard_map/ppermute | solution.py:43

commit v3 on v2

--- a/solution.py
+++ b/solution.py
@@ -13,6 +13,7 @@
 BLOCK, SUB, LANES = 64, 8, 128
 STEP = SUB
 CHUNK = 8
+FIRST = 96
 
 
 def row_at(z, x, c):
@@ -59,15 +60,12 @@
     lax.fori_loop(0, acc.shape[0], one, 0)
 
 
-def hand_out(acc, outs):
-    for k, out in enumerate(outs):
-        size = out.shape[0]
-
-        def one(n, carry):
-            out[n] = acc[k * size + n]
-            return carry
-
-        lax.fori_loop(0, size, one, 0)
+def each(count, one):
+    def step(n, carry):
+        one(n)
+        return carry
+
+    lax.fori_loop(0, count, step, 0)
 
 
 def slot_loop(table, blocks, tiles, sems, prepare, add):
@@ -129,46 +127,65 @@
         )
 
     slot_loop(table, blocks, tiles, sems, prepare, add)
-    hand_out(acc, outs)
+    part = N_X * N_ZH
+    for k in range(N_CORE * N_X):
+
+        def first(n, k=k):
+            outs[k][n] = acc[k * N_ZH + n, :FIRST]
+
+        each(N_ZH, first)
+    for k in range(N_CORE):
+
+        def second(n, k=k):
+            outs[N_CORE * N_X + k][n] = acc[k * part + (n & (N_X - 1)) * N_ZH + n // N_X, FIRST:]
+
+        each(part, second)
 
 
 def direct_kernel(table, blocks, *refs):
-    n = N_CORE * N_X
+    n = N_X + 1
     pieces, outs, (vectors, acc, tiles, sems) = refs[:n], refs[n:-4], refs[-4:]
 
     def prepare():
         clear(acc)
-        for k, piece in enumerate(pieces):
-            vectors[k * N_ZH : (k + 1) * N_ZH] = piece[...]
+        at = 0
+        for piece in pieces:
+            vectors[at : at + piece.shape[0]] = piece[...]
+            at += piece.shape[0]
 
     def add(tile, rp, cp):
         acc[row_spot(table, rp)] += jnp.dot(tile, vectors[col_spot(table, cp)], preferred_element_type=F32)
 
     slot_loop(table, blocks, tiles, sems, prepare, add)
-    hand_out(acc, outs)
-
-
-def products_of(kernel, table, blocks, pieces, n_out, out_blocks):
+    for k, out in enumerate(outs):
+
+        def one(n, k=k, out=out):
+            out[n] = acc[k * N_ZL + n]
+
+        each(N_ZL, one)
+
+
+def products_of(kernel, table, blocks, pieces, outs):
     edge, width = pieces[0].shape[1:]
     vmem = pl.BlockSpec(memory_space=pltpu.VMEM)
-    n_in = len(pieces) * pieces[0].shape[0]
+    n_in, n_acc = (sum(v.shape[0] for v in pieces), sum(n * rows for n, rows in outs) // edge)
     return pl.pallas_call(
         kernel,
-        out_shape=(jax.ShapeDtypeStruct((out_blocks, edge, width), F32),) * n_out,
+        out_shape=tuple(jax.ShapeDtypeStruct((n, rows, width), F32) for n, rows in outs),
         in_specs=[pl.BlockSpec(memory_space=pltpu.SMEM), pl.BlockSpec(memory_space=pltpu.HBM)] + [vmem] * len(pieces),
-        out_specs=(vmem,) * n_out,
+        out_specs=(vmem,) * len(outs),
         scratch_shapes=[
             pltpu.VMEM((n_in, edge, width), jnp.bfloat16),
-            pltpu.VMEM((n_out * out_blocks, edge, width), F32),
+            pltpu.VMEM((n_acc, edge, width), F32),
             pltpu.VMEM(blocks.shape, blocks.dtype),
             pltpu.SemaphoreType.DMA((blocks.shape[0] // CHUNK,)),
         ],
         cost_estimate=pl.CostEstimate(
             flops=2 * blocks.shape[0] * edge * edge * width,
-            bytes_accessed=2 * blocks.size + 2 * n_in * edge * width + 4 * n_out * out_blocks * edge * width,
+            bytes_accessed=2 * blocks.size + 2 * n_in * edge * width + 4 * n_acc * edge * width,
             transcendentals=0,
         ),
-        compiler_params=pltpu.CompilerParams(vmem_limit_bytes=16 << 20),
+        compiler_params=pltpu.CompilerParams(vmem_limit_bytes=14 << 20),
     )(table, pltpu.with_memory_space_constraint(blocks, pltpu.HBM), *pieces)
 
 
@@ -294,6 +311,7 @@
 
 
 def body(blocks, block_rows, block_cols, counts, trials):
+    edge, _ = trials.shape
     r, c = lax.axis_index("row").astype(jnp.int32), lax.axis_index("col").astype(jnp.int32)
     slots = block_rows.shape[1]
     at = lax.broadcasted_iota(jnp.int32, (1, slots), 1)
@@ -304,16 +322,28 @@
     zs = jnp.stack([trials] + [to_z(trials, -k) for k in range(1, N_ZH)])
     row_pieces = [first] + [to_y(first, -k) for k in range(1, N_Y)]
     col_pieces = [zs] + [to_x(zs, -k) for k in range(1, N_X)]
-    outs = products_of(mirror_kernel, table, blocks[0], row_pieces, N_CORE * N_X, N_ZH)
-    keep, send = outs[:N_X], outs[N_X:]
-    col_pieces = col_pieces + [to_core(v) for v in col_pieces]
-    row_outs = products_of(direct_kernel, table, blocks[0], col_pieces, N_Y, N_ZL)
+    outs = products_of(
+        mirror_kernel,
+        table,
+        blocks[0],
+        row_pieces,
+        [(N_ZH, FIRST)] * (N_CORE * N_X) + [(N_X * N_ZH, edge - FIRST)] * N_CORE,
+    )
+    keep, send, (keep_b, send_b) = outs[:N_X], outs[N_X : 2 * N_X], outs[2 * N_X :]
+    col_pieces = col_pieces + [to_core(jnp.concatenate(col_pieces, 0))]
+    row_outs = products_of(direct_kernel, table, blocks[0], col_pieces, [(N_ZL, edge)] * N_Y)
     theirs = {k: to_core(send[k]) for k in (1, 3, 2, 0)}
-    sent = {k: to_x(keep[k] + theirs[k], k) for k in (1, 3, 2)}
+    pair = {k: keep[k] + theirs[k] for k in (1, 3, 2)}
+    sent = {k: to_x(pair[k], k) for k in (1, 3, 2)}
     got = ring_sum([keep[0] + theirs[0]] + [sent[k] for k in range(1, N_X)])
+    both = keep_b + to_core(send_b)
+    parts = [both[k * N_X : (k + 1) * N_X] for k in range(N_ZH)]
+    got_b = ring_sum([parts[0]] + [to_z(parts[k], k) for k in range(1, N_ZH)])
     rows = ring_sum([row_outs[0]] + [to_y(row_outs[k], k) for k in range(1, N_Y)])
     row_sum = rows[0] + to_zl(rows[1])
-    col_sum = ring_sum([got[0]] + [to_z(got[k], k) for k in range(1, N_ZH)])
+    sum_b = ring_sum([got_b[0]] + [to_x(got_b[k], k) for k in range(1, N_X)])
+    sum_a = ring_sum([got[0]] + [to_z(got[k], k) for k in range(1, N_ZH)])
+    col_sum = jnp.concatenate([sum_a, sum_b], 0)
     products = row_sum + col_sum
     return factor_and_basis(table, gram_pieces(products, r, c), products)
 

time: 155 us -> 155 us (level)
  waiting for transfers between devices: 54.6 us -> 44.7 us
  local copies, waits for them, and re-layouts: 0.15 us -> 5.76 us
  other arithmetic: 3.06 us -> 6.59 us
    ppermute x9 -> x12, waiting for transfers between devices: 22.8 us -> 13.7 us  [to_x(): return lax.ppermute(v, 'row', row_pairs(lambda z, x, c: (z, x + k, c)))]
    ppermute x9 -> x12, starting transfers between devices: 24.4 us -> 33.2 us  [to_z(): return lax.ppermute(v, 'row', row_pairs(lambda z, x, c: (z + k, x, c)))]
    ppermute x12, starting transfers between devices: 26.5 us -> 20.1 us  [to_y(): lax.ppermute(v, 'col', [(col_at(zl, y), col_at(zl, y + k)) for zl in rang...]
    unnamed x0 -> x6, local copies, waits for them, and re-layouts: none -> 4.86 us
    ppermute x12, waiting for transfers between devices: 12.2 us -> 7.45 us  [to_y(): lax.ppermute(v, 'col', [(col_at(zl, y), col_at(zl, y + k)) for zl in rang...]
    ppermute x9 -> x12, waiting for transfers between devices: 13.1 us -> 17.3 us  [to_z(): return lax.ppermute(v, 'row', row_pairs(lambda z, x, c: (z + k, x, c)))]
    add x3 -> x4, other arithmetic: 0.21 us -> 2.53 us  [the longest x3 2.46 us: body(): pair = {k: keep[k] + theirs[k] for k in (1, 3, 2)}]
    ppermute x10 -> x8, starting transfers between devices: 1.99 us -> 0.36 us  [to_core(): return lax.ppermute(v, 'row', row_pairs(lambda z, x, c: (z, x, 1 - c)))]
  transfers between devices with their start and end apart: 43 -> 47, of which waited for: 20 -> 22; matrix products, arithmetic and copies ran while one was open for 2% -> 8% of each run, Pallas kernels for 5% -> 5%
where the time goes in v3:
time: 155 us; the launch traced here: 153 us
  starting transfers between devices  74.7 us (48%)
  waiting for transfers between devices  44.7 us (29%)
  Pallas kernels  19.3 us (12%)
  other arithmetic  6.59 us (4%)
  local copies, waits for them, and re-layouts  5.76 us (4%)
    ppermute x12, starting transfers between devices, to_z(): return lax.ppermute(v, 'row', row_pairs(lambda z, x, c: (z + k, x, c)))  33.2 us
    ppermute x12, starting transfers between devices, to_y(): lax.ppermute(v, 'col', [(col_at(zl, y), col_at(zl, y + k)) for zl in rang...  20.1 us
    ppermute x12, waiting for transfers between devices, to_z(): return lax.ppermute(v, 'row', row_pairs(lambda z, x, c: (z + k, x, c)))  17.3 us
    ppermute x12, starting transfers between devices, to_x(): return lax.ppermute(v, 'row', row_pairs(lambda z, x, c: (z, x + k, c)))  16.7 us
    ppermute x12, waiting for transfers between devices, to_x(): return lax.ppermute(v, 'row', row_pairs(lambda z, x, c: (z, x + k, c)))  13.7 us
    pallas_call x1, Pallas kernels, factor_and_basis(): pl.pallas_call(factor_kernel, out_shape=(jax.ShapeDtypeStruct((edge, size...  11.2 us
    pallas_call x2, Pallas kernels, products_of(): pl.pallas_call(kernel, out_shape=tuple((jax.ShapeDtypeStruct((n, rows, wi...  8.1 us
    ppermute x12, waiting for transfers between devices, to_y(): lax.ppermute(v, 'col', [(col_at(zl, y), col_at(zl, y + k)) for zl in rang...  7.45 us
  transfers between devices with their start and end apart: 47, of which 22 were waited for; matrix products, arithmetic and copies ran while one was open for 8% of the time, Pallas kernels for 5%

profile of v3, /device:TPU:2, one launch (start us, length us, event | category | flops | bytes accessed | tf_op | source)
XLA Modules:
  0.0 153.0 jit_solution(13052821258633259964)
XLA Ops:
  0.6 2.0 %collective-permute-start.11 = (bf16[128,256]{1,0:T(8,128)(2,1)}, bf16[128,256]{1,0:T(8,128)(2,1)S(1)}, u32[]{:S(2)}, u32[]{:S(2)}) collective-permute-start(bf16[128,256]{1,0:T(8,128)(2,1)} %param.9), channel_id=1, source_target_pairs={{0,4},{1,5},{2,6},{3,7},{4,0},{5,1},{6,2},{7,3},{8,12},{9,13},{10,... | collective-permute-start | bytes 196616 | tf_op jit(solution)/shard_map/ppermute | solution.py:48
  2.6 5.4 %collective-permute-start = (bf16[128,256]{1,0:T(8,128)(2,1)}, bf16[128,256]{1,0:T(8,128)(2,1)S(1)}, u32[]{:S(2)}, u32[]{:S(2)}) collective-permute-start(bf16[128,256]{1,0:T(8,128)(2,1)} %param.9), channel_id=1, source_target_pairs={{0,192},{8,200},{16,208},{24,216},{32,224},{40,232},{48,240},{56,2... | collective-permute-start | bytes 196616 | tf_op jit(solution)/shard_map/ppermute | solution.py:32
  8.0 1.4 collective-permute-start.1
  9.5 2.4 %collective-permute-start.2 = (bf16[128,256]{1,0:T(8,128)(2,1)}, bf16[128,256]{1,0:T(8,128)(2,1)S(1)}, u32[]{:S(2)}, u32[]{:S(2)}) collective-permute-start(bf16[128,256]{1,0:T(8,128)(2,1)} %param.9), channel_id=1, source_target_pairs={{0,64},{8,72},{16,80},{24,88},{32,96},{40,104},{48,112},{56,120},{... | collective-permute-start | bytes 196616 | tf_op jit(solution)/shard_map/ppermute | solution.py:32
  11.8 1.5 constant_dynamic-update-slice_fusion.6
  15.7 3.1 %collective-permute-start.12 = (bf16[2,128,256]{2,1,0:T(8,128)(2,1)S(1)}, bf16[2,128,256]{2,1,0:T(8,128)(2,1)S(1)}, u32[]{:S(2)}, u32[]{:S(2)}) collective-permute-start(bf16[2,128,256]{2,1,0:T(8,128)(2,1)S(1)} %pad_maximum_fusion.1.refs_0_), channel_id=1, source_target_pairs={{0,3},{1,0},{2,1},{3,2},{4,7},{5,4},{6,5},{7,6},{8,11},{9,8},{10,9... | collective-permute-start | bytes 393224 | tf_op jit(solution)/shard_map/ppermute | solution.py:44
  19.4 1.0 collective-permute-start.14
  21.9 2.4 %collective-permute-start.4 = (bf16[4,128,256]{2,1,0:T(8,128)(2,1)S(1)}, bf16[4,128,256]{2,1,0:T(8,128)(2,1)S(1)}, u32[]{:S(2)}, u32[]{:S(2)}) collective-permute-start(bf16[4,128,256]{2,1,0:T(8,128)(2,1)S(1)} %pad_maximum_fusion.refs_0_), channel_id=1, source_target_pairs={{0,32},{8,40},{16,48},{24,56},{32,0},{40,8},{48,16},{56,24},{64,96... | collective-permute-start | bytes 786440 | tf_op jit(solution)/shard_map/ppermute | solution.py:36
  25.6 1.8 %collective-permute-start.5 = (bf16[4,128,256]{2,1,0:T(8,128)(2,1)S(1)}, bf16[4,128,256]{2,1,0:T(8,128)(2,1)S(1)}, u32[]{:S(2)}, u32[]{:S(2)}) collective-permute-start(bf16[4,128,256]{2,1,0:T(8,128)(2,1)S(1)} %pad_maximum_fusion.refs_0_), channel_id=1, source_target_pairs={{0,16},{8,24},{16,32},{24,40},{32,48},{40,56},{48,0},{56,8},{64,80... | collective-permute-start | bytes 786440 | tf_op jit(solution)/shard_map/ppermute | solution.py:36
  27.4 4.5 %shard_map.69 = (f32[4,96,256]{2,1,0:T(8,128)S(1)}, f32[4,96,256]{2,1,0:T(8,128)S(1)}, f32[4,96,256]{2,1,0:T(8,128)S(1)}, f32[4,96,256]{2,1,0:T(8,128)S(1)}, f32...) custom-call(s32[4,64]{1,0:T(4,128)S(1)} %pad_add_fusion.table, ...), custom_call_target="tpu_custom_call" | custom-call | flops 536870912 | bytes 6815744 | tf_op jit(solution)/shard_map/pallas_call | solution.py:172
  35.7 3.0 %collective-permute-start.26 = (f32[4,32,256]{2,1,0:T(8,128)S(1)}, f32[4,32,256]{2,1,0:T(8,128)S(1)}, u32[]{:S(2)}, u32[]{:S(2)}) collective-permute-start(f32[4,32,256]{2,1,0:T(8,128)S(1)} %get-tuple-element.32), channel_id=1, source_target_pairs={{0,128},{8,136},{16,144},{24,152},{32,160},{40,168},{48,176},{56,1... | collective-permute-start | bytes 393224 | tf_op jit(solution)/shard_map/ppermute | solution.py:32
  38.7 1.2 collective-permute-start.27
  39.9 2.9 %collective-permute-start.28 = (f32[4,32,256]{2,1,0:T(8,128)S(1)}, f32[4,32,256]{2,1,0:T(8,128)S(1)}, u32[]{:S(2)}, u32[]{:S(2)}) collective-permute-start(f32[4,32,256]{2,1,0:T(8,128)S(1)} %get-tuple-element.30), channel_id=1, source_target_pairs={{0,192},{8,200},{16,208},{24,216},{32,224},{40,232},{48,240},{56,2... | collective-permute-start | bytes 393224 | tf_op jit(solution)/shard_map/ppermute | solution.py:32
  42.8 4.6 %collective-permute-done.26 = f32[4,32,256]{2,1,0:T(8,128)S(1)} collective-permute-done((f32[4,32,256]{2,1,0:T(8,128)S(1)}, f32[4,32,256]{2,1,0:T(8,128)S(1)}, u32[]{:S(2)}, u32[]{:S(2)}) %collective-permute-start.26) | collective-permute-done | bytes 131104 | tf_op jit(solution)/shard_map/ppermute | solution.py:32
  47.4 4.1 %collective-permute-done.27 = f32[4,32,256]{2,1,0:T(8,128)S(1)} collective-permute-done((f32[4,32,256]{2,1,0:T(8,128)S(1)}, f32[4,32,256]{2,1,0:T(8,128)S(1)}, u32[]{:S(2)}, u32[]{:S(2)}) %collective-permute-start.27) | collective-permute-done | bytes 131104 | tf_op jit(solution)/shard_map/ppermute | solution.py:32
  52.5 3.1 %collective-permute-start.29 = (f32[32,256]{1,0:T(8,128)S(1)}, f32[32,256]{1,0:T(8,128)S(1)}, u32[]{:S(2)}, u32[]{:S(2)}) collective-permute-start(f32[32,256]{1,0:T(8,128)S(1)} %get-tuple-element.41), channel_id=1, source_target_pairs={{0,32},{8,40},{16,48},{24,56},{32,0},{40,8},{48,16},{56,24},{64,96... | collective-permute-start | bytes 98312 | tf_op jit(solution)/shard_map/ppermute | solution.py:36
  55.6 1.2 collective-permute-start.30
  61.0 2.3 %collective-permute-start.19 = (f32[4,96,256]{2,1,0:T(8,128)}, f32[4,96,256]{2,1,0:T(8,128)}, u32[]{:S(2)}, u32[]{:S(2)}) collective-permute-start(f32[4,96,256]{2,1,0:T(8,128)} %add.133), channel_id=1, source_target_pairs={{0,16},{8,24},{16,32},{24,40},{32,48},{40,56},{48,0},{56,8},{64,80... | collective-permute-start | bytes 1179656 | tf_op jit(solution)/shard_map/ppermute | solution.py:36
  63.4 3.6 %shard_map.68 = (f32[2,128,256]{2,1,0:T(8,128)S(1)}, f32[2,128,256]{2,1,0:T(8,128)S(1)}, f32[2,128,256]{2,1,0:T(8,128)S(1)}, f32[2,128,256]{2,1,0:T(8,128)S(1)}) custom-call(s32[4,64]{1,0:T(4,128)S(1)} %pad_add_fusion.table, bf16[64,128,128]{2,1,0:T(8,128)(2,1)} %bitcast.51, bf16[4,128,256]{2,1,0:T(8,128)(2,1)S(1)} %pad_maximum_fusion.refs_0_, ...), custom_call_target="tpu_custom_call" | custom-call | flops 536870912 | bytes 5242880 | tf_op jit(solution)/shard_map/pallas_call | solution.py:172
  67.1 3.2 %collective-permute-start.7 = (f32[2,128,256]{2,1,0:T(8,128)S(1)}, f32[2,128,256]{2,1,0:T(8,128)S(1)}, u32[]{:S(2)}, u32[]{:S(2)}) collective-permute-start(f32[2,128,256]{2,1,0:T(8,128)S(1)} %get-tuple-element.17), channel_id=1, source_target_pairs={{0,2},{1,3},{2,0},{3,1},{4,6},{5,7},{6,4},{7,5},{8,10},{9,11},{10,... | collective-permute-start | bytes 786440 | tf_op jit(solution)/shard_map/ppermute | solution.py:44
  70.3 3.6 %collective-permute-done.17 = f32[4,96,256]{2,1,0:T(8,128)} collective-permute-done((f32[4,96,256]{2,1,0:T(8,128)}, f32[4,96,256]{2,1,0:T(8,128)}, u32[]{:S(2)}, u32[]{:S(2)}) %collective-permute-start.17) | collective-permute-done | bytes 393248 | tf_op jit(solution)/shard_map/ppermute | solution.py:36
  73.9 2.5 %collective-permute-start.9 = (f32[2,128,256]{2,1,0:T(8,128)S(1)}, f32[2,128,256]{2,1,0:T(8,128)S(1)}, u32[]{:S(2)}, u32[]{:S(2)}) collective-permute-start(f32[2,128,256]{2,1,0:T(8,128)S(1)} %get-tuple-element.19), channel_id=1, source_target_pairs={{0,3},{1,0},{2,1},{3,2},{4,7},{5,4},{6,5},{7,6},{8,11},{9,8},{10,9... | collective-permute-start | bytes 786440 | tf_op jit(solution)/shard_map/ppermute | solution.py:44
  76.4 5.2 %collective-permute-done.19 = f32[4,96,256]{2,1,0:T(8,128)} collective-permute-done((f32[4,96,256]{2,1,0:T(8,128)}, f32[4,96,256]{2,1,0:T(8,128)}, u32[]{:S(2)}, u32[]{:S(2)}) %collective-permute-start.19) | collective-permute-done | bytes 393248 | tf_op jit(solution)/shard_map/ppermute | solution.py:36
  81.9 1.4 add_add_fusion
  83.2 4.6 %collective-permute-start.22 = (f32[96,256]{1,0:T(8,128)S(1)}, f32[96,256]{1,0:T(8,128)S(1)}, u32[]{:S(2)}, u32[]{:S(2)}) collective-permute-start(f32[96,256]{1,0:T(8,128)S(1)} %get-tuple-element.35), channel_id=1, source_target_pairs={{0,128},{8,136},{16,144},{24,152},{32,160},{40,168},{48,176},{56,1... | collective-permute-start | bytes 294920 | tf_op jit(solution)/shard_map/ppermute | solution.py:32
  88.4 3.5 %collective-permute-start.24 = (f32[96,256]{1,0:T(8,128)S(1)}, f32[96,256]{1,0:T(8,128)S(1)}, u32[]{:S(2)}, u32[]{:S(2)}) collective-permute-start(f32[96,256]{1,0:T(8,128)S(1)} %get-tuple-element.33), channel_id=1, source_target_pairs={{0,192},{8,200},{16,208},{24,216},{32,224},{40,232},{48,240},{56,2... | collective-permute-start | bytes 294920 | tf_op jit(solution)/shard_map/ppermute | solution.py:32
  92.5 5.8 %collective-permute-done.23 = f32[96,256]{1,0:T(8,128)S(1)} collective-permute-done((f32[96,256]{1,0:T(8,128)S(1)}, f32[96,256]{1,0:T(8,128)S(1)}, u32[]{:S(2)}, u32[]{:S(2)}) %collective-permute-start.23) | collective-permute-done | bytes 98336 | tf_op jit(solution)/shard_map/ppermute | solution.py:32
  98.4 1.7 %collective-permute-done.10 = f32[128,256]{1,0:T(8,128)S(1)} collective-permute-done((f32[128,256]{1,0:T(8,128)S(1)}, f32[128,256]{1,0:T(8,128)S(1)}, u32[]{:S(2)}, u32[]{:S(2)}) %collective-permute-start.10) | collective-permute-done | bytes 131104 | tf_op jit(solution)/shard_map/ppermute | solution.py:48
  100.7 1.3 collective-permute-done.32
  102.0 2.2 %collective-permute-start.33 = (f32[32,256]{1,0:T(8,128)S(1)}, f32[32,256]{1,0:T(8,128)S(1)}, u32[]{:S(2)}, u32[]{:S(2)}) collective-permute-start(f32[32,256]{1,0:T(8,128)S(1)} %get-tuple-element.36), channel_id=1, source_target_pairs={{0,2},{1,3},{2,0},{3,1},{4,6},{5,7},{6,4},{7,5},{8,10},{9,11},{10,... | collective-permute-start | bytes 98312 | tf_op jit(solution)/shard_map/ppermute | solution.py:44
  104.3 1.0 collective-permute-start.34
  105.2 2.3 %collective-permute-start.35 = (f32[32,256]{1,0:T(8,128)S(1)}, f32[32,256]{1,0:T(8,128)S(1)}, u32[]{:S(2)}, u32[]{:S(2)}) collective-permute-start(f32[32,256]{1,0:T(8,128)S(1)} %get-tuple-element.37), channel_id=1, source_target_pairs={{0,3},{1,0},{2,1},{3,2},{4,7},{5,4},{6,5},{7,6},{8,11},{9,8},{10,9... | collective-permute-start | bytes 98312 | tf_op jit(solution)/shard_map/ppermute | solution.py:44
  107.5 1.8 %collective-permute-done.34 = f32[32,256]{1,0:T(8,128)S(1)} collective-permute-done((f32[32,256]{1,0:T(8,128)S(1)}, f32[32,256]{1,0:T(8,128)S(1)}, u32[]{:S(2)}, u32[]{:S(2)}) %collective-permute-start.34) | collective-permute-done | bytes 32800 | tf_op jit(solution)/shard_map/ppermute | solution.py:44
  109.4 0.9 collective-permute-start.36
  110.3 2.4 %collective-permute-start.37 = (f32[32,256]{1,0:T(8,128)S(1)}, f32[32,256]{1,0:T(8,128)S(1)}, u32[]{:S(2)}, u32[]{:S(2)}) collective-permute-start(f32[32,256]{1,0:T(8,128)S(1)} %add_add_fusion.4), channel_id=1, source_target_pairs={{0,16},{8,24},{16,32},{24,40},{32,48},{40,56},{48,0},{56,8},{64,80... | collective-permute-start | bytes 98312 | tf_op jit(solution)/shard_map/ppermute | solution.py:36
  112.8 2.1 %collective-permute-done.36 = f32[32,256]{1,0:T(8,128)S(1)} collective-permute-done((f32[32,256]{1,0:T(8,128)S(1)}, f32[32,256]{1,0:T(8,128)S(1)}, u32[]{:S(2)}, u32[]{:S(2)}) %collective-permute-start.36) | collective-permute-done | bytes 32800 | tf_op jit(solution)/shard_map/ppermute | solution.py:36
  115.0 1.6 %collective-permute-done.38 = f32[32,256]{1,0:T(8,128)S(1)} collective-permute-done((f32[32,256]{1,0:T(8,128)S(1)}, f32[32,256]{1,0:T(8,128)S(1)}, u32[]{:S(2)}, u32[]{:S(2)}) %collective-permute-start.38) | collective-permute-done | bytes 32800 | tf_op jit(solution)/shard_map/ppermute | solution.py:36
  116.6 1.9 %collective-permute-start.39 = (f32[32,256]{1,0:T(8,128)S(1)}, f32[32,256]{1,0:T(8,128)S(1)}, u32[]{:S(2)}, u32[]{:S(2)}) collective-permute-start(f32[32,256]{1,0:T(8,128)S(1)} %add_add_fusion.3), channel_id=1, source_target_pairs={{0,4},{1,5},{2,6},{3,7},{4,0},{5,1},{6,2},{7,3},{8,12},{9,13},{10,... | collective-permute-start | bytes 98312 | tf_op jit(solution)/shard_map/ppermute | solution.py:48
  118.5 2.1 %collective-permute-done.39 = f32[32,256]{1,0:T(8,128)S(1)} collective-permute-done((f32[32,256]{1,0:T(8,128)S(1)}, f32[32,256]{1,0:T(8,128)S(1)}, u32[]{:S(2)}, u32[]{:S(2)}) %collective-permute-start.39) | collective-permute-done | bytes 32800 | tf_op jit(solution)/shard_map/ppermute | solution.py:48
  120.6 4.1 %collective-permute-start.40 = (f32[32,256]{1,0:T(8,128)S(1)}, f32[32,256]{1,0:T(8,128)S(1)}, u32[]{:S(2)}, u32[]{:S(2)}) collective-permute-start(f32[32,256]{1,0:T(8,128)S(1)} %add.164), channel_id=1, source_target_pairs={{0,128},{8,136},{16,144},{24,152},{32,160},{40,168},{48,176},{56,1... | collective-permute-start | bytes 98312 | tf_op jit(solution)/shard_map/ppermute | solution.py:32
  125.5 3.4 %collective-permute-start.42 = (f32[32,256]{1,0:T(8,128)S(1)}, f32[32,256]{1,0:T(8,128)S(1)}, u32[]{:S(2)}, u32[]{:S(2)}) collective-permute-start(f32[32,256]{1,0:T(8,128)S(1)} %add.164), channel_id=1, source_target_pairs={{0,192},{8,200},{16,208},{24,216},{32,224},{40,232},{48,240},{56,2... | collective-permute-start | bytes 98312 | tf_op jit(solution)/shard_map/ppermute | solution.py:32
  128.9 1.9 %collective-permute-done.41 = f32[32,256]{1,0:T(8,128)S(1)} collective-permute-done((f32[32,256]{1,0:T(8,128)S(1)}, f32[32,256]{1,0:T(8,128)S(1)}, u32[]{:S(2)}, u32[]{:S(2)}) %collective-permute-start.41) | collective-permute-done | bytes 32800 | tf_op jit(solution)/shard_map/ppermute | solution.py:32
  130.9 1.2 collective-permute-done.43
  132.1 3.2 %collective-permute-start.44 = (f32[2,32,256]{2,1,0:T(8,128)S(1)}, f32[2,32,256]{2,1,0:T(8,128)S(1)}, u32[]{:S(2)}, u32[]{:S(2)}) collective-permute-start(f32[2,32,256]{2,1,0:T(8,128)S(1)} %pad_maximum_fusion.2.piece0), channel_id=1, source_target_pairs={{0,3},{1,0},{2,1},{3,2},{4,7},{5,4},{6,5},{7,6},{8,11},{9,8},{10,9... | collective-permute-start | bytes 196616 | tf_op jit(solution)/shard_map/ppermute | solution.py:44
  135.3 1.0 collective-permute-start.46
  136.3 2.2 %collective-permute-done.44.piece1 = f32[2,32,256]{2,1,0:T(8,128)S(1)} collective-permute-done((f32[2,32,256]{2,1,0:T(8,128)S(1)}, f32[2,32,256]{2,1,0:T(8,128)S(1)}, u32[]{:S(2)}, u32[]{:S(2)}) %collective-permute-start.44) | collective-permute-done | bytes 65568 | tf_op jit(solution)/shard_map/ppermute | solution.py:44
  138.4 3.0 %collective-permute-done.45.piece2 = f32[2,32,256]{2,1,0:T(8,128)S(1)} collective-permute-done((f32[2,32,256]{2,1,0:T(8,128)S(1)}, f32[2,32,256]{2,1,0:T(8,128)S(1)}, u32[]{:S(2)}, u32[]{:S(2)}) %collective-permute-start.45) | collective-permute-done | bytes 65568 | tf_op jit(solution)/shard_map/ppermute | solution.py:44
  141.8 11.2 %factor.1 = (f32[128,256]{1,0:T(8,128)}, f32[256,256]{1,0:T(8,128)}) custom-call(s32[4,64]{1,0:T(4,128)S(1)} %pad_add_fusion.table, f32[2,32,256]{2,1,0:T(8,128)S(1)} %pad_maximum_fusion.2.piece0, f32[2,32,256]{2,1,0:T(8,128)S(1)} %collective-permute-done.44.piece1, f32[2,32,256]{2,1,0:T(8,128)S(1)} %collective-permute-done.45.piece2, ...), custom_call_target="tpu_custom_call" | custom-call | tf_op jit(solution)/shard_map/factor/pallas_call | solution.py:285
  (84 shorter events, 17.9 us)
Async XLA Ops:
  0.6 14.2 %collective-permute-start.11 = (bf16[128,256]{1,0:T(8,128)(2,1)}, bf16[128,256]{1,0:T(8,128)(2,1)S(1)}, u32[]{:S(2)}, u32[]{:S(2)}) collective-permute-start(bf16[128,256]{1,0:T(8,128)(2,1)} %param.9), channel_id=1, source_target_pairs={{0,4},{1,5},{2,6},{3,7},{4,0},{5,1},{6,2},{7,3},{8,12},{9,13},{10,... | collective-permute-start | bytes 196616 | tf_op jit(solution)/shard_map/ppermute | solution.py:48
  2.6 16.8 %collective-permute-start = (bf16[128,256]{1,0:T(8,128)(2,1)}, bf16[128,256]{1,0:T(8,128)(2,1)S(1)}, u32[]{:S(2)}, u32[]{:S(2)}) collective-permute-start(bf16[128,256]{1,0:T(8,128)(2,1)} %param.9), channel_id=1, source_target_pairs={{0,192},{8,200},{16,208},{24,216},{32,224},{40,232},{48,240},{56,2... | collective-permute-start | bytes 196616 | tf_op jit(solution)/shard_map/ppermute | solution.py:32
  8.0 12.4 %collective-permute-start.1 = (bf16[128,256]{1,0:T(8,128)(2,1)}, bf16[128,256]{1,0:T(8,128)(2,1)S(1)}, u32[]{:S(2)}, u32[]{:S(2)}) collective-permute-start(bf16[128,256]{1,0:T(8,128)(2,1)} %param.9), channel_id=1, source_target_pairs={{0,128},{8,136},{16,144},{24,152},{32,160},{40,168},{48,176},{56,1... | collective-permute-start | bytes 196616 | tf_op jit(solution)/shard_map/ppermute | solution.py:32
  9.5 10.9 %collective-permute-start.2 = (bf16[128,256]{1,0:T(8,128)(2,1)}, bf16[128,256]{1,0:T(8,128)(2,1)S(1)}, u32[]{:S(2)}, u32[]{:S(2)}) collective-permute-start(bf16[128,256]{1,0:T(8,128)(2,1)} %param.9), channel_id=1, source_target_pairs={{0,64},{8,72},{16,80},{24,88},{32,96},{40,104},{48,112},{56,120},{... | collective-permute-start | bytes 196616 | tf_op jit(solution)/shard_map/ppermute | solution.py:32
  15.7 9.9 %collective-permute-start.12 = (bf16[2,128,256]{2,1,0:T(8,128)(2,1)S(1)}, bf16[2,128,256]{2,1,0:T(8,128)(2,1)S(1)}, u32[]{:S(2)}, u32[]{:S(2)}) collective-permute-start(bf16[2,128,256]{2,1,0:T(8,128)(2,1)S(1)} %pad_maximum_fusion.1.refs_0_), channel_id=1, source_target_pairs={{0,3},{1,0},{2,1},{3,2},{4,7},{5,4},{6,5},{7,6},{8,11},{9,8},{10,9... | collective-permute-start | bytes 393224 | tf_op jit(solution)/shard_map/ppermute | solution.py:44
  18.8 8.6 %collective-permute-start.13 = (bf16[2,128,256]{2,1,0:T(8,128)(2,1)S(1)}, bf16[2,128,256]{2,1,0:T(8,128)(2,1)S(1)}, u32[]{:S(2)}, u32[]{:S(2)}) collective-permute-start(bf16[2,128,256]{2,1,0:T(8,128)(2,1)S(1)} %pad_maximum_fusion.1.refs_0_), channel_id=1, source_target_pairs={{0,2},{1,3},{2,0},{3,1},{4,6},{5,7},{6,4},{7,5},{8,10},{9,11},{10,... | collective-permute-start | bytes 393224 | tf_op jit(solution)/shard_map/ppermute | solution.py:44
  19.4 8.0 %collective-permute-start.14 = (bf16[2,128,256]{2,1,0:T(8,128)(2,1)S(1)}, bf16[2,128,256]{2,1,0:T(8,128)(2,1)S(1)}, u32[]{:S(2)}, u32[]{:S(2)}) collective-permute-start(bf16[2,128,256]{2,1,0:T(8,128)(2,1)S(1)} %pad_maximum_fusion.1.refs_0_), channel_id=1, source_target_pairs={{0,1},{1,2},{2,3},{3,0},{4,5},{5,6},{6,7},{7,4},{8,9},{9,10},{10,1... | collective-permute-start | bytes 393224 | tf_op jit(solution)/shard_map/ppermute | solution.py:44
  21.3 11.3 %collective-permute-start.3 = (bf16[4,128,256]{2,1,0:T(8,128)(2,1)S(1)}, bf16[4,128,256]{2,1,0:T(8,128)(2,1)S(1)}, u32[]{:S(2)}, u32[]{:S(2)}) collective-permute-start(bf16[4,128,256]{2,1,0:T(8,128)(2,1)S(1)} %pad_maximum_fusion.refs_0_), channel_id=1, source_target_pairs={{0,48},{8,56},{16,0},{24,8},{32,16},{40,24},{48,32},{56,40},{64,11... | collective-permute-start | bytes 786440 | tf_op jit(solution)/shard_map/ppermute | solution.py:36
  21.9 12.1 %collective-permute-start.4 = (bf16[4,128,256]{2,1,0:T(8,128)(2,1)S(1)}, bf16[4,128,256]{2,1,0:T(8,128)(2,1)S(1)}, u32[]{:S(2)}, u32[]{:S(2)}) collective-permute-start(bf16[4,128,256]{2,1,0:T(8,128)(2,1)S(1)} %pad_maximum_fusion.refs_0_), channel_id=1, source_target_pairs={{0,32},{8,40},{16,48},{24,56},{32,0},{40,8},{48,16},{56,24},{64,96... | collective-permute-start | bytes 786440 | tf_op jit(solution)/shard_map/ppermute | solution.py:36
  25.6 9.3 %collective-permute-start.5 = (bf16[4,128,256]{2,1,0:T(8,128)(2,1)S(1)}, bf16[4,128,256]{2,1,0:T(8,128)(2,1)S(1)}, u32[]{:S(2)}, u32[]{:S(2)}) collective-permute-start(bf16[4,128,256]{2,1,0:T(8,128)(2,1)S(1)} %pad_maximum_fusion.refs_0_), channel_id=1, source_target_pairs={{0,16},{8,24},{16,32},{24,40},{32,48},{40,56},{48,0},{56,8},{64,80... | collective-permute-start | bytes 786440 | tf_op jit(solution)/shard_map/ppermute | solution.py:36
  31.9 3.7 %collective-permute-start.25 = (f32[16,32,256]{2,1,0:T(8,128)S(1)}, f32[16,32,256]{2,1,0:T(8,128)S(1)}, u32[]{:S(2)}, u32[]{:S(2)}) collective-permute-start(f32[16,32,256]{2,1,0:T(8,128)S(1)} %get-tuple-element.29), channel_id=1, source_target_pairs={{0,8},{8,0},{16,24},{24,16},{32,40},{40,32},{48,56},{56,48},{64,72... | collective-permute-start | bytes 1572872 | tf_op jit(solution)/shard_map/ppermute | solution.py:40
  35.6 27.9 %collective-permute-start.6 = (bf16[16,128,256]{2,1,0:T(8,128)(2,1)}, bf16[16,128,256]{2,1,0:T(8,128)(2,1)S(1)}, u32[]{:S(2)}, u32[]{:S(2)}) collective-permute-start(bf16[16,128,256]{2,1,0:T(8,128)(2,1)} %constant_dynamic-update-slice_fusion), channel_id=1, source_target_pairs={{0,8},{8,0},{16,24},{24,16},{32,40},{40,32},{48,56},{56,48},{64,72... | collective-permute-start | bytes 3145736 | tf_op jit(solution)/shard_map/ppermute | solution.py:40
  35.7 11.7 %collective-permute-start.26 = (f32[4,32,256]{2,1,0:T(8,128)S(1)}, f32[4,32,256]{2,1,0:T(8,128)S(1)}, u32[]{:S(2)}, u32[]{:S(2)}) collective-permute-start(f32[4,32,256]{2,1,0:T(8,128)S(1)} %get-tuple-element.32), channel_id=1, source_target_pairs={{0,128},{8,136},{16,144},{24,152},{32,160},{40,168},{48,176},{56,1... | collective-permute-start | bytes 393224 | tf_op jit(solution)/shard_map/ppermute | solution.py:32
  38.7 12.8 %collective-permute-start.27 = (f32[4,32,256]{2,1,0:T(8,128)S(1)}, f32[4,32,256]{2,1,0:T(8,128)S(1)}, u32[]{:S(2)}, u32[]{:S(2)}) collective-permute-start(f32[4,32,256]{2,1,0:T(8,128)S(1)} %get-tuple-element.31), channel_id=1, source_target_pairs={{0,64},{8,72},{16,80},{24,88},{32,96},{40,104},{48,112},{56,120},{... | collective-permute-start | bytes 393224 | tf_op jit(solution)/shard_map/ppermute | solution.py:32
  39.9 12.5 %collective-permute-start.28 = (f32[4,32,256]{2,1,0:T(8,128)S(1)}, f32[4,32,256]{2,1,0:T(8,128)S(1)}, u32[]{:S(2)}, u32[]{:S(2)}) collective-permute-start(f32[4,32,256]{2,1,0:T(8,128)S(1)} %get-tuple-element.30), channel_id=1, source_target_pairs={{0,192},{8,200},{16,208},{24,216},{32,224},{40,232},{48,240},{56,2... | collective-permute-start | bytes 393224 | tf_op jit(solution)/shard_map/ppermute | solution.py:32
  42.8 12.8 %collective-permute-start.16 = (f32[4,96,256]{2,1,0:T(8,128)S(1)}, f32[4,96,256]{2,1,0:T(8,128)S(1)}, u32[]{:S(2)}, u32[]{:S(2)}) collective-permute-start(f32[4,96,256]{2,1,0:T(8,128)S(1)} %get-tuple-element.23), channel_id=1, source_target_pairs={{0,8},{8,0},{16,24},{24,16},{32,40},{40,32},{48,56},{56,48},{64,72... | collective-permute-start | bytes 1179656 | tf_op jit(solution)/shard_map/ppermute | solution.py:40
  47.4 9.3 %collective-permute-start.18 = (f32[4,96,256]{2,1,0:T(8,128)S(1)}, f32[4,96,256]{2,1,0:T(8,128)S(1)}, u32[]{:S(2)}, u32[]{:S(2)}) collective-permute-start(f32[4,96,256]{2,1,0:T(8,128)S(1)} %get-tuple-element.25), channel_id=1, source_target_pairs={{0,8},{8,0},{16,24},{24,16},{32,40},{40,32},{48,56},{56,48},{64,72... | collective-permute-start | bytes 1179656 | tf_op jit(solution)/shard_map/ppermute | solution.py:40
  51.5 7.8 %collective-permute-start.20 = (f32[4,96,256]{2,1,0:T(8,128)S(1)}, f32[4,96,256]{2,1,0:T(8,128)S(1)}, u32[]{:S(2)}, u32[]{:S(2)}) collective-permute-start(f32[4,96,256]{2,1,0:T(8,128)S(1)} %get-tuple-element.27), channel_id=1, source_target_pairs={{0,8},{8,0},{16,24},{24,16},{32,40},{40,32},{48,56},{56,48},{64,72... | collective-permute-start | bytes 1179656 | tf_op jit(solution)/shard_map/ppermute | solution.py:40
  52.5 7.6 %collective-permute-start.29 = (f32[32,256]{1,0:T(8,128)S(1)}, f32[32,256]{1,0:T(8,128)S(1)}, u32[]{:S(2)}, u32[]{:S(2)}) collective-permute-start(f32[32,256]{1,0:T(8,128)S(1)} %get-tuple-element.41), channel_id=1, source_target_pairs={{0,32},{8,40},{16,48},{24,56},{32,0},{40,8},{48,16},{56,24},{64,96... | collective-permute-start | bytes 98312 | tf_op jit(solution)/shard_map/ppermute | solution.py:36
  55.6 5.4 %collective-permute-start.30 = (f32[32,256]{1,0:T(8,128)S(1)}, f32[32,256]{1,0:T(8,128)S(1)}, u32[]{:S(2)}, u32[]{:S(2)}) collective-permute-start(f32[32,256]{1,0:T(8,128)S(1)} %get-tuple-element.40), channel_id=1, source_target_pairs={{0,16},{8,24},{16,32},{24,40},{32,48},{40,56},{48,0},{56,8},{64,80... | collective-permute-start | bytes 98312 | tf_op jit(solution)/shard_map/ppermute | solution.py:36
  56.8 6.5 %collective-permute-start.31 = (f32[32,256]{1,0:T(8,128)S(1)}, f32[32,256]{1,0:T(8,128)S(1)}, u32[]{:S(2)}, u32[]{:S(2)}) collective-permute-start(f32[32,256]{1,0:T(8,128)S(1)} %get-tuple-element.39), channel_id=1, source_target_pairs={{0,48},{8,56},{16,0},{24,8},{32,16},{40,24},{48,32},{56,40},{64,11... | collective-permute-start | bytes 98312 | tf_op jit(solution)/shard_map/ppermute | solution.py:36
  59.3 11.1 %collective-permute-start.15 = (f32[4,96,256]{2,1,0:T(8,128)S(1)}, f32[4,96,256]{2,1,0:T(8,128)S(1)}, u32[]{:S(2)}, u32[]{:S(2)}) collective-permute-start(f32[4,96,256]{2,1,0:T(8,128)S(1)} %get-tuple-element.21), channel_id=1, source_target_pairs={{0,8},{8,0},{16,24},{24,16},{32,40},{40,32},{48,56},{56,48},{64,72... | collective-permute-start | bytes 1179656 | tf_op jit(solution)/shard_map/ppermute | solution.py:40
  60.1 13.9 %collective-permute-start.17 = (f32[4,96,256]{2,1,0:T(8,128)}, f32[4,96,256]{2,1,0:T(8,128)}, u32[]{:S(2)}, u32[]{:S(2)}) collective-permute-start(f32[4,96,256]{2,1,0:T(8,128)} %add.131), channel_id=1, source_target_pairs={{0,32},{8,40},{16,48},{24,56},{32,0},{40,8},{48,16},{56,24},{64,96... | collective-permute-start | bytes 1179656 | tf_op jit(solution)/shard_map/ppermute | solution.py:36
  61.0 20.6 %collective-permute-start.19 = (f32[4,96,256]{2,1,0:T(8,128)}, f32[4,96,256]{2,1,0:T(8,128)}, u32[]{:S(2)}, u32[]{:S(2)}) collective-permute-start(f32[4,96,256]{2,1,0:T(8,128)} %add.133), channel_id=1, source_target_pairs={{0,16},{8,24},{16,32},{24,40},{32,48},{40,56},{48,0},{56,8},{64,80... | collective-permute-start | bytes 1179656 | tf_op jit(solution)/shard_map/ppermute | solution.py:36
  63.3 18.6 %collective-permute-start.21 = (f32[4,96,256]{2,1,0:T(8,128)}, f32[4,96,256]{2,1,0:T(8,128)}, u32[]{:S(2)}, u32[]{:S(2)}) collective-permute-start(f32[4,96,256]{2,1,0:T(8,128)} %add.134), channel_id=1, source_target_pairs={{0,48},{8,56},{16,0},{24,8},{32,16},{40,24},{48,32},{56,40},{64,11... | collective-permute-start | bytes 1179656 | tf_op jit(solution)/shard_map/ppermute | solution.py:36
  67.1 21.3 %collective-permute-start.7 = (f32[2,128,256]{2,1,0:T(8,128)S(1)}, f32[2,128,256]{2,1,0:T(8,128)S(1)}, u32[]{:S(2)}, u32[]{:S(2)}) collective-permute-start(f32[2,128,256]{2,1,0:T(8,128)S(1)} %get-tuple-element.17), channel_id=1, source_target_pairs={{0,2},{1,3},{2,0},{3,1},{4,6},{5,7},{6,4},{7,5},{8,10},{9,11},{10,... | collective-permute-start | bytes 786440 | tf_op jit(solution)/shard_map/ppermute | solution.py:44
  70.3 21.6 %collective-permute-start.8 = (f32[2,128,256]{2,1,0:T(8,128)S(1)}, f32[2,128,256]{2,1,0:T(8,128)S(1)}, u32[]{:S(2)}, u32[]{:S(2)}) collective-permute-start(f32[2,128,256]{2,1,0:T(8,128)S(1)} %get-tuple-element.18), channel_id=1, source_target_pairs={{0,1},{1,2},{2,3},{3,0},{4,5},{5,6},{6,7},{7,4},{8,9},{9,10},{10,1... | collective-permute-start | bytes 786440 | tf_op jit(solution)/shard_map/ppermute | solution.py:44
  73.9 18.0 %collective-permute-start.9 = (f32[2,128,256]{2,1,0:T(8,128)S(1)}, f32[2,128,256]{2,1,0:T(8,128)S(1)}, u32[]{:S(2)}, u32[]{:S(2)}) collective-permute-start(f32[2,128,256]{2,1,0:T(8,128)S(1)} %get-tuple-element.19), channel_id=1, source_target_pairs={{0,3},{1,0},{2,1},{3,2},{4,7},{5,4},{6,5},{7,6},{8,11},{9,8},{10,9... | collective-permute-start | bytes 786440 | tf_op jit(solution)/shard_map/ppermute | solution.py:44
  83.2 9.3 %collective-permute-start.22 = (f32[96,256]{1,0:T(8,128)S(1)}, f32[96,256]{1,0:T(8,128)S(1)}, u32[]{:S(2)}, u32[]{:S(2)}) collective-permute-start(f32[96,256]{1,0:T(8,128)S(1)} %get-tuple-element.35), channel_id=1, source_target_pairs={{0,128},{8,136},{16,144},{24,152},{32,160},{40,168},{48,176},{56,1... | collective-permute-start | bytes 294920 | tf_op jit(solution)/shard_map/ppermute | solution.py:32
  87.8 10.6 %collective-permute-start.23 = (f32[96,256]{1,0:T(8,128)S(1)}, f32[96,256]{1,0:T(8,128)S(1)}, u32[]{:S(2)}, u32[]{:S(2)}) collective-permute-start(f32[96,256]{1,0:T(8,128)S(1)} %get-tuple-element.34), channel_id=1, source_target_pairs={{0,64},{8,72},{16,80},{24,88},{32,96},{40,104},{48,112},{56,120},{... | collective-permute-start | bytes 294920 | tf_op jit(solution)/shard_map/ppermute | solution.py:32
  88.4 9.9 %collective-permute-start.24 = (f32[96,256]{1,0:T(8,128)S(1)}, f32[96,256]{1,0:T(8,128)S(1)}, u32[]{:S(2)}, u32[]{:S(2)}) collective-permute-start(f32[96,256]{1,0:T(8,128)S(1)} %get-tuple-element.33), channel_id=1, source_target_pairs={{0,192},{8,200},{16,208},{24,216},{32,224},{40,232},{48,240},{56,2... | collective-permute-start | bytes 294920 | tf_op jit(solution)/shard_map/ppermute | solution.py:32
  92.0 8.0 %collective-permute-start.10 = (f32[128,256]{1,0:T(8,128)S(1)}, f32[128,256]{1,0:T(8,128)S(1)}, u32[]{:S(2)}, u32[]{:S(2)}) collective-permute-start(f32[128,256]{1,0:T(8,128)S(1)} %slice_bitcast_fusion), channel_id=1, source_target_pairs={{0,4},{1,5},{2,6},{3,7},{4,0},{5,1},{6,2},{7,3},{8,12},{9,13},{10,... | collective-permute-start | bytes 393224 | tf_op jit(solution)/shard_map/ppermute | solution.py:48
  100.6 1.4 collective-permute-start.32
  102.0 5.5 %collective-permute-start.33 = (f32[32,256]{1,0:T(8,128)S(1)}, f32[32,256]{1,0:T(8,128)S(1)}, u32[]{:S(2)}, u32[]{:S(2)}) collective-permute-start(f32[32,256]{1,0:T(8,128)S(1)} %get-tuple-element.36), channel_id=1, source_target_pairs={{0,2},{1,3},{2,0},{3,1},{4,6},{5,7},{6,4},{7,5},{8,10},{9,11},{10,... | collective-permute-start | bytes 98312 | tf_op jit(solution)/shard_map/ppermute | solution.py:44
  104.3 5.1 %collective-permute-start.34 = (f32[32,256]{1,0:T(8,128)S(1)}, f32[32,256]{1,0:T(8,128)S(1)}, u32[]{:S(2)}, u32[]{:S(2)}) collective-permute-start(f32[32,256]{1,0:T(8,128)S(1)} %get-tuple-element.38), channel_id=1, source_target_pairs={{0,1},{1,2},{2,3},{3,0},{4,5},{5,6},{6,7},{7,4},{8,9},{9,10},{10,1... | collective-permute-start | bytes 98312 | tf_op jit(solution)/shard_map/ppermute | solution.py:44
  105.2 4.2 %collective-permute-start.35 = (f32[32,256]{1,0:T(8,128)S(1)}, f32[32,256]{1,0:T(8,128)S(1)}, u32[]{:S(2)}, u32[]{:S(2)}) collective-permute-start(f32[32,256]{1,0:T(8,128)S(1)} %get-tuple-element.37), channel_id=1, source_target_pairs={{0,3},{1,0},{2,1},{3,2},{4,7},{5,4},{6,5},{7,6},{8,11},{9,8},{10,9... | collective-permute-start | bytes 98312 | tf_op jit(solution)/shard_map/ppermute | solution.py:44
  109.4 5.5 %collective-permute-start.36 = (f32[32,256]{1,0:T(8,128)S(1)}, f32[32,256]{1,0:T(8,128)S(1)}, u32[]{:S(2)}, u32[]{:S(2)}) collective-permute-start(f32[32,256]{1,0:T(8,128)S(1)} %add_add_fusion.4), channel_id=1, source_target_pairs={{0,32},{8,40},{16,48},{24,56},{32,0},{40,8},{48,16},{56,24},{64,96... | collective-permute-start | bytes 98312 | tf_op jit(solution)/shard_map/ppermute | solution.py:36
  110.3 4.7 %collective-permute-start.37 = (f32[32,256]{1,0:T(8,128)S(1)}, f32[32,256]{1,0:T(8,128)S(1)}, u32[]{:S(2)}, u32[]{:S(2)}) collective-permute-start(f32[32,256]{1,0:T(8,128)S(1)} %add_add_fusion.4), channel_id=1, source_target_pairs={{0,16},{8,24},{16,32},{24,40},{32,48},{40,56},{48,0},{56,8},{64,80... | collective-permute-start | bytes 98312 | tf_op jit(solution)/shard_map/ppermute | solution.py:36
  112.7 3.9 %collective-permute-start.38 = (f32[32,256]{1,0:T(8,128)S(1)}, f32[32,256]{1,0:T(8,128)S(1)}, u32[]{:S(2)}, u32[]{:S(2)}) collective-permute-start(f32[32,256]{1,0:T(8,128)S(1)} %add_add_fusion.4), channel_id=1, source_target_pairs={{0,48},{8,56},{16,0},{24,8},{32,16},{40,24},{48,32},{56,40},{64,11... | collective-permute-start | bytes 98312 | tf_op jit(solution)/shard_map/ppermute | solution.py:36
  116.6 4.0 %collective-permute-start.39 = (f32[32,256]{1,0:T(8,128)S(1)}, f32[32,256]{1,0:T(8,128)S(1)}, u32[]{:S(2)}, u32[]{:S(2)}) collective-permute-start(f32[32,256]{1,0:T(8,128)S(1)} %add_add_fusion.3), channel_id=1, source_target_pairs={{0,4},{1,5},{2,6},{3,7},{4,0},{5,1},{6,2},{7,3},{8,12},{9,13},{10,... | collective-permute-start | bytes 98312 | tf_op jit(solution)/shard_map/ppermute | solution.py:48
  120.6 8.2 %collective-permute-start.40 = (f32[32,256]{1,0:T(8,128)S(1)}, f32[32,256]{1,0:T(8,128)S(1)}, u32[]{:S(2)}, u32[]{:S(2)}) collective-permute-start(f32[32,256]{1,0:T(8,128)S(1)} %add.164), channel_id=1, source_target_pairs={{0,128},{8,136},{16,144},{24,152},{32,160},{40,168},{48,176},{56,1... | collective-permute-start | bytes 98312 | tf_op jit(solution)/shard_map/ppermute | solution.py:32
  124.7 6.0 %collective-permute-start.41 = (f32[32,256]{1,0:T(8,128)S(1)}, f32[32,256]{1,0:T(8,128)S(1)}, u32[]{:S(2)}, u32[]{:S(2)}) collective-permute-start(f32[32,256]{1,0:T(8,128)S(1)} %add.164), channel_id=1, source_target_pairs={{0,64},{8,72},{16,80},{24,88},{32,96},{40,104},{48,112},{56,120},{... | collective-permute-start | bytes 98312 | tf_op jit(solution)/shard_map/ppermute | solution.py:32
  125.5 5.2 %collective-permute-start.42 = (f32[32,256]{1,0:T(8,128)S(1)}, f32[32,256]{1,0:T(8,128)S(1)}, u32[]{:S(2)}, u32[]{:S(2)}) collective-permute-start(f32[32,256]{1,0:T(8,128)S(1)} %add.164), channel_id=1, source_target_pairs={{0,192},{8,200},{16,208},{24,216},{32,224},{40,232},{48,240},{56,2... | collective-permute-start | bytes 98312 | tf_op jit(solution)/shard_map/ppermute | solution.py:32
  130.8 1.3 collective-permute-start.43
  132.1 6.3 %collective-permute-start.44 = (f32[2,32,256]{2,1,0:T(8,128)S(1)}, f32[2,32,256]{2,1,0:T(8,128)S(1)}, u32[]{:S(2)}, u32[]{:S(2)}) collective-permute-start(f32[2,32,256]{2,1,0:T(8,128)S(1)} %pad_maximum_fusion.2.piece0), channel_id=1, source_target_pairs={{0,3},{1,0},{2,1},{3,2},{4,7},{5,4},{6,5},{7,6},{8,11},{9,8},{10,9... | collective-permute-start | bytes 196616 | tf_op jit(solution)/shard_map/ppermute | solution.py:44
  135.3 6.1 %collective-permute-start.45 = (f32[2,32,256]{2,1,0:T(8,128)S(1)}, f32[2,32,256]{2,1,0:T(8,128)S(1)}, u32[]{:S(2)}, u32[]{:S(2)}) collective-permute-start(f32[2,32,256]{2,1,0:T(8,128)S(1)} %pad_maximum_fusion.2.piece0), channel_id=1, source_target_pairs={{0,2},{1,3},{2,0},{3,1},{4,6},{5,7},{6,4},{7,5},{8,10},{9,11},{10,... | collective-permute-start | bytes 196616 | tf_op jit(solution)/shard_map/ppermute | solution.py:44
  135.3 6.5 %collective-permute-start.46 = (f32[2,32,256]{2,1,0:T(8,128)S(1)}, f32[2,32,256]{2,1,0:T(8,128)S(1)}, u32[]{:S(2)}, u32[]{:S(2)}) collective-permute-start(f32[2,32,256]{2,1,0:T(8,128)S(1)} %pad_maximum_fusion.2.piece0), channel_id=1, source_target_pairs={{0,1},{1,2},{2,3},{3,0},{4,5},{5,6},{6,7},{7,4},{8,9},{9,10},{10,1... | collective-permute-start | bytes 196616 | tf_op jit(solution)/shard_map/ppermute | solution.py:44

commit v4 on v2

--- a/solution.py
+++ b/solution.py
@@ -28,11 +28,11 @@
 
 
 def to_z(v, k):
-    return lax.ppermute(v, "row", row_pairs(lambda z, x, c: (z + k, x, c)))
+    return lax.ppermute(v, "row", row_pairs(lambda z, x, c: (z + (1 - 2 * c) * k, x, c)))
 
 
 def to_x(v, k):
-    return lax.ppermute(v, "row", row_pairs(lambda z, x, c: (z, x + k, c)))
+    return lax.ppermute(v, "row", row_pairs(lambda z, x, c: (z, x + (1 - 2 * c) * k, c)))
 
 
 def to_core(v):
@@ -111,7 +111,8 @@
 
 def col_spot(table, cp):
     r = table[3, 0]
-    zk, xk, cx = ((cp >> 3) - (r >> 3)) & 3, ((cp >> 1) - (r >> 1)) & 3, (cp ^ r) & 1
+    way = 1 - 2 * (cp & 1)
+    zk, xk, cx = (((cp >> 3) - (r >> 3)) * way) & 3, (((cp >> 1) - (r >> 1)) * way) & 3, (cp ^ r) & 1
     return cx * N_X * N_ZH + xk * N_ZH + zk
 
 

time: 155 us -> 151 us (0.974)
  the two profiles are of different devices: /device:TPU:2 before, /device:TPU:1 now
where the time goes in v4:
time: 151 us
  starting transfers between devices  74.7 us (49%)
  waiting for transfers between devices  53.4 us (35%)
  Pallas kernels  18 us (12%)
  other arithmetic  3.06 us (2%)
    ppermute x9, waiting for transfers between devices, to_x(): lax.ppermute(v, 'row', row_pairs(lambda z, x, c: (z, x + (1 - 2 * c) * k,...  22.7 us
    ppermute x9, starting transfers between devices, to_z(): lax.ppermute(v, 'row', row_pairs(lambda z, x, c: (z + (1 - 2 * c) * k, x,...  19.4 us
    ppermute x12, starting transfers between devices, to_y(): lax.ppermute(v, 'col', [(col_at(zl, y), col_at(zl, y + k)) for zl in rang...  19.3 us
    ppermute x10, starting transfers between devices, to_core(): return lax.ppermute(v, 'row', row_pairs(lambda z, x, c: (z, x, 1 - c)))  19.2 us
    ppermute x9, waiting for transfers between devices, to_z(): lax.ppermute(v, 'row', row_pairs(lambda z, x, c: (z + (1 - 2 * c) * k, x,...  16.5 us
    pallas_call x1, Pallas kernels, factor_and_basis(): pl.pallas_call(factor_kernel, out_shape=(jax.ShapeDtypeStruct((edge, size...  11.2 us
    ppermute x9, starting transfers between devices, to_x(): lax.ppermute(v, 'row', row_pairs(lambda z, x, c: (z, x + (1 - 2 * c) * k,...  10.6 us
    ppermute x12, waiting for transfers between devices, to_y(): lax.ppermute(v, 'col', [(col_at(zl, y), col_at(zl, y + k)) for zl in rang...  9.84 us
  transfers between devices with their start and end apart: 43, of which 23 were waited for; matrix products, arithmetic and copies ran while one was open for 2% of the time, Pallas kernels for 4%

profile of v4, /device:TPU:1, one launch (start us, length us, event | category | flops | bytes accessed | tf_op | source)
XLA Modules:
  0.0 151.2 jit_solution(8588691751469978498)
XLA Ops:
  0.6 2.5 %collective-permute-start.14 = (bf16[128,256]{1,0:T(8,128)(2,1)}, bf16[128,256]{1,0:T(8,128)(2,1)S(1)}, u32[]{:S(2)}, u32[]{:S(2)}) collective-permute-start(bf16[128,256]{1,0:T(8,128)(2,1)} %param.9), channel_id=1, source_target_pairs={{0,4},{1,5},{2,6},{3,7},{4,0},{5,1},{6,2},{7,3},{8,12},{9,13},{10,... | collective-permute-start | bytes 196616 | tf_op jit(solution)/shard_map/ppermute | solution.py:47
  3.2 5.1 %collective-permute-start.2 = (bf16[128,256]{1,0:T(8,128)(2,1)}, bf16[128,256]{1,0:T(8,128)(2,1)S(1)}, u32[]{:S(2)}, u32[]{:S(2)}) collective-permute-start(bf16[128,256]{1,0:T(8,128)(2,1)} %param.9), channel_id=1, source_target_pairs={{0,64},{8,200},{16,80},{24,216},{32,96},{40,232},{48,112},{56,248}... | collective-permute-start | bytes 196616 | tf_op jit(solution)/shard_map/ppermute | solution.py:31
  8.3 1.2 collective-permute-start.1
  9.5 2.1 %collective-permute-start = (bf16[128,256]{1,0:T(8,128)(2,1)}, bf16[128,256]{1,0:T(8,128)(2,1)S(1)}, u32[]{:S(2)}, u32[]{:S(2)}) collective-permute-start(bf16[128,256]{1,0:T(8,128)(2,1)} %param.9), channel_id=1, source_target_pairs={{0,192},{8,72},{16,208},{24,88},{32,224},{40,104},{48,240},{56,120... | collective-permute-start | bytes 196616 | tf_op jit(solution)/shard_map/ppermute | solution.py:31
  12.4 2.8 %collective-permute-start.15 = (bf16[2,128,256]{2,1,0:T(8,128)(2,1)S(1)}, bf16[2,128,256]{2,1,0:T(8,128)(2,1)S(1)}, u32[]{:S(2)}, u32[]{:S(2)}) collective-permute-start(bf16[2,128,256]{2,1,0:T(8,128)(2,1)S(1)} %pad_maximum_fusion.1.refs_0_), channel_id=1, source_target_pairs={{0,3},{1,0},{2,1},{3,2},{4,7},{5,4},{6,5},{7,6},{8,11},{9,8},{10,9... | collective-permute-start | bytes 393224 | tf_op jit(solution)/shard_map/ppermute | solution.py:43
  15.3 1.8 %collective-permute-done.1 = bf16[128,256]{1,0:T(8,128)(2,1)S(1)} collective-permute-done((bf16[128,256]{1,0:T(8,128)(2,1)}, bf16[128,256]{1,0:T(8,128)(2,1)S(1)}, u32[]{:S(2)}, u32[]{:S(2)}) %collective-permute-start.1) | collective-permute-done | bytes 65568 | tf_op jit(solution)/shard_map/ppermute | solution.py:31
  18.2 1.3 collective-permute-start.3
  20.2 2.9 %collective-permute-start.16 = (bf16[2,128,256]{2,1,0:T(8,128)(2,1)S(1)}, bf16[2,128,256]{2,1,0:T(8,128)(2,1)S(1)}, u32[]{:S(2)}, u32[]{:S(2)}) collective-permute-start(bf16[2,128,256]{2,1,0:T(8,128)(2,1)S(1)} %pad_maximum_fusion.1.refs_0_), channel_id=1, source_target_pairs={{0,2},{1,3},{2,0},{3,1},{4,6},{5,7},{6,4},{7,5},{8,10},{9,11},{10,... | collective-permute-start | bytes 393224 | tf_op jit(solution)/shard_map/ppermute | solution.py:43
  23.6 2.5 %collective-permute-start.4 = (bf16[4,128,256]{2,1,0:T(8,128)(2,1)S(1)}, bf16[4,128,256]{2,1,0:T(8,128)(2,1)S(1)}, u32[]{:S(2)}, u32[]{:S(2)}) collective-permute-start(bf16[4,128,256]{2,1,0:T(8,128)(2,1)S(1)} %pad_maximum_fusion.refs_0_), channel_id=1, source_target_pairs={{0,32},{8,40},{16,48},{24,56},{32,0},{40,8},{48,16},{56,24},{64,96... | collective-permute-start | bytes 786440 | tf_op jit(solution)/shard_map/ppermute | solution.py:35
  27.9 1.8 %collective-permute-start.6 = (bf16[4,128,256]{2,1,0:T(8,128)(2,1)S(1)}, bf16[4,128,256]{2,1,0:T(8,128)(2,1)S(1)}, u32[]{:S(2)}, u32[]{:S(2)}) collective-permute-start(bf16[4,128,256]{2,1,0:T(8,128)(2,1)S(1)} %pad_maximum_fusion.refs_0_), channel_id=1, source_target_pairs={{0,8},{8,0},{16,24},{24,16},{32,40},{40,32},{48,56},{56,48},{64,72... | collective-permute-start | bytes 786440 | tf_op jit(solution)/shard_map/ppermute | solution.py:39
  29.7 3.7 %shard_map.69 = (f32[4,128,256]{2,1,0:T(8,128)S(1)}, f32[4,128,256]{2,1,0:T(8,128)S(1)}, f32[4,128,256]{2,1,0:T(8,128)S(1)}, f32[4,128,256]{2,1,0:T(8,128)S(1)},...) custom-call(s32[4,64]{1,0:T(4,128)S(1)} %pad_add_fusion.table, ...), custom_call_target="tpu_custom_call" | custom-call | flops 536870912 | bytes 6815744 | tf_op jit(solution)/shard_map/pallas_call | solution.py:156
  33.4 3.1 %collective-permute-start.21 = (f32[4,128,256]{2,1,0:T(8,128)S(1)}, f32[4,128,256]{2,1,0:T(8,128)S(1)}, u32[]{:S(2)}, u32[]{:S(2)}) collective-permute-start(f32[4,128,256]{2,1,0:T(8,128)S(1)} %get-tuple-element.23), channel_id=1, source_target_pairs={{0,8},{8,0},{16,24},{24,16},{32,40},{40,32},{48,56},{56,48},{64,72... | collective-permute-start | bytes 1572872 | tf_op jit(solution)/shard_map/ppermute | solution.py:39
  38.8 3.1 %shard_map.68 = (f32[2,128,256]{2,1,0:T(8,128)S(1)}, f32[2,128,256]{2,1,0:T(8,128)S(1)}, f32[2,128,256]{2,1,0:T(8,128)S(1)}, f32[2,128,256]{2,1,0:T(8,128)S(1)}) custom-call(s32[4,64]{1,0:T(4,128)S(1)} %pad_add_fusion.table, bf16[64,128,128]{2,1,0:T(8,128)(2,1)} %bitcast.37, bf16[4,128,256]{2,1,0:T(8,128)(2,1)S(1)} %pad_maximum_fusion.refs_0_, ...), custom_call_target="tpu_custom_call" | custom-call | flops 536870912 | bytes 5242880 | tf_op jit(solution)/shard_map/pallas_call | solution.py:156
  42.0 1.8 %collective-permute-start.11 = (f32[2,128,256]{2,1,0:T(8,128)S(1)}, f32[2,128,256]{2,1,0:T(8,128)S(1)}, u32[]{:S(2)}, u32[]{:S(2)}) collective-permute-start(f32[2,128,256]{2,1,0:T(8,128)S(1)} %get-tuple-element.16), channel_id=1, source_target_pairs={{0,1},{1,2},{2,3},{3,0},{4,5},{5,6},{6,7},{7,4},{8,9},{9,10},{10,1... | collective-permute-start | bytes 786440 | tf_op jit(solution)/shard_map/ppermute | solution.py:43
  43.7 1.2 collective-permute-start.12
  44.9 2.1 %collective-permute-start.10 = (f32[2,128,256]{2,1,0:T(8,128)S(1)}, f32[2,128,256]{2,1,0:T(8,128)S(1)}, u32[]{:S(2)}, u32[]{:S(2)}) collective-permute-start(f32[2,128,256]{2,1,0:T(8,128)S(1)} %get-tuple-element.15), channel_id=1, source_target_pairs={{0,2},{1,3},{2,0},{3,1},{4,6},{5,7},{6,4},{7,5},{8,10},{9,11},{10,... | collective-permute-start | bytes 786440 | tf_op jit(solution)/shard_map/ppermute | solution.py:43
  47.1 2.7 %collective-permute-start.18 = (f32[4,128,256]{2,1,0:T(8,128)S(1)}, f32[4,128,256]{2,1,0:T(8,128)S(1)}, u32[]{:S(2)}, u32[]{:S(2)}) collective-permute-start(f32[4,128,256]{2,1,0:T(8,128)S(1)} %get-tuple-element.19), channel_id=1, source_target_pairs={{0,8},{8,0},{16,24},{24,16},{32,40},{40,32},{48,56},{56,48},{64,72... | collective-permute-start | bytes 1572872 | tf_op jit(solution)/shard_map/ppermute | solution.py:39
  49.9 2.9 %collective-permute-start.22 = (f32[4,128,256]{2,1,0:T(8,128)S(1)}, f32[4,128,256]{2,1,0:T(8,128)S(1)}, u32[]{:S(2)}, u32[]{:S(2)}) collective-permute-start(f32[4,128,256]{2,1,0:T(8,128)S(1)} %add.112), channel_id=1, source_target_pairs={{0,16},{8,56},{16,32},{24,8},{32,48},{40,24},{48,0},{56,40},{64,80... | collective-permute-start | bytes 1572872 | tf_op jit(solution)/shard_map/ppermute | solution.py:35
  53.0 1.2 collective-permute-start.20
  54.2 2.5 %collective-permute-done.10 = f32[2,128,256]{2,1,0:T(8,128)S(1)} collective-permute-done((f32[2,128,256]{2,1,0:T(8,128)S(1)}, f32[2,128,256]{2,1,0:T(8,128)S(1)}, u32[]{:S(2)}, u32[]{:S(2)}) %collective-permute-start.10) | collective-permute-done | bytes 262176 | tf_op jit(solution)/shard_map/ppermute | solution.py:43
  56.8 2.4 %collective-permute-start.13 = (f32[128,256]{1,0:T(8,128)S(1)}, f32[128,256]{1,0:T(8,128)S(1)}, u32[]{:S(2)}, u32[]{:S(2)}) collective-permute-start(f32[128,256]{1,0:T(8,128)S(1)} %slice_bitcast_fusion.4), channel_id=1, source_target_pairs={{0,4},{1,5},{2,6},{3,7},{4,0},{5,1},{6,2},{7,3},{8,12},{9,13},{10,... | collective-permute-start | bytes 393224 | tf_op jit(solution)/shard_map/ppermute | solution.py:47
  59.2 4.0 %collective-permute-done.22 = f32[4,128,256]{2,1,0:T(8,128)S(1)} collective-permute-done((f32[4,128,256]{2,1,0:T(8,128)S(1)}, f32[4,128,256]{2,1,0:T(8,128)S(1)}, u32[]{:S(2)}, u32[]{:S(2)}) %collective-permute-start.22) | collective-permute-done | bytes 524320 | tf_op jit(solution)/shard_map/ppermute | solution.py:35
  63.2 2.1 %collective-permute-done.24 = f32[4,128,256]{2,1,0:T(8,128)S(1)} collective-permute-done((f32[4,128,256]{2,1,0:T(8,128)S(1)}, f32[4,128,256]{2,1,0:T(8,128)S(1)}, u32[]{:S(2)}, u32[]{:S(2)}) %collective-permute-start.24) | collective-permute-done | bytes 524320 | tf_op jit(solution)/shard_map/ppermute | solution.py:35
  65.3 12.3 %collective-permute-done.20 = f32[4,128,256]{2,1,0:T(8,128)S(1)} collective-permute-done((f32[4,128,256]{2,1,0:T(8,128)S(1)}, f32[4,128,256]{2,1,0:T(8,128)S(1)}, u32[]{:S(2)}, u32[]{:S(2)}) %collective-permute-start.20) | collective-permute-done | bytes 524320 | tf_op jit(solution)/shard_map/ppermute | solution.py:35
  77.8 2.3 %collective-permute-start.25 = (f32[128,256]{1,0:T(8,128)S(1)}, f32[128,256]{1,0:T(8,128)S(1)}, u32[]{:S(2)}, u32[]{:S(2)}) collective-permute-start(f32[128,256]{1,0:T(8,128)S(1)} %get-tuple-element.28), channel_id=1, source_target_pairs={{0,128},{8,136},{16,144},{24,152},{32,160},{40,168},{48,176},{56,1... | collective-permute-start | bytes 393224 | tf_op jit(solution)/shard_map/ppermute | solution.py:31
  80.1 4.2 %collective-permute-start.26 = (f32[128,256]{1,0:T(8,128)S(1)}, f32[128,256]{1,0:T(8,128)S(1)}, u32[]{:S(2)}, u32[]{:S(2)}) collective-permute-start(f32[128,256]{1,0:T(8,128)S(1)} %get-tuple-element.27), channel_id=1, source_target_pairs={{0,64},{8,200},{16,80},{24,216},{32,96},{40,232},{48,112},{56,248}... | collective-permute-start | bytes 393224 | tf_op jit(solution)/shard_map/ppermute | solution.py:31
  84.3 4.6 %collective-permute-done.25 = f32[128,256]{1,0:T(8,128)S(1)} collective-permute-done((f32[128,256]{1,0:T(8,128)S(1)}, f32[128,256]{1,0:T(8,128)S(1)}, u32[]{:S(2)}, u32[]{:S(2)}) %collective-permute-start.25) | collective-permute-done | bytes 131104 | tf_op jit(solution)/shard_map/ppermute | solution.py:31
  89.0 4.6 %collective-permute-done.26 = f32[128,256]{1,0:T(8,128)S(1)} collective-permute-done((f32[128,256]{1,0:T(8,128)S(1)}, f32[128,256]{1,0:T(8,128)S(1)}, u32[]{:S(2)}, u32[]{:S(2)}) %collective-permute-start.26) | collective-permute-done | bytes 131104 | tf_op jit(solution)/shard_map/ppermute | solution.py:31
  96.8 1.5 %collective-permute-start.30 = (f32[32,256]{1,0:T(8,128)S(1)}, f32[32,256]{1,0:T(8,128)S(1)}, u32[]{:S(2)}, u32[]{:S(2)}) collective-permute-start(f32[32,256]{1,0:T(8,128)S(1)} %get-tuple-element.31), channel_id=1, source_target_pairs={{0,1},{1,2},{2,3},{3,0},{4,5},{5,6},{6,7},{7,4},{8,9},{9,10},{10,1... | collective-permute-start | bytes 98312 | tf_op jit(solution)/shard_map/ppermute | solution.py:43
  98.3 1.2 collective-permute-start.31
  99.6 1.8 %collective-permute-start.29 = (f32[32,256]{1,0:T(8,128)S(1)}, f32[32,256]{1,0:T(8,128)S(1)}, u32[]{:S(2)}, u32[]{:S(2)}) collective-permute-start(f32[32,256]{1,0:T(8,128)S(1)} %get-tuple-element.29), channel_id=1, source_target_pairs={{0,2},{1,3},{2,0},{3,1},{4,6},{5,7},{6,4},{7,5},{8,10},{9,11},{10,... | collective-permute-start | bytes 98312 | tf_op jit(solution)/shard_map/ppermute | solution.py:43
  101.4 2.4 %collective-permute-done.29 = f32[32,256]{1,0:T(8,128)S(1)} collective-permute-done((f32[32,256]{1,0:T(8,128)S(1)}, f32[32,256]{1,0:T(8,128)S(1)}, u32[]{:S(2)}, u32[]{:S(2)}) %collective-permute-start.29) | collective-permute-done | bytes 32800 | tf_op jit(solution)/shard_map/ppermute | solution.py:43
  103.9 1.5 collective-permute-start.34
  105.4 1.3 collective-permute-done.33
  106.7 1.3 collective-permute-done.34
  108.0 1.7 %collective-permute-done.32 = f32[32,256]{1,0:T(8,128)S(1)} collective-permute-done((f32[32,256]{1,0:T(8,128)S(1)}, f32[32,256]{1,0:T(8,128)S(1)}, u32[]{:S(2)}, u32[]{:S(2)}) %collective-permute-start.32) | collective-permute-done | bytes 32800 | tf_op jit(solution)/shard_map/ppermute | solution.py:35
  109.7 1.3 collective-permute-start.35
  110.9 1.6 %collective-permute-done.35 = f32[32,256]{1,0:T(8,128)S(1)} collective-permute-done((f32[32,256]{1,0:T(8,128)S(1)}, f32[32,256]{1,0:T(8,128)S(1)}, u32[]{:S(2)}, u32[]{:S(2)}) %collective-permute-start.35) | collective-permute-done | bytes 32800 | tf_op jit(solution)/shard_map/ppermute | solution.py:47
  113.4 1.5 %collective-permute-start.38 = (f32[32,256]{1,0:T(8,128)S(1)}, f32[32,256]{1,0:T(8,128)S(1)}, u32[]{:S(2)}, u32[]{:S(2)}) collective-permute-start(f32[32,256]{1,0:T(8,128)S(1)} %add.136), channel_id=1, source_target_pairs={{0,192},{8,72},{16,208},{24,88},{32,224},{40,104},{48,240},{56,120... | collective-permute-start | bytes 98312 | tf_op jit(solution)/shard_map/ppermute | solution.py:31
  114.9 2.1 %collective-permute-start.36 = (f32[32,256]{1,0:T(8,128)S(1)}, f32[32,256]{1,0:T(8,128)S(1)}, u32[]{:S(2)}, u32[]{:S(2)}) collective-permute-start(f32[32,256]{1,0:T(8,128)S(1)} %add.136), channel_id=1, source_target_pairs={{0,128},{8,136},{16,144},{24,152},{32,160},{40,168},{48,176},{56,1... | collective-permute-start | bytes 98312 | tf_op jit(solution)/shard_map/ppermute | solution.py:31
  117.0 1.3 collective-permute-done.38
  118.4 3.3 %collective-permute-done.36 = f32[32,256]{1,0:T(8,128)S(1)} collective-permute-done((f32[32,256]{1,0:T(8,128)S(1)}, f32[32,256]{1,0:T(8,128)S(1)}, u32[]{:S(2)}, u32[]{:S(2)}) %collective-permute-start.36) | collective-permute-done | bytes 32800 | tf_op jit(solution)/shard_map/ppermute | solution.py:31
  121.7 9.0 %collective-permute-start.39 = (f32[32,256]{1,0:T(8,128)S(1)}, f32[32,256]{1,0:T(8,128)S(1)}, u32[]{:S(2)}, u32[]{:S(2)}) collective-permute-start(f32[32,256]{1,0:T(8,128)S(1)} %add_add_fusion.2), channel_id=1, source_target_pairs={{0,8},{8,0},{16,24},{24,16},{32,40},{40,32},{48,56},{56,48},{64,72... | collective-permute-start | bytes 98312 | tf_op jit(solution)/shard_map/ppermute | solution.py:39
  131.6 1.4 collective-permute-start.40
  133.0 1.5 collective-permute-start.41
  135.2 2.4 %collective-permute-done.41.piece2 = f32[2,32,256]{2,1,0:T(8,128)S(1)} collective-permute-done((f32[2,32,256]{2,1,0:T(8,128)S(1)}, f32[2,32,256]{2,1,0:T(8,128)S(1)}, u32[]{:S(2)}, u32[]{:S(2)}) %collective-permute-start.41) | collective-permute-done | bytes 65568 | tf_op jit(solution)/shard_map/ppermute | solution.py:43
  137.6 2.4 %collective-permute-done.42.piece3 = f32[2,32,256]{2,1,0:T(8,128)S(1)} collective-permute-done((f32[2,32,256]{2,1,0:T(8,128)S(1)}, f32[2,32,256]{2,1,0:T(8,128)S(1)}, u32[]{:S(2)}, u32[]{:S(2)}) %collective-permute-start.42) | collective-permute-done | bytes 65568 | tf_op jit(solution)/shard_map/ppermute | solution.py:43
  140.0 11.2 %factor.1 = (f32[128,256]{1,0:T(8,128)}, f32[256,256]{1,0:T(8,128)}) custom-call(s32[4,64]{1,0:T(4,128)S(1)} %pad_add_fusion.table, f32[2,32,256]{2,1,0:T(8,128)S(1)} %pad_maximum_fusion.2.piece0, f32[2,32,256]{2,1,0:T(8,128)S(1)} %collective-permute-done.40.piece1, f32[2,32,256]{2,1,0:T(8,128)S(1)} %collective-permute-done.41.piece2, ...), custom_call_target="tpu_custom_call" | custom-call | tf_op jit(solution)/shard_map/factor/pallas_call | solution.py:269
  (63 shorter events, 13.2 us)
Async XLA Ops:
  0.6 10.9 %collective-permute-start.14 = (bf16[128,256]{1,0:T(8,128)(2,1)}, bf16[128,256]{1,0:T(8,128)(2,1)S(1)}, u32[]{:S(2)}, u32[]{:S(2)}) collective-permute-start(bf16[128,256]{1,0:T(8,128)(2,1)} %param.9), channel_id=1, source_target_pairs={{0,4},{1,5},{2,6},{3,7},{4,0},{5,1},{6,2},{7,3},{8,12},{9,13},{10,... | collective-permute-start | bytes 196616 | tf_op jit(solution)/shard_map/ppermute | solution.py:47
  3.2 12.1 %collective-permute-start.2 = (bf16[128,256]{1,0:T(8,128)(2,1)}, bf16[128,256]{1,0:T(8,128)(2,1)S(1)}, u32[]{:S(2)}, u32[]{:S(2)}) collective-permute-start(bf16[128,256]{1,0:T(8,128)(2,1)} %param.9), channel_id=1, source_target_pairs={{0,64},{8,200},{16,80},{24,216},{32,96},{40,232},{48,112},{56,248}... | collective-permute-start | bytes 196616 | tf_op jit(solution)/shard_map/ppermute | solution.py:31
  8.3 8.8 %collective-permute-start.1 = (bf16[128,256]{1,0:T(8,128)(2,1)}, bf16[128,256]{1,0:T(8,128)(2,1)S(1)}, u32[]{:S(2)}, u32[]{:S(2)}) collective-permute-start(bf16[128,256]{1,0:T(8,128)(2,1)} %param.9), channel_id=1, source_target_pairs={{0,128},{8,136},{16,144},{24,152},{32,160},{40,168},{48,176},{56,1... | collective-permute-start | bytes 196616 | tf_op jit(solution)/shard_map/ppermute | solution.py:31
  9.5 7.9 %collective-permute-start = (bf16[128,256]{1,0:T(8,128)(2,1)}, bf16[128,256]{1,0:T(8,128)(2,1)S(1)}, u32[]{:S(2)}, u32[]{:S(2)}) collective-permute-start(bf16[128,256]{1,0:T(8,128)(2,1)} %param.9), channel_id=1, source_target_pairs={{0,192},{8,72},{16,208},{24,88},{32,224},{40,104},{48,240},{56,120... | collective-permute-start | bytes 196616 | tf_op jit(solution)/shard_map/ppermute | solution.py:31
  12.4 13.6 %collective-permute-start.15 = (bf16[2,128,256]{2,1,0:T(8,128)(2,1)S(1)}, bf16[2,128,256]{2,1,0:T(8,128)(2,1)S(1)}, u32[]{:S(2)}, u32[]{:S(2)}) collective-permute-start(bf16[2,128,256]{2,1,0:T(8,128)(2,1)S(1)} %pad_maximum_fusion.1.refs_0_), channel_id=1, source_target_pairs={{0,3},{1,0},{2,1},{3,2},{4,7},{5,4},{6,5},{7,6},{8,11},{9,8},{10,9... | collective-permute-start | bytes 393224 | tf_op jit(solution)/shard_map/ppermute | solution.py:43
  18.2 11.5 %collective-permute-start.3 = (bf16[4,128,256]{2,1,0:T(8,128)(2,1)S(1)}, bf16[4,128,256]{2,1,0:T(8,128)(2,1)S(1)}, u32[]{:S(2)}, u32[]{:S(2)}) collective-permute-start(bf16[4,128,256]{2,1,0:T(8,128)(2,1)S(1)} %pad_maximum_fusion.refs_0_), channel_id=1, source_target_pairs={{0,48},{8,24},{16,0},{24,40},{32,16},{40,56},{48,32},{56,8},{64,11... | collective-permute-start | bytes 786440 | tf_op jit(solution)/shard_map/ppermute | solution.py:35
  20.2 7.7 %collective-permute-start.16 = (bf16[2,128,256]{2,1,0:T(8,128)(2,1)S(1)}, bf16[2,128,256]{2,1,0:T(8,128)(2,1)S(1)}, u32[]{:S(2)}, u32[]{:S(2)}) collective-permute-start(bf16[2,128,256]{2,1,0:T(8,128)(2,1)S(1)} %pad_maximum_fusion.1.refs_0_), channel_id=1, source_target_pairs={{0,2},{1,3},{2,0},{3,1},{4,6},{5,7},{6,4},{7,5},{8,10},{9,11},{10,... | collective-permute-start | bytes 393224 | tf_op jit(solution)/shard_map/ppermute | solution.py:43
  23.2 6.5 %collective-permute-start.17 = (bf16[2,128,256]{2,1,0:T(8,128)(2,1)S(1)}, bf16[2,128,256]{2,1,0:T(8,128)(2,1)S(1)}, u32[]{:S(2)}, u32[]{:S(2)}) collective-permute-start(bf16[2,128,256]{2,1,0:T(8,128)(2,1)S(1)} %pad_maximum_fusion.1.refs_0_), channel_id=1, source_target_pairs={{0,1},{1,2},{2,3},{3,0},{4,5},{5,6},{6,7},{7,4},{8,9},{9,10},{10,1... | collective-permute-start | bytes 393224 | tf_op jit(solution)/shard_map/ppermute | solution.py:43
  23.6 13.0 %collective-permute-start.4 = (bf16[4,128,256]{2,1,0:T(8,128)(2,1)S(1)}, bf16[4,128,256]{2,1,0:T(8,128)(2,1)S(1)}, u32[]{:S(2)}, u32[]{:S(2)}) collective-permute-start(bf16[4,128,256]{2,1,0:T(8,128)(2,1)S(1)} %pad_maximum_fusion.refs_0_), channel_id=1, source_target_pairs={{0,32},{8,40},{16,48},{24,56},{32,0},{40,8},{48,16},{56,24},{64,96... | collective-permute-start | bytes 786440 | tf_op jit(solution)/shard_map/ppermute | solution.py:35
  26.0 10.6 %collective-permute-start.5 = (bf16[4,128,256]{2,1,0:T(8,128)(2,1)S(1)}, bf16[4,128,256]{2,1,0:T(8,128)(2,1)S(1)}, u32[]{:S(2)}, u32[]{:S(2)}) collective-permute-start(bf16[4,128,256]{2,1,0:T(8,128)(2,1)S(1)} %pad_maximum_fusion.refs_0_), channel_id=1, source_target_pairs={{0,16},{8,56},{16,32},{24,8},{32,48},{40,24},{48,0},{56,40},{64,80... | collective-permute-start | bytes 786440 | tf_op jit(solution)/shard_map/ppermute | solution.py:35
  27.9 9.5 %collective-permute-start.6 = (bf16[4,128,256]{2,1,0:T(8,128)(2,1)S(1)}, bf16[4,128,256]{2,1,0:T(8,128)(2,1)S(1)}, u32[]{:S(2)}, u32[]{:S(2)}) collective-permute-start(bf16[4,128,256]{2,1,0:T(8,128)(2,1)S(1)} %pad_maximum_fusion.refs_0_), channel_id=1, source_target_pairs={{0,8},{8,0},{16,24},{24,16},{32,40},{40,32},{48,56},{56,48},{64,72... | collective-permute-start | bytes 786440 | tf_op jit(solution)/shard_map/ppermute | solution.py:39
  29.7 7.7 %collective-permute-start.7 = (bf16[4,128,256]{2,1,0:T(8,128)(2,1)S(1)}, bf16[4,128,256]{2,1,0:T(8,128)(2,1)S(1)}, u32[]{:S(2)}, u32[]{:S(2)}) collective-permute-start(bf16[4,128,256]{2,1,0:T(8,128)(2,1)S(1)} %collective-permute-done.3.refs_1_), channel_id=1, source_target_pairs={{0,8},{8,0},{16,24},{24,16},{32,40},{40,32},{48,56},{56,48},{64,72... | collective-permute-start | bytes 786440 | tf_op jit(solution)/shard_map/ppermute | solution.py:39
  33.4 11.5 %collective-permute-start.21 = (f32[4,128,256]{2,1,0:T(8,128)S(1)}, f32[4,128,256]{2,1,0:T(8,128)S(1)}, u32[]{:S(2)}, u32[]{:S(2)}) collective-permute-start(f32[4,128,256]{2,1,0:T(8,128)S(1)} %get-tuple-element.23), channel_id=1, source_target_pairs={{0,8},{8,0},{16,24},{24,16},{32,40},{40,32},{48,56},{56,48},{64,72... | collective-permute-start | bytes 1572872 | tf_op jit(solution)/shard_map/ppermute | solution.py:39
  36.5 1.9 %collective-permute-start.8 = (bf16[4,128,256]{2,1,0:T(8,128)(2,1)S(1)}, bf16[4,128,256]{2,1,0:T(8,128)(2,1)S(1)}, u32[]{:S(2)}, u32[]{:S(2)}) collective-permute-start(bf16[4,128,256]{2,1,0:T(8,128)(2,1)S(1)} %collective-permute-done.4.refs_2_), channel_id=1, source_target_pairs={{0,8},{8,0},{16,24},{24,16},{32,40},{40,32},{48,56},{56,48},{64,72... | collective-permute-start | bytes 786440 | tf_op jit(solution)/shard_map/ppermute | solution.py:39
  36.7 2.2 %collective-permute-start.9 = (bf16[4,128,256]{2,1,0:T(8,128)(2,1)S(1)}, bf16[4,128,256]{2,1,0:T(8,128)(2,1)S(1)}, u32[]{:S(2)}, u32[]{:S(2)}) collective-permute-start(bf16[4,128,256]{2,1,0:T(8,128)(2,1)S(1)} %collective-permute-done.5.refs_3_), channel_id=1, source_target_pairs={{0,8},{8,0},{16,24},{24,16},{32,40},{40,32},{48,56},{56,48},{64,72... | collective-permute-start | bytes 786440 | tf_op jit(solution)/shard_map/ppermute | solution.py:39
  37.4 9.7 %collective-permute-start.23 = (f32[4,128,256]{2,1,0:T(8,128)S(1)}, f32[4,128,256]{2,1,0:T(8,128)S(1)}, u32[]{:S(2)}, u32[]{:S(2)}) collective-permute-start(f32[4,128,256]{2,1,0:T(8,128)S(1)} %get-tuple-element.25), channel_id=1, source_target_pairs={{0,8},{8,0},{16,24},{24,16},{32,40},{40,32},{48,56},{56,48},{64,72... | collective-permute-start | bytes 1572872 | tf_op jit(solution)/shard_map/ppermute | solution.py:39
  37.4 12.5 %collective-permute-start.19 = (f32[4,128,256]{2,1,0:T(8,128)S(1)}, f32[4,128,256]{2,1,0:T(8,128)S(1)}, u32[]{:S(2)}, u32[]{:S(2)}) collective-permute-start(f32[4,128,256]{2,1,0:T(8,128)S(1)} %get-tuple-element.21), channel_id=1, source_target_pairs={{0,8},{8,0},{16,24},{24,16},{32,40},{40,32},{48,56},{56,48},{64,72... | collective-permute-start | bytes 1572872 | tf_op jit(solution)/shard_map/ppermute | solution.py:39
  42.0 11.0 %collective-permute-start.11 = (f32[2,128,256]{2,1,0:T(8,128)S(1)}, f32[2,128,256]{2,1,0:T(8,128)S(1)}, u32[]{:S(2)}, u32[]{:S(2)}) collective-permute-start(f32[2,128,256]{2,1,0:T(8,128)S(1)} %get-tuple-element.16), channel_id=1, source_target_pairs={{0,1},{1,2},{2,3},{3,0},{4,5},{5,6},{6,7},{7,4},{8,9},{9,10},{10,1... | collective-permute-start | bytes 786440 | tf_op jit(solution)/shard_map/ppermute | solution.py:43
  43.7 9.3 %collective-permute-start.12 = (f32[2,128,256]{2,1,0:T(8,128)S(1)}, f32[2,128,256]{2,1,0:T(8,128)S(1)}, u32[]{:S(2)}, u32[]{:S(2)}) collective-permute-start(f32[2,128,256]{2,1,0:T(8,128)S(1)} %get-tuple-element.17), channel_id=1, source_target_pairs={{0,3},{1,0},{2,1},{3,2},{4,7},{5,4},{6,5},{7,6},{8,11},{9,8},{10,9... | collective-permute-start | bytes 786440 | tf_op jit(solution)/shard_map/ppermute | solution.py:43
  44.9 11.8 %collective-permute-start.10 = (f32[2,128,256]{2,1,0:T(8,128)S(1)}, f32[2,128,256]{2,1,0:T(8,128)S(1)}, u32[]{:S(2)}, u32[]{:S(2)}) collective-permute-start(f32[2,128,256]{2,1,0:T(8,128)S(1)} %get-tuple-element.15), channel_id=1, source_target_pairs={{0,2},{1,3},{2,0},{3,1},{4,6},{5,7},{6,4},{7,5},{8,10},{9,11},{10,... | collective-permute-start | bytes 786440 | tf_op jit(solution)/shard_map/ppermute | solution.py:43
  47.1 12.1 %collective-permute-start.18 = (f32[4,128,256]{2,1,0:T(8,128)S(1)}, f32[4,128,256]{2,1,0:T(8,128)S(1)}, u32[]{:S(2)}, u32[]{:S(2)}) collective-permute-start(f32[4,128,256]{2,1,0:T(8,128)S(1)} %get-tuple-element.19), channel_id=1, source_target_pairs={{0,8},{8,0},{16,24},{24,16},{32,40},{40,32},{48,56},{56,48},{64,72... | collective-permute-start | bytes 1572872 | tf_op jit(solution)/shard_map/ppermute | solution.py:39
  49.9 13.3 %collective-permute-start.22 = (f32[4,128,256]{2,1,0:T(8,128)S(1)}, f32[4,128,256]{2,1,0:T(8,128)S(1)}, u32[]{:S(2)}, u32[]{:S(2)}) collective-permute-start(f32[4,128,256]{2,1,0:T(8,128)S(1)} %add.112), channel_id=1, source_target_pairs={{0,16},{8,56},{16,32},{24,8},{32,48},{40,24},{48,0},{56,40},{64,80... | collective-permute-start | bytes 1572872 | tf_op jit(solution)/shard_map/ppermute | solution.py:35
  52.9 12.4 %collective-permute-start.24 = (f32[4,128,256]{2,1,0:T(8,128)S(1)}, f32[4,128,256]{2,1,0:T(8,128)S(1)}, u32[]{:S(2)}, u32[]{:S(2)}) collective-permute-start(f32[4,128,256]{2,1,0:T(8,128)S(1)} %add.113), channel_id=1, source_target_pairs={{0,48},{8,24},{16,0},{24,40},{32,16},{40,56},{48,32},{56,8},{64,11... | collective-permute-start | bytes 1572872 | tf_op jit(solution)/shard_map/ppermute | solution.py:35
  53.0 24.6 %collective-permute-start.20 = (f32[4,128,256]{2,1,0:T(8,128)S(1)}, f32[4,128,256]{2,1,0:T(8,128)S(1)}, u32[]{:S(2)}, u32[]{:S(2)}) collective-permute-start(f32[4,128,256]{2,1,0:T(8,128)S(1)} %add.110), channel_id=1, source_target_pairs={{0,32},{8,40},{16,48},{24,56},{32,0},{40,8},{48,16},{56,24},{64,96... | collective-permute-start | bytes 1572872 | tf_op jit(solution)/shard_map/ppermute | solution.py:35
  56.8 27.5 %collective-permute-start.13 = (f32[128,256]{1,0:T(8,128)S(1)}, f32[128,256]{1,0:T(8,128)S(1)}, u32[]{:S(2)}, u32[]{:S(2)}) collective-permute-start(f32[128,256]{1,0:T(8,128)S(1)} %slice_bitcast_fusion.4), channel_id=1, source_target_pairs={{0,4},{1,5},{2,6},{3,7},{4,0},{5,1},{6,2},{7,3},{8,12},{9,13},{10,... | collective-permute-start | bytes 393224 | tf_op jit(solution)/shard_map/ppermute | solution.py:47
  77.8 11.2 %collective-permute-start.25 = (f32[128,256]{1,0:T(8,128)S(1)}, f32[128,256]{1,0:T(8,128)S(1)}, u32[]{:S(2)}, u32[]{:S(2)}) collective-permute-start(f32[128,256]{1,0:T(8,128)S(1)} %get-tuple-element.28), channel_id=1, source_target_pairs={{0,128},{8,136},{16,144},{24,152},{32,160},{40,168},{48,176},{56,1... | collective-permute-start | bytes 393224 | tf_op jit(solution)/shard_map/ppermute | solution.py:31
  80.1 13.5 %collective-permute-start.26 = (f32[128,256]{1,0:T(8,128)S(1)}, f32[128,256]{1,0:T(8,128)S(1)}, u32[]{:S(2)}, u32[]{:S(2)}) collective-permute-start(f32[128,256]{1,0:T(8,128)S(1)} %get-tuple-element.27), channel_id=1, source_target_pairs={{0,64},{8,200},{16,80},{24,216},{32,96},{40,232},{48,112},{56,248}... | collective-permute-start | bytes 393224 | tf_op jit(solution)/shard_map/ppermute | solution.py:31
  84.3 9.8 %collective-permute-start.27 = (f32[128,256]{1,0:T(8,128)S(1)}, f32[128,256]{1,0:T(8,128)S(1)}, u32[]{:S(2)}, u32[]{:S(2)}) collective-permute-start(f32[128,256]{1,0:T(8,128)S(1)} %get-tuple-element.26), channel_id=1, source_target_pairs={{0,192},{8,72},{16,208},{24,88},{32,224},{40,104},{48,240},{56,120... | collective-permute-start | bytes 393224 | tf_op jit(solution)/shard_map/ppermute | solution.py:31
  94.6 2.1 %collective-permute-start.28 = (f32[128,256]{1,0:T(8,128)S(1)}, f32[128,256]{1,0:T(8,128)S(1)}, u32[]{:S(2)}, u32[]{:S(2)}) collective-permute-start(f32[128,256]{1,0:T(8,128)S(1)} %constant_dynamic-slice_fusion.3), channel_id=1, source_target_pairs={{0,8},{8,0},{16,24},{24,16},{32,40},{40,32},{48,56},{56,48},{64,72... | collective-permute-start | bytes 393224 | tf_op jit(solution)/shard_map/ppermute | solution.py:39
  96.8 4.5 %collective-permute-start.30 = (f32[32,256]{1,0:T(8,128)S(1)}, f32[32,256]{1,0:T(8,128)S(1)}, u32[]{:S(2)}, u32[]{:S(2)}) collective-permute-start(f32[32,256]{1,0:T(8,128)S(1)} %get-tuple-element.31), channel_id=1, source_target_pairs={{0,1},{1,2},{2,3},{3,0},{4,5},{5,6},{6,7},{7,4},{8,9},{9,10},{10,1... | collective-permute-start | bytes 98312 | tf_op jit(solution)/shard_map/ppermute | solution.py:43
  98.3 3.1 %collective-permute-start.31 = (f32[32,256]{1,0:T(8,128)S(1)}, f32[32,256]{1,0:T(8,128)S(1)}, u32[]{:S(2)}, u32[]{:S(2)}) collective-permute-start(f32[32,256]{1,0:T(8,128)S(1)} %get-tuple-element.30), channel_id=1, source_target_pairs={{0,3},{1,0},{2,1},{3,2},{4,7},{5,4},{6,5},{7,6},{8,11},{9,8},{10,9... | collective-permute-start | bytes 98312 | tf_op jit(solution)/shard_map/ppermute | solution.py:43
  99.6 4.3 %collective-permute-start.29 = (f32[32,256]{1,0:T(8,128)S(1)}, f32[32,256]{1,0:T(8,128)S(1)}, u32[]{:S(2)}, u32[]{:S(2)}) collective-permute-start(f32[32,256]{1,0:T(8,128)S(1)} %get-tuple-element.29), channel_id=1, source_target_pairs={{0,2},{1,3},{2,0},{3,1},{4,6},{5,7},{6,4},{7,5},{8,10},{9,11},{10,... | collective-permute-start | bytes 98312 | tf_op jit(solution)/shard_map/ppermute | solution.py:43
  103.8 2.8 %collective-permute-start.33 = (f32[32,256]{1,0:T(8,128)S(1)}, f32[32,256]{1,0:T(8,128)S(1)}, u32[]{:S(2)}, u32[]{:S(2)}) collective-permute-start(f32[32,256]{1,0:T(8,128)S(1)} %add_add_fusion.4), channel_id=1, source_target_pairs={{0,16},{8,56},{16,32},{24,8},{32,48},{40,24},{48,0},{56,40},{64,80... | collective-permute-start | bytes 98312 | tf_op jit(solution)/shard_map/ppermute | solution.py:35
  103.9 4.1 %collective-permute-start.34 = (f32[32,256]{1,0:T(8,128)S(1)}, f32[32,256]{1,0:T(8,128)S(1)}, u32[]{:S(2)}, u32[]{:S(2)}) collective-permute-start(f32[32,256]{1,0:T(8,128)S(1)} %add_add_fusion.4), channel_id=1, source_target_pairs={{0,48},{8,24},{16,0},{24,40},{32,16},{40,56},{48,32},{56,8},{64,11... | collective-permute-start | bytes 98312 | tf_op jit(solution)/shard_map/ppermute | solution.py:35
  105.4 4.3 %collective-permute-start.32 = (f32[32,256]{1,0:T(8,128)S(1)}, f32[32,256]{1,0:T(8,128)S(1)}, u32[]{:S(2)}, u32[]{:S(2)}) collective-permute-start(f32[32,256]{1,0:T(8,128)S(1)} %add_add_fusion.4), channel_id=1, source_target_pairs={{0,32},{8,40},{16,48},{24,56},{32,0},{40,8},{48,16},{56,24},{64,96... | collective-permute-start | bytes 98312 | tf_op jit(solution)/shard_map/ppermute | solution.py:35
  109.7 2.9 %collective-permute-start.35 = (f32[32,256]{1,0:T(8,128)S(1)}, f32[32,256]{1,0:T(8,128)S(1)}, u32[]{:S(2)}, u32[]{:S(2)}) collective-permute-start(f32[32,256]{1,0:T(8,128)S(1)} %add_add_fusion.3), channel_id=1, source_target_pairs={{0,4},{1,5},{2,6},{3,7},{4,0},{5,1},{6,2},{7,3},{8,12},{9,13},{10,... | collective-permute-start | bytes 98312 | tf_op jit(solution)/shard_map/ppermute | solution.py:47
  112.5 4.5 %collective-permute-start.37 = (f32[32,256]{1,0:T(8,128)S(1)}, f32[32,256]{1,0:T(8,128)S(1)}, u32[]{:S(2)}, u32[]{:S(2)}) collective-permute-start(f32[32,256]{1,0:T(8,128)S(1)} %add.136), channel_id=1, source_target_pairs={{0,64},{8,200},{16,80},{24,216},{32,96},{40,232},{48,112},{56,248}... | collective-permute-start | bytes 98312 | tf_op jit(solution)/shard_map/ppermute | solution.py:31
  113.4 5.0 %collective-permute-start.38 = (f32[32,256]{1,0:T(8,128)S(1)}, f32[32,256]{1,0:T(8,128)S(1)}, u32[]{:S(2)}, u32[]{:S(2)}) collective-permute-start(f32[32,256]{1,0:T(8,128)S(1)} %add.136), channel_id=1, source_target_pairs={{0,192},{8,72},{16,208},{24,88},{32,224},{40,104},{48,240},{56,120... | collective-permute-start | bytes 98312 | tf_op jit(solution)/shard_map/ppermute | solution.py:31
  114.9 6.8 %collective-permute-start.36 = (f32[32,256]{1,0:T(8,128)S(1)}, f32[32,256]{1,0:T(8,128)S(1)}, u32[]{:S(2)}, u32[]{:S(2)}) collective-permute-start(f32[32,256]{1,0:T(8,128)S(1)} %add.136), channel_id=1, source_target_pairs={{0,128},{8,136},{16,144},{24,152},{32,160},{40,168},{48,176},{56,1... | collective-permute-start | bytes 98312 | tf_op jit(solution)/shard_map/ppermute | solution.py:31
  121.7 9.9 %collective-permute-start.39 = (f32[32,256]{1,0:T(8,128)S(1)}, f32[32,256]{1,0:T(8,128)S(1)}, u32[]{:S(2)}, u32[]{:S(2)}) collective-permute-start(f32[32,256]{1,0:T(8,128)S(1)} %add_add_fusion.2), channel_id=1, source_target_pairs={{0,8},{8,0},{16,24},{24,16},{32,40},{40,32},{48,56},{56,48},{64,72... | collective-permute-start | bytes 98312 | tf_op jit(solution)/shard_map/ppermute | solution.py:39
  131.6 3.6 %collective-permute-start.40 = (f32[2,32,256]{2,1,0:T(8,128)S(1)}, f32[2,32,256]{2,1,0:T(8,128)S(1)}, u32[]{:S(2)}, u32[]{:S(2)}) collective-permute-start(f32[2,32,256]{2,1,0:T(8,128)S(1)} %pad_maximum_fusion.2.piece0), channel_id=1, source_target_pairs={{0,3},{1,0},{2,1},{3,2},{4,7},{5,4},{6,5},{7,6},{8,11},{9,8},{10,9... | collective-permute-start | bytes 196616 | tf_op jit(solution)/shard_map/ppermute | solution.py:43
  133.0 4.6 %collective-permute-start.41 = (f32[2,32,256]{2,1,0:T(8,128)S(1)}, f32[2,32,256]{2,1,0:T(8,128)S(1)}, u32[]{:S(2)}, u32[]{:S(2)}) collective-permute-start(f32[2,32,256]{2,1,0:T(8,128)S(1)} %pad_maximum_fusion.2.piece0), channel_id=1, source_target_pairs={{0,2},{1,3},{2,0},{3,1},{4,6},{5,7},{6,4},{7,5},{8,10},{9,11},{10,... | collective-permute-start | bytes 196616 | tf_op jit(solution)/shard_map/ppermute | solution.py:43
  134.4 5.6 %collective-permute-start.42 = (f32[2,32,256]{2,1,0:T(8,128)S(1)}, f32[2,32,256]{2,1,0:T(8,128)S(1)}, u32[]{:S(2)}, u32[]{:S(2)}) collective-permute-start(f32[2,32,256]{2,1,0:T(8,128)S(1)} %pad_maximum_fusion.2.piece0), channel_id=1, source_target_pairs={{0,1},{1,2},{2,3},{3,0},{4,5},{5,6},{6,7},{7,4},{8,9},{9,10},{10,1... | collective-permute-start | bytes 196616 | tf_op jit(solution)/shard_map/ppermute | solution.py:43

commit v5 on v3

--- a/solution.py
+++ b/solution.py
@@ -1,3 +1,5 @@
+import math
+
 import jax
 import jax.numpy as jnp
 from jax import lax
@@ -13,7 +15,7 @@
 BLOCK, SUB, LANES = 64, 8, 128
 STEP = SUB
 CHUNK = 8
-FIRST = 96
+FIRST = 104
 
 
 def row_at(z, x, c):
@@ -127,23 +129,27 @@
         )
 
     slot_loop(table, blocks, tiles, sems, prepare, add)
-    part = N_X * N_ZH
-    for k in range(N_CORE * N_X):
-
-        def first(n, k=k):
-            outs[k][n] = acc[k * N_ZH + n, :FIRST]
+    part, edge = N_X * N_ZH, acc.shape[1]
+    for side in range(N_CORE):
+        flat, ones, threes = outs[side * 3 : side * 3 + 3]
+
+        def first(n, side=side, flat=flat, ones=ones, threes=threes):
+            base = side * part + n
+            ones[n] = acc[base + N_ZH, :FIRST]
+            threes[n] = acc[base + 3 * N_ZH, :FIRST]
+            flat[pl.ds(pl.multiple_of(n * FIRST, SUB), FIRST), :] = acc[base + 2 * N_ZH, :FIRST]
+            flat[pl.ds(pl.multiple_of((N_ZH + n) * FIRST, SUB), FIRST), :] = acc[base, :FIRST]
+
+        def second(n, side=side, flat=flat):
+            at = pl.multiple_of(2 * N_ZH * FIRST + n * (edge - FIRST), SUB)
+            flat[pl.ds(at, edge - FIRST), :] = acc[side * part + (n & (N_X - 1)) * N_ZH + n // N_X, FIRST:]
 
         each(N_ZH, first)
-    for k in range(N_CORE):
-
-        def second(n, k=k):
-            outs[N_CORE * N_X + k][n] = acc[k * part + (n & (N_X - 1)) * N_ZH + n // N_X, FIRST:]
-
         each(part, second)
 
 
 def direct_kernel(table, blocks, *refs):
-    n = N_X + 1
+    n = N_CORE * N_X
     pieces, outs, (vectors, acc, tiles, sems) = refs[:n], refs[n:-4], refs[-4:]
 
     def prepare():
@@ -168,10 +174,10 @@
 def products_of(kernel, table, blocks, pieces, outs):
     edge, width = pieces[0].shape[1:]
     vmem = pl.BlockSpec(memory_space=pltpu.VMEM)
-    n_in, n_acc = (sum(v.shape[0] for v in pieces), sum(n * rows for n, rows in outs) // edge)
+    n_in, n_acc = (sum(v.shape[0] for v in pieces), sum(math.prod(v) for v in outs) // edge)
     return pl.pallas_call(
         kernel,
-        out_shape=tuple(jax.ShapeDtypeStruct((n, rows, width), F32) for n, rows in outs),
+        out_shape=tuple(jax.ShapeDtypeStruct(v + (width,), F32) for v in outs),
         in_specs=[pl.BlockSpec(memory_space=pltpu.SMEM), pl.BlockSpec(memory_space=pltpu.HBM)] + [vmem] * len(pieces),
         out_specs=(vmem,) * len(outs),
         scratch_shapes=[
@@ -311,7 +317,7 @@
 
 
 def body(blocks, block_rows, block_cols, counts, trials):
-    edge, _ = trials.shape
+    edge, width = trials.shape
     r, c = lax.axis_index("row").astype(jnp.int32), lax.axis_index("col").astype(jnp.int32)
     slots = block_rows.shape[1]
     at = lax.broadcasted_iota(jnp.int32, (1, slots), 1)
@@ -327,16 +333,20 @@
         table,
         blocks[0],
         row_pieces,
-        [(N_ZH, FIRST)] * (N_CORE * N_X) + [(N_X * N_ZH, edge - FIRST)] * N_CORE,
+        ([(2 * N_ZH * FIRST + N_X * N_ZH * (edge - FIRST),)] + [(N_ZH, FIRST)] * 2) * N_CORE,
     )
-    keep, send, (keep_b, send_b) = outs[:N_X], outs[N_X : 2 * N_X], outs[2 * N_X :]
-    col_pieces = col_pieces + [to_core(jnp.concatenate(col_pieces, 0))]
+    keep, send = dict(zip((0, 1, 3), outs[:3])), dict(zip((0, 1, 3), outs[3:]))
+    col_pieces = col_pieces + [to_core(v) for v in col_pieces]
     row_outs = products_of(direct_kernel, table, blocks[0], col_pieces, [(N_ZL, edge)] * N_Y)
-    theirs = {k: to_core(send[k]) for k in (1, 3, 2, 0)}
-    pair = {k: keep[k] + theirs[k] for k in (1, 3, 2)}
+    theirs = {k: to_core(send[k]) for k in (1, 3)}
+    theirs[0] = to_core(send[0])
+    cut = N_ZH * FIRST
+    pair = {k: keep[k] + theirs[k] for k in (1, 3)}
+    pair[2] = (keep[0][:cut] + theirs[0][:cut]).reshape(N_ZH, FIRST, width)
     sent = {k: to_x(pair[k], k) for k in (1, 3, 2)}
-    got = ring_sum([keep[0] + theirs[0]] + [sent[k] for k in range(1, N_X)])
-    both = keep_b + to_core(send_b)
+    own = (keep[0][cut : 2 * cut] + theirs[0][cut : 2 * cut]).reshape(N_ZH, FIRST, width)
+    got = ring_sum([own] + [sent[k] for k in range(1, N_X)])
+    both = (keep[0][2 * cut :] + theirs[0][2 * cut :]).reshape(N_X * N_ZH, edge - FIRST, width)
     parts = [both[k * N_X : (k + 1) * N_X] for k in range(N_ZH)]
     got_b = ring_sum([parts[0]] + [to_z(parts[k], k) for k in range(1, N_ZH)])
     rows = ring_sum([row_outs[0]] + [to_y(row_outs[k], k) for k in range(1, N_Y)])

time: 155 us -> 158 us (1.019)
  waiting for transfers between devices: 44.7 us -> 50.4 us
  local copies, waits for them, and re-layouts: 5.76 us -> 0.93 us
  other arithmetic: 6.59 us -> 8.5 us
  Pallas kernels: 19.3 us -> 21 us
    ppermute x12, waiting for transfers between devices: 7.45 us -> 14.6 us  [to_y(): lax.ppermute(v, 'col', [(col_at(zl, y), col_at(zl, y + k)) for zl in rang...]
    unnamed x6 -> x2, local copies, waits for them, and re-layouts: 4.86 us -> 0.75 us
    ppermute x12, starting transfers between devices: 33.2 us -> 29.7 us  [to_z(): return lax.ppermute(v, 'row', row_pairs(lambda z, x, c: (z + k, x, c)))]
    ppermute x12, waiting for transfers between devices: 13.7 us -> 11.6 us  [to_x(): return lax.ppermute(v, 'row', row_pairs(lambda z, x, c: (z, x + k, c)))]
    add x4, other arithmetic: 2.53 us -> 4.54 us  [the longest x2 2.17 us: body(): pair = {k: keep[k] + theirs[k] for k in (1, 3)}]
    pallas_call x2, Pallas kernels: 8.1 us -> 9.82 us  [products_of(): pl.pallas_call(kernel, out_shape=tuple((jax.ShapeDtypeStruct(v + (width,)...]
    ppermute x8 -> x9, waiting for transfers between devices: 2.53 us -> 3.55 us  [to_core(): return lax.ppermute(v, 'row', row_pairs(lambda z, x, c: (z, x, 1 - c)))]
  transfers between devices with their start and end apart: 47 -> 48, of which waited for: 22 -> 23; matrix products, arithmetic and copies ran while one was open for 8% -> 5% of each run, Pallas kernels for 5% -> 6%
where the time goes in v5:
time: 158 us; the launch traced here: 157 us
  starting transfers between devices  74.6 us (47%)
  waiting for transfers between devices  50.4 us (32%)
  Pallas kernels  21 us (13%)
  other arithmetic  8.5 us (5%)
    ppermute x12, starting transfers between devices, to_z(): return lax.ppermute(v, 'row', row_pairs(lambda z, x, c: (z + k, x, c)))  29.7 us
    ppermute x12, starting transfers between devices, to_y(): lax.ppermute(v, 'col', [(col_at(zl, y), col_at(zl, y + k)) for zl in rang...  20.9 us
    ppermute x12, starting transfers between devices, to_x(): return lax.ppermute(v, 'row', row_pairs(lambda z, x, c: (z, x + k, c)))  17.3 us
    ppermute x12, waiting for transfers between devices, to_z(): return lax.ppermute(v, 'row', row_pairs(lambda z, x, c: (z + k, x, c)))  16.7 us
    ppermute x12, waiting for transfers between devices, to_y(): lax.ppermute(v, 'col', [(col_at(zl, y), col_at(zl, y + k)) for zl in rang...  14.6 us
    ppermute x12, waiting for transfers between devices, to_x(): return lax.ppermute(v, 'row', row_pairs(lambda z, x, c: (z, x + k, c)))  11.6 us
    pallas_call x1, Pallas kernels, factor_and_basis(): pl.pallas_call(factor_kernel, out_shape=(jax.ShapeDtypeStruct((edge, size...  11.2 us
    pallas_call x2, Pallas kernels, products_of(): pl.pallas_call(kernel, out_shape=tuple((jax.ShapeDtypeStruct(v + (width,)...  9.82 us
  transfers between devices with their start and end apart: 48, of which 23 were waited for; matrix products, arithmetic and copies ran while one was open for 5% of the time, Pallas kernels for 6%

profile of v5, /device:TPU:2, one launch (start us, length us, event | category | flops | bytes accessed | tf_op | source)
XLA Modules:
  0.0 157.4 jit_solution(12367530712729394944)
XLA Ops:
  0.6 2.0 %collective-permute-start.14 = (bf16[128,256]{1,0:T(8,128)(2,1)}, bf16[128,256]{1,0:T(8,128)(2,1)S(1)}, u32[]{:S(2)}, u32[]{:S(2)}) collective-permute-start(bf16[128,256]{1,0:T(8,128)(2,1)} %param.9), channel_id=1, source_target_pairs={{0,4},{1,5},{2,6},{3,7},{4,0},{5,1},{6,2},{7,3},{8,12},{9,13},{10,... | collective-permute-start | bytes 196616 | tf_op jit(solution)/shard_map/ppermute | solution.py:50
  2.6 6.3 %collective-permute-start.1 = (bf16[128,256]{1,0:T(8,128)(2,1)}, bf16[128,256]{1,0:T(8,128)(2,1)S(1)}, u32[]{:S(2)}, u32[]{:S(2)}) collective-permute-start(bf16[128,256]{1,0:T(8,128)(2,1)} %param.9), channel_id=1, source_target_pairs={{0,128},{8,136},{16,144},{24,152},{32,160},{40,168},{48,176},{56,1... | collective-permute-start | bytes 196616 | tf_op jit(solution)/shard_map/ppermute | solution.py:34
  9.5 2.4 %collective-permute-start.2 = (bf16[128,256]{1,0:T(8,128)(2,1)}, bf16[128,256]{1,0:T(8,128)(2,1)S(1)}, u32[]{:S(2)}, u32[]{:S(2)}) collective-permute-start(bf16[128,256]{1,0:T(8,128)(2,1)} %param.9), channel_id=1, source_target_pairs={{0,64},{8,72},{16,80},{24,88},{32,96},{40,104},{48,112},{56,120},{... | collective-permute-start | bytes 196616 | tf_op jit(solution)/shard_map/ppermute | solution.py:34
  12.7 1.7 %collective-permute-start.17 = (bf16[2,128,256]{2,1,0:T(8,128)(2,1)S(1)}, bf16[2,128,256]{2,1,0:T(8,128)(2,1)S(1)}, u32[]{:S(2)}, u32[]{:S(2)}) collective-permute-start(bf16[2,128,256]{2,1,0:T(8,128)(2,1)S(1)} %pad_maximum_fusion.1.refs_0_), channel_id=1, source_target_pairs={{0,1},{1,2},{2,3},{3,0},{4,5},{5,6},{6,7},{7,4},{8,9},{9,10},{10,1... | collective-permute-start | bytes 393224 | tf_op jit(solution)/shard_map/ppermute | solution.py:46
  14.4 2.9 %collective-permute-start.16 = (bf16[2,128,256]{2,1,0:T(8,128)(2,1)S(1)}, bf16[2,128,256]{2,1,0:T(8,128)(2,1)S(1)}, u32[]{:S(2)}, u32[]{:S(2)}) collective-permute-start(bf16[2,128,256]{2,1,0:T(8,128)(2,1)S(1)} %pad_maximum_fusion.1.refs_0_), channel_id=1, source_target_pairs={{0,2},{1,3},{2,0},{3,1},{4,6},{5,7},{6,4},{7,5},{8,10},{9,11},{10,... | collective-permute-start | bytes 393224 | tf_op jit(solution)/shard_map/ppermute | solution.py:46
  18.0 1.4 collective-permute-start.15
  20.4 1.6 collective-permute-start.5
  23.1 2.2 %collective-permute-start.3 = (bf16[4,128,256]{2,1,0:T(8,128)(2,1)S(1)}, bf16[4,128,256]{2,1,0:T(8,128)(2,1)S(1)}, u32[]{:S(2)}, u32[]{:S(2)}) collective-permute-start(bf16[4,128,256]{2,1,0:T(8,128)(2,1)S(1)} %pad_maximum_fusion.refs_0_), channel_id=1, source_target_pairs={{0,48},{8,56},{16,0},{24,8},{32,16},{40,24},{48,32},{56,40},{64,11... | collective-permute-start | bytes 786440 | tf_op jit(solution)/shard_map/ppermute | solution.py:38
  26.0 5.5 %shard_map.69 = (f32[1216,256]{1,0:T(8,128)S(1)}, f32[4,104,256]{2,1,0:T(8,128)S(1)}, f32[4,104,256]{2,1,0:T(8,128)S(1)}, f32[1216,256]{1,0:T(8,128)}, f32[4,104...) custom-call(s32[4,64]{1,0:T(4,128)S(1)} %pad_add_fusion.table, bf16[64,128,128]{2,1,0:T(8,128)(2,1)} %bitcast.52, ...), custom_call_target="tpu_custom_call" | custom-call | flops 536870912 | bytes 6815744 | tf_op jit(solution)/shard_map/pallas_call | solution.py:178
  32.7 4.1 %collective-permute-done.3.refs_1_ = bf16[4,128,256]{2,1,0:T(8,128)(2,1)S(1)} collective-permute-done((bf16[4,128,256]{2,1,0:T(8,128)(2,1)S(1)}, bf16[4,128,256]{2,1,0:T(8,128)(2,1)S(1)}, u32[]{:S(2)}, u32[]{:S(2)}) %collective-permute-start.3) | collective-permute-done | bytes 262176 | tf_op jit(solution)/shard_map/ppermute | solution.py:38
  38.3 4.3 %shard_map.68 = (f32[2,128,256]{2,1,0:T(8,128)S(1)}, f32[2,128,256]{2,1,0:T(8,128)S(1)}, f32[2,128,256]{2,1,0:T(8,128)}, f32[2,128,256]{2,1,0:T(8,128)S(1)}) custom-call(s32[4,64]{1,0:T(4,128)S(1)} %pad_add_fusion.table, bf16[64,128,128]{2,1,0:T(8,128)(2,1)} %bitcast.53, bf16[4,128,256]{2,1,0:T(8,128)(2,1)S(1)} %pad_maximum_fusion.refs_0_, ...), custom_call_target="tpu_custom_call" | custom-call | flops 536870912 | bytes 5242880 | tf_op jit(solution)/shard_map/pallas_call | solution.py:178
  42.6 1.4 collective-permute-start.10
  44.9 3.1 %collective-permute-start.12 = (f32[2,128,256]{2,1,0:T(8,128)S(1)}, f32[2,128,256]{2,1,0:T(8,128)}, u32[]{:S(2)}, u32[]{:S(2)}) collective-permute-start(f32[2,128,256]{2,1,0:T(8,128)S(1)} %get-tuple-element.15), channel_id=1, source_target_pairs={{0,3},{1,0},{2,1},{3,2},{4,7},{5,4},{6,5},{7,6},{8,11},{9,8},{10,9... | collective-permute-start | bytes 786440 | tf_op jit(solution)/shard_map/ppermute | solution.py:46
  49.1 1.7 %collective-permute-start.21 = (f32[4,104,256]{2,1,0:T(8,128)S(1)}, f32[4,104,256]{2,1,0:T(8,128)S(1)}, u32[]{:S(2)}, u32[]{:S(2)}) collective-permute-start(f32[4,104,256]{2,1,0:T(8,128)S(1)} %add.133), channel_id=1, source_target_pairs={{0,16},{8,24},{16,32},{24,40},{32,48},{40,56},{48,0},{56,8},{64,80... | collective-permute-start | bytes 1277960 | tf_op jit(solution)/shard_map/ppermute | solution.py:38
  51.9 1.9 %collective-permute-done.10 = f32[2,128,256]{2,1,0:T(8,128)} collective-permute-done((f32[2,128,256]{2,1,0:T(8,128)}, f32[2,128,256]{2,1,0:T(8,128)}, u32[]{:S(2)}, u32[]{:S(2)}) %collective-permute-start.10) | collective-permute-done | bytes 262176 | tf_op jit(solution)/shard_map/ppermute | solution.py:46
  54.8 3.5 %collective-permute-done.11 = f32[2,128,256]{2,1,0:T(8,128)} collective-permute-done((f32[2,128,256]{2,1,0:T(8,128)S(1)}, f32[2,128,256]{2,1,0:T(8,128)}, u32[]{:S(2)}, u32[]{:S(2)}) %collective-permute-start.11) | collective-permute-done | bytes 262176 | tf_op jit(solution)/shard_map/ppermute | solution.py:46
  58.3 1.2 add_add_fusion.1
  61.2 5.5 %collective-permute-start.27 = (f32[4,24,256]{2,1,0:T(8,128)S(1)}, f32[4,24,256]{2,1,0:T(8,128)S(1)}, u32[]{:S(2)}, u32[]{:S(2)}) collective-permute-start(f32[4,24,256]{2,1,0:T(8,128)S(1)} %bitcast.61), channel_id=1, source_target_pairs={{0,128},{8,136},{16,144},{24,152},{32,160},{40,168},{48,176},{56,1... | collective-permute-start | bytes 294920 | tf_op jit(solution)/shard_map/ppermute | solution.py:34
  66.7 1.3 slice_add_fusion
  68.2 3.1 %collective-permute-start.13 = (f32[128,256]{1,0:T(8,128)S(1)}, f32[128,256]{1,0:T(8,128)S(1)}, u32[]{:S(2)}, u32[]{:S(2)}) collective-permute-start(f32[128,256]{1,0:T(8,128)S(1)} %slice_bitcast_fusion), channel_id=1, source_target_pairs={{0,4},{1,5},{2,6},{3,7},{4,0},{5,1},{6,2},{7,3},{8,12},{9,13},{10,... | collective-permute-start | bytes 393224 | tf_op jit(solution)/shard_map/ppermute | solution.py:50
  71.2 1.4 collective-permute-done.27
  72.6 2.3 %collective-permute-start.19 = (f32[4,104,256]{2,1,0:T(8,128)S(1)}, f32[4,104,256]{2,1,0:T(8,128)S(1)}, u32[]{:S(2)}, u32[]{:S(2)}) collective-permute-start(f32[4,104,256]{2,1,0:T(8,128)S(1)} %bitcast.55), channel_id=1, source_target_pairs={{0,32},{8,40},{16,48},{24,56},{32,0},{40,8},{48,16},{56,24},{64,96... | collective-permute-start | bytes 1277960 | tf_op jit(solution)/shard_map/ppermute | solution.py:38
  76.0 1.6 collective-permute-start.32
  78.2 3.1 %collective-permute-start.30 = (f32[24,256]{1,0:T(8,128)S(1)}, f32[24,256]{1,0:T(8,128)S(1)}, u32[]{:S(2)}, u32[]{:S(2)}) collective-permute-start(f32[24,256]{1,0:T(8,128)S(1)} %get-tuple-element.36), channel_id=1, source_target_pairs={{0,32},{8,40},{16,48},{24,56},{32,0},{40,8},{48,16},{56,24},{64,96... | collective-permute-start | bytes 73736 | tf_op jit(solution)/shard_map/ppermute | solution.py:38
  81.2 1.6 collective-permute-done.19
  82.9 2.8 %collective-permute-start.26 = (f32[104,256]{1,0:T(8,128)S(1)}, f32[104,256]{1,0:T(8,128)S(1)}, u32[]{:S(2)}, u32[]{:S(2)}) collective-permute-start(f32[104,256]{1,0:T(8,128)S(1)} %get-tuple-element.24), channel_id=1, source_target_pairs={{0,192},{8,200},{16,208},{24,216},{32,224},{40,232},{48,240},{56,2... | collective-permute-start | bytes 319496 | tf_op jit(solution)/shard_map/ppermute | solution.py:34
  85.7 2.6 %collective-permute-start.25 = (f32[104,256]{1,0:T(8,128)S(1)}, f32[104,256]{1,0:T(8,128)S(1)}, u32[]{:S(2)}, u32[]{:S(2)}) collective-permute-start(f32[104,256]{1,0:T(8,128)S(1)} %get-tuple-element.25), channel_id=1, source_target_pairs={{0,64},{8,72},{16,80},{24,88},{32,96},{40,104},{48,112},{56,120},{... | collective-permute-start | bytes 319496 | tf_op jit(solution)/shard_map/ppermute | solution.py:34
  88.3 3.7 %collective-permute-start.24 = (f32[104,256]{1,0:T(8,128)S(1)}, f32[104,256]{1,0:T(8,128)S(1)}, u32[]{:S(2)}, u32[]{:S(2)}) collective-permute-start(f32[104,256]{1,0:T(8,128)S(1)} %get-tuple-element.26), channel_id=1, source_target_pairs={{0,128},{8,136},{16,144},{24,152},{32,160},{40,168},{48,176},{56,1... | collective-permute-start | bytes 319496 | tf_op jit(solution)/shard_map/ppermute | solution.py:34
  92.9 8.0 %collective-permute-done.24 = f32[104,256]{1,0:T(8,128)S(1)} collective-permute-done((f32[104,256]{1,0:T(8,128)S(1)}, f32[104,256]{1,0:T(8,128)S(1)}, u32[]{:S(2)}, u32[]{:S(2)}) %collective-permute-start.24) | collective-permute-done | bytes 106528 | tf_op jit(solution)/shard_map/ppermute | solution.py:34
  101.4 1.3 collective-permute-done.33
  102.8 2.4 %collective-permute-start.34 = (f32[32,256]{1,0:T(8,128)S(1)}, f32[32,256]{1,0:T(8,128)S(1)}, u32[]{:S(2)}, u32[]{:S(2)}) collective-permute-start(f32[32,256]{1,0:T(8,128)S(1)} %get-tuple-element.31), channel_id=1, source_target_pairs={{0,2},{1,3},{2,0},{3,1},{4,6},{5,7},{6,4},{7,5},{8,10},{9,11},{10,... | collective-permute-start | bytes 98312 | tf_op jit(solution)/shard_map/ppermute | solution.py:46
  105.2 4.8 %collective-permute-start.36 = (f32[32,256]{1,0:T(8,128)S(1)}, f32[32,256]{1,0:T(8,128)S(1)}, u32[]{:S(2)}, u32[]{:S(2)}) collective-permute-start(f32[32,256]{1,0:T(8,128)S(1)} %get-tuple-element.32), channel_id=1, source_target_pairs={{0,3},{1,0},{2,1},{3,2},{4,7},{5,4},{6,5},{7,6},{8,11},{9,8},{10,9... | collective-permute-start | bytes 98312 | tf_op jit(solution)/shard_map/ppermute | solution.py:46
  110.0 1.6 %collective-permute-done.36 = f32[32,256]{1,0:T(8,128)S(1)} collective-permute-done((f32[32,256]{1,0:T(8,128)S(1)}, f32[32,256]{1,0:T(8,128)S(1)}, u32[]{:S(2)}, u32[]{:S(2)}) %collective-permute-start.36) | collective-permute-done | bytes 32800 | tf_op jit(solution)/shard_map/ppermute | solution.py:46
  111.6 3.5 %collective-permute-done.35 = f32[32,256]{1,0:T(8,128)S(1)} collective-permute-done((f32[32,256]{1,0:T(8,128)S(1)}, f32[32,256]{1,0:T(8,128)S(1)}, u32[]{:S(2)}, u32[]{:S(2)}) %collective-permute-start.35) | collective-permute-done | bytes 32800 | tf_op jit(solution)/shard_map/ppermute | solution.py:46
  115.2 2.0 %collective-permute-start.38 = (f32[32,256]{1,0:T(8,128)S(1)}, f32[32,256]{1,0:T(8,128)S(1)}, u32[]{:S(2)}, u32[]{:S(2)}) collective-permute-start(f32[32,256]{1,0:T(8,128)S(1)} %add_add_fusion.5), channel_id=1, source_target_pairs={{0,16},{8,24},{16,32},{24,40},{32,48},{40,56},{48,0},{56,8},{64,80... | collective-permute-start | bytes 98312 | tf_op jit(solution)/shard_map/ppermute | solution.py:38
  117.2 1.9 %collective-permute-done.39 = f32[32,256]{1,0:T(8,128)S(1)} collective-permute-done((f32[32,256]{1,0:T(8,128)S(1)}, f32[32,256]{1,0:T(8,128)S(1)}, u32[]{:S(2)}, u32[]{:S(2)}) %collective-permute-start.39) | collective-permute-done | bytes 32800 | tf_op jit(solution)/shard_map/ppermute | solution.py:38
  119.2 3.4 %collective-permute-done.37 = f32[32,256]{1,0:T(8,128)S(1)} collective-permute-done((f32[32,256]{1,0:T(8,128)S(1)}, f32[32,256]{1,0:T(8,128)S(1)}, u32[]{:S(2)}, u32[]{:S(2)}) %collective-permute-start.37) | collective-permute-done | bytes 32800 | tf_op jit(solution)/shard_map/ppermute | solution.py:38
  122.7 4.0 %collective-permute-done.40 = f32[32,256]{1,0:T(8,128)S(1)} collective-permute-done((f32[32,256]{1,0:T(8,128)S(1)}, f32[32,256]{1,0:T(8,128)S(1)}, u32[]{:S(2)}, u32[]{:S(2)}) %collective-permute-start.40) | collective-permute-done | bytes 32800 | tf_op jit(solution)/shard_map/ppermute | solution.py:50
  126.7 1.4 collective-permute-start.43
  128.1 1.5 collective-permute-start.42
  129.7 2.5 %collective-permute-start.41 = (f32[32,256]{1,0:T(8,128)S(1)}, f32[32,256]{1,0:T(8,128)S(1)}, u32[]{:S(2)}, u32[]{:S(2)}) collective-permute-start(f32[32,256]{1,0:T(8,128)S(1)} %add.164), channel_id=1, source_target_pairs={{0,128},{8,136},{16,144},{24,152},{32,160},{40,168},{48,176},{56,1... | collective-permute-start | bytes 98312 | tf_op jit(solution)/shard_map/ppermute | solution.py:34
  132.1 2.0 %collective-permute-done.42 = f32[32,256]{1,0:T(8,128)S(1)} collective-permute-done((f32[32,256]{1,0:T(8,128)S(1)}, f32[32,256]{1,0:T(8,128)S(1)}, u32[]{:S(2)}, u32[]{:S(2)}) %collective-permute-start.42) | collective-permute-done | bytes 32800 | tf_op jit(solution)/shard_map/ppermute | solution.py:34
  134.1 3.3 %collective-permute-done.41 = f32[32,256]{1,0:T(8,128)S(1)} collective-permute-done((f32[32,256]{1,0:T(8,128)S(1)}, f32[32,256]{1,0:T(8,128)S(1)}, u32[]{:S(2)}, u32[]{:S(2)}) %collective-permute-start.41) | collective-permute-done | bytes 32800 | tf_op jit(solution)/shard_map/ppermute | solution.py:34
  137.6 1.2 collective-permute-done.44
  138.8 1.7 %collective-permute-start.46 = (f32[2,32,256]{2,1,0:T(8,128)S(1)}, f32[2,32,256]{2,1,0:T(8,128)S(1)}, u32[]{:S(2)}, u32[]{:S(2)}) collective-permute-start(f32[2,32,256]{2,1,0:T(8,128)S(1)} %pad_maximum_fusion.2.piece0), channel_id=1, source_target_pairs={{0,2},{1,3},{2,0},{3,1},{4,6},{5,7},{6,4},{7,5},{8,10},{9,11},{10,... | collective-permute-start | bytes 196616 | tf_op jit(solution)/shard_map/ppermute | solution.py:46
  140.5 1.5 collective-permute-start.45
  142.0 3.5 %collective-permute-done.47.piece3 = f32[2,32,256]{2,1,0:T(8,128)S(1)} collective-permute-done((f32[2,32,256]{2,1,0:T(8,128)S(1)}, f32[2,32,256]{2,1,0:T(8,128)S(1)}, u32[]{:S(2)}, u32[]{:S(2)}) %collective-permute-start.47) | collective-permute-done | bytes 65568 | tf_op jit(solution)/shard_map/ppermute | solution.py:46
  146.1 11.2 %factor.1 = (f32[128,256]{1,0:T(8,128)}, f32[256,256]{1,0:T(8,128)}) custom-call(s32[4,64]{1,0:T(4,128)S(1)} %pad_add_fusion.table, f32[2,32,256]{2,1,0:T(8,128)S(1)} %pad_maximum_fusion.2.piece0, f32[2,32,256]{2,1,0:T(8,128)S(1)} %collective-permute-done.45.piece1, f32[2,32,256]{2,1,0:T(8,128)S(1)} %collective-permute-done.46.piece2, ...), custom_call_target="tpu_custom_call" | custom-call | tf_op jit(solution)/shard_map/factor/pallas_call | solution.py:291
  (81 shorter events, 17.4 us)
Async XLA Ops:
  0.6 11.2 %collective-permute-start.14 = (bf16[128,256]{1,0:T(8,128)(2,1)}, bf16[128,256]{1,0:T(8,128)(2,1)S(1)}, u32[]{:S(2)}, u32[]{:S(2)}) collective-permute-start(bf16[128,256]{1,0:T(8,128)(2,1)} %param.9), channel_id=1, source_target_pairs={{0,4},{1,5},{2,6},{3,7},{4,0},{5,1},{6,2},{7,3},{8,12},{9,13},{10,... | collective-permute-start | bytes 196616 | tf_op jit(solution)/shard_map/ppermute | solution.py:50
  2.6 15.4 %collective-permute-start.1 = (bf16[128,256]{1,0:T(8,128)(2,1)}, bf16[128,256]{1,0:T(8,128)(2,1)S(1)}, u32[]{:S(2)}, u32[]{:S(2)}) collective-permute-start(bf16[128,256]{1,0:T(8,128)(2,1)} %param.9), channel_id=1, source_target_pairs={{0,128},{8,136},{16,144},{24,152},{32,160},{40,168},{48,176},{56,1... | collective-permute-start | bytes 196616 | tf_op jit(solution)/shard_map/ppermute | solution.py:34
  8.9 10.5 %collective-permute-start = (bf16[128,256]{1,0:T(8,128)(2,1)}, bf16[128,256]{1,0:T(8,128)(2,1)S(1)}, u32[]{:S(2)}, u32[]{:S(2)}) collective-permute-start(bf16[128,256]{1,0:T(8,128)(2,1)} %param.9), channel_id=1, source_target_pairs={{0,192},{8,200},{16,208},{24,216},{32,224},{40,232},{48,240},{56,2... | collective-permute-start | bytes 196616 | tf_op jit(solution)/shard_map/ppermute | solution.py:34
  9.5 9.9 %collective-permute-start.2 = (bf16[128,256]{1,0:T(8,128)(2,1)}, bf16[128,256]{1,0:T(8,128)(2,1)S(1)}, u32[]{:S(2)}, u32[]{:S(2)}) collective-permute-start(bf16[128,256]{1,0:T(8,128)(2,1)} %param.9), channel_id=1, source_target_pairs={{0,64},{8,72},{16,80},{24,88},{32,96},{40,104},{48,112},{56,120},{... | collective-permute-start | bytes 196616 | tf_op jit(solution)/shard_map/ppermute | solution.py:34
  12.7 9.2 %collective-permute-start.17 = (bf16[2,128,256]{2,1,0:T(8,128)(2,1)S(1)}, bf16[2,128,256]{2,1,0:T(8,128)(2,1)S(1)}, u32[]{:S(2)}, u32[]{:S(2)}) collective-permute-start(bf16[2,128,256]{2,1,0:T(8,128)(2,1)S(1)} %pad_maximum_fusion.1.refs_0_), channel_id=1, source_target_pairs={{0,1},{1,2},{2,3},{3,0},{4,5},{5,6},{6,7},{7,4},{8,9},{9,10},{10,1... | collective-permute-start | bytes 393224 | tf_op jit(solution)/shard_map/ppermute | solution.py:46
  14.4 8.7 %collective-permute-start.16 = (bf16[2,128,256]{2,1,0:T(8,128)(2,1)S(1)}, bf16[2,128,256]{2,1,0:T(8,128)(2,1)S(1)}, u32[]{:S(2)}, u32[]{:S(2)}) collective-permute-start(bf16[2,128,256]{2,1,0:T(8,128)(2,1)S(1)} %pad_maximum_fusion.1.refs_0_), channel_id=1, source_target_pairs={{0,2},{1,3},{2,0},{3,1},{4,6},{5,7},{6,4},{7,5},{8,10},{9,11},{10,... | collective-permute-start | bytes 393224 | tf_op jit(solution)/shard_map/ppermute | solution.py:46
  18.0 7.9 %collective-permute-start.15 = (bf16[2,128,256]{2,1,0:T(8,128)(2,1)S(1)}, bf16[2,128,256]{2,1,0:T(8,128)(2,1)S(1)}, u32[]{:S(2)}, u32[]{:S(2)}) collective-permute-start(bf16[2,128,256]{2,1,0:T(8,128)(2,1)S(1)} %pad_maximum_fusion.1.refs_0_), channel_id=1, source_target_pairs={{0,3},{1,0},{2,1},{3,2},{4,7},{5,4},{6,5},{7,6},{8,11},{9,8},{10,9... | collective-permute-start | bytes 393224 | tf_op jit(solution)/shard_map/ppermute | solution.py:46
  20.3 11.8 %collective-permute-start.6 = (bf16[4,128,256]{2,1,0:T(8,128)(2,1)S(1)}, bf16[4,128,256]{2,1,0:T(8,128)(2,1)S(1)}, u32[]{:S(2)}, u32[]{:S(2)}) collective-permute-start(bf16[4,128,256]{2,1,0:T(8,128)(2,1)S(1)} %pad_maximum_fusion.refs_0_), channel_id=1, source_target_pairs={{0,8},{8,0},{16,24},{24,16},{32,40},{40,32},{48,56},{56,48},{64,72... | collective-permute-start | bytes 786440 | tf_op jit(solution)/shard_map/ppermute | solution.py:42
  20.4 11.2 %collective-permute-start.5 = (bf16[4,128,256]{2,1,0:T(8,128)(2,1)S(1)}, bf16[4,128,256]{2,1,0:T(8,128)(2,1)S(1)}, u32[]{:S(2)}, u32[]{:S(2)}) collective-permute-start(bf16[4,128,256]{2,1,0:T(8,128)(2,1)S(1)} %pad_maximum_fusion.refs_0_), channel_id=1, source_target_pairs={{0,16},{8,24},{16,32},{24,40},{32,48},{40,56},{48,0},{56,8},{64,80... | collective-permute-start | bytes 786440 | tf_op jit(solution)/shard_map/ppermute | solution.py:38
  22.0 10.7 %collective-permute-start.4 = (bf16[4,128,256]{2,1,0:T(8,128)(2,1)S(1)}, bf16[4,128,256]{2,1,0:T(8,128)(2,1)S(1)}, u32[]{:S(2)}, u32[]{:S(2)}) collective-permute-start(bf16[4,128,256]{2,1,0:T(8,128)(2,1)S(1)} %pad_maximum_fusion.refs_0_), channel_id=1, source_target_pairs={{0,32},{8,40},{16,48},{24,56},{32,0},{40,8},{48,16},{56,24},{64,96... | collective-permute-start | bytes 786440 | tf_op jit(solution)/shard_map/ppermute | solution.py:38
  23.1 13.7 %collective-permute-start.3 = (bf16[4,128,256]{2,1,0:T(8,128)(2,1)S(1)}, bf16[4,128,256]{2,1,0:T(8,128)(2,1)S(1)}, u32[]{:S(2)}, u32[]{:S(2)}) collective-permute-start(bf16[4,128,256]{2,1,0:T(8,128)(2,1)S(1)} %pad_maximum_fusion.refs_0_), channel_id=1, source_target_pairs={{0,48},{8,56},{16,0},{24,8},{32,16},{40,24},{48,32},{56,40},{64,11... | collective-permute-start | bytes 786440 | tf_op jit(solution)/shard_map/ppermute | solution.py:38
  31.5 28.0 %collective-permute-start.18 = (f32[1216,256]{1,0:T(8,128)}, f32[1216,256]{1,0:T(8,128)}, u32[]{:S(2)}, u32[]{:S(2)}) collective-permute-start(f32[1216,256]{1,0:T(8,128)} %get-tuple-element.17), channel_id=1, source_target_pairs={{0,8},{8,0},{16,24},{24,16},{32,40},{40,32},{48,56},{56,48},{64,72... | collective-permute-start | bytes 3735560 | tf_op jit(solution)/shard_map/ppermute | solution.py:42
  31.6 5.2 %collective-permute-start.9 = (bf16[4,128,256]{2,1,0:T(8,128)(2,1)S(1)}, bf16[4,128,256]{2,1,0:T(8,128)(2,1)S(1)}, u32[]{:S(2)}, u32[]{:S(2)}) collective-permute-start(bf16[4,128,256]{2,1,0:T(8,128)(2,1)S(1)} %collective-permute-done.5.refs_3_), channel_id=1, source_target_pairs={{0,8},{8,0},{16,24},{24,16},{32,40},{40,32},{48,56},{56,48},{64,72... | collective-permute-start | bytes 786440 | tf_op jit(solution)/shard_map/ppermute | solution.py:42
  32.1 12.1 %collective-permute-start.20 = (f32[4,104,256]{2,1,0:T(8,128)S(1)}, f32[4,104,256]{2,1,0:T(8,128)S(1)}, u32[]{:S(2)}, u32[]{:S(2)}) collective-permute-start(f32[4,104,256]{2,1,0:T(8,128)S(1)} %get-tuple-element.19), channel_id=1, source_target_pairs={{0,8},{8,0},{16,24},{24,16},{32,40},{40,32},{48,56},{56,48},{64,72... | collective-permute-start | bytes 1277960 | tf_op jit(solution)/shard_map/ppermute | solution.py:42
  32.7 4.6 %collective-permute-start.8 = (bf16[4,128,256]{2,1,0:T(8,128)(2,1)S(1)}, bf16[4,128,256]{2,1,0:T(8,128)(2,1)S(1)}, u32[]{:S(2)}, u32[]{:S(2)}) collective-permute-start(bf16[4,128,256]{2,1,0:T(8,128)(2,1)S(1)} %collective-permute-done.4.refs_2_), channel_id=1, source_target_pairs={{0,8},{8,0},{16,24},{24,16},{32,40},{40,32},{48,56},{56,48},{64,72... | collective-permute-start | bytes 786440 | tf_op jit(solution)/shard_map/ppermute | solution.py:42
  36.8 1.5 collective-permute-start.7
  36.8 12.3 %collective-permute-start.22 = (f32[4,104,256]{2,1,0:T(8,128)S(1)}, f32[4,104,256]{2,1,0:T(8,128)}, u32[]{:S(2)}, u32[]{:S(2)}) collective-permute-start(f32[4,104,256]{2,1,0:T(8,128)S(1)} %get-tuple-element.21), channel_id=1, source_target_pairs={{0,8},{8,0},{16,24},{24,16},{32,40},{40,32},{48,56},{56,48},{64,72... | collective-permute-start | bytes 1277960 | tf_op jit(solution)/shard_map/ppermute | solution.py:42
  42.6 11.1 %collective-permute-start.10 = (f32[2,128,256]{2,1,0:T(8,128)}, f32[2,128,256]{2,1,0:T(8,128)}, u32[]{:S(2)}, u32[]{:S(2)}) collective-permute-start(f32[2,128,256]{2,1,0:T(8,128)} %get-tuple-element.13), channel_id=1, source_target_pairs={{0,2},{1,3},{2,0},{3,1},{4,6},{5,7},{6,4},{7,5},{8,10},{9,11},{10,... | collective-permute-start | bytes 786440 | tf_op jit(solution)/shard_map/ppermute | solution.py:46
  44.0 14.2 %collective-permute-start.11 = (f32[2,128,256]{2,1,0:T(8,128)S(1)}, f32[2,128,256]{2,1,0:T(8,128)}, u32[]{:S(2)}, u32[]{:S(2)}) collective-permute-start(f32[2,128,256]{2,1,0:T(8,128)S(1)} %get-tuple-element.14), channel_id=1, source_target_pairs={{0,1},{1,2},{2,3},{3,0},{4,5},{5,6},{6,7},{7,4},{8,9},{9,10},{10,1... | collective-permute-start | bytes 786440 | tf_op jit(solution)/shard_map/ppermute | solution.py:46
  44.9 13.4 %collective-permute-start.12 = (f32[2,128,256]{2,1,0:T(8,128)S(1)}, f32[2,128,256]{2,1,0:T(8,128)}, u32[]{:S(2)}, u32[]{:S(2)}) collective-permute-start(f32[2,128,256]{2,1,0:T(8,128)S(1)} %get-tuple-element.15), channel_id=1, source_target_pairs={{0,3},{1,0},{2,1},{3,2},{4,7},{5,4},{6,5},{7,6},{8,11},{9,8},{10,9... | collective-permute-start | bytes 786440 | tf_op jit(solution)/shard_map/ppermute | solution.py:46
  49.1 28.4 %collective-permute-start.21 = (f32[4,104,256]{2,1,0:T(8,128)S(1)}, f32[4,104,256]{2,1,0:T(8,128)S(1)}, u32[]{:S(2)}, u32[]{:S(2)}) collective-permute-start(f32[4,104,256]{2,1,0:T(8,128)S(1)} %add.133), channel_id=1, source_target_pairs={{0,16},{8,24},{16,32},{24,40},{32,48},{40,56},{48,0},{56,8},{64,80... | collective-permute-start | bytes 1277960 | tf_op jit(solution)/shard_map/ppermute | solution.py:38
  53.8 24.4 %collective-permute-start.23 = (f32[4,104,256]{2,1,0:T(8,128)S(1)}, f32[4,104,256]{2,1,0:T(8,128)S(1)}, u32[]{:S(2)}, u32[]{:S(2)}) collective-permute-start(f32[4,104,256]{2,1,0:T(8,128)S(1)} %add.134), channel_id=1, source_target_pairs={{0,48},{8,56},{16,0},{24,8},{32,16},{40,24},{48,32},{56,40},{64,11... | collective-permute-start | bytes 1277960 | tf_op jit(solution)/shard_map/ppermute | solution.py:38
  60.6 7.6 %collective-permute-start.29 = (f32[4,24,256]{2,1,0:T(8,128)S(1)}, f32[4,24,256]{2,1,0:T(8,128)S(1)}, u32[]{:S(2)}, u32[]{:S(2)}) collective-permute-start(f32[4,24,256]{2,1,0:T(8,128)S(1)} %bitcast.62), channel_id=1, source_target_pairs={{0,192},{8,200},{16,208},{24,216},{32,224},{40,232},{48,240},{56,2... | collective-permute-start | bytes 294920 | tf_op jit(solution)/shard_map/ppermute | solution.py:34
  61.2 11.4 %collective-permute-start.27 = (f32[4,24,256]{2,1,0:T(8,128)S(1)}, f32[4,24,256]{2,1,0:T(8,128)S(1)}, u32[]{:S(2)}, u32[]{:S(2)}) collective-permute-start(f32[4,24,256]{2,1,0:T(8,128)S(1)} %bitcast.61), channel_id=1, source_target_pairs={{0,128},{8,136},{16,144},{24,152},{32,160},{40,168},{48,176},{56,1... | collective-permute-start | bytes 294920 | tf_op jit(solution)/shard_map/ppermute | solution.py:34
  66.7 9.2 %collective-permute-start.28 = (f32[4,24,256]{2,1,0:T(8,128)S(1)}, f32[4,24,256]{2,1,0:T(8,128)S(1)}, u32[]{:S(2)}, u32[]{:S(2)}) collective-permute-start(f32[4,24,256]{2,1,0:T(8,128)S(1)} %bitcast.60), channel_id=1, source_target_pairs={{0,64},{8,72},{16,80},{24,88},{32,96},{40,104},{48,112},{56,120},{... | collective-permute-start | bytes 294920 | tf_op jit(solution)/shard_map/ppermute | solution.py:34
  68.2 32.7 %collective-permute-start.13 = (f32[128,256]{1,0:T(8,128)S(1)}, f32[128,256]{1,0:T(8,128)S(1)}, u32[]{:S(2)}, u32[]{:S(2)}) collective-permute-start(f32[128,256]{1,0:T(8,128)S(1)} %slice_bitcast_fusion), channel_id=1, source_target_pairs={{0,4},{1,5},{2,6},{3,7},{4,0},{5,1},{6,2},{7,3},{8,12},{9,13},{10,... | collective-permute-start | bytes 393224 | tf_op jit(solution)/shard_map/ppermute | solution.py:50
  72.6 10.2 %collective-permute-start.19 = (f32[4,104,256]{2,1,0:T(8,128)S(1)}, f32[4,104,256]{2,1,0:T(8,128)S(1)}, u32[]{:S(2)}, u32[]{:S(2)}) collective-permute-start(f32[4,104,256]{2,1,0:T(8,128)S(1)} %bitcast.55), channel_id=1, source_target_pairs={{0,32},{8,40},{16,48},{24,56},{32,0},{40,8},{48,16},{56,24},{64,96... | collective-permute-start | bytes 1277960 | tf_op jit(solution)/shard_map/ppermute | solution.py:38
  76.0 9.8 %collective-permute-start.32 = (f32[24,256]{1,0:T(8,128)S(1)}, f32[24,256]{1,0:T(8,128)S(1)}, u32[]{:S(2)}, u32[]{:S(2)}) collective-permute-start(f32[24,256]{1,0:T(8,128)S(1)} %get-tuple-element.34), channel_id=1, source_target_pairs={{0,48},{8,56},{16,0},{24,8},{32,16},{40,24},{48,32},{56,40},{64,11... | collective-permute-start | bytes 73736 | tf_op jit(solution)/shard_map/ppermute | solution.py:38
  77.5 10.8 %collective-permute-start.31 = (f32[24,256]{1,0:T(8,128)S(1)}, f32[24,256]{1,0:T(8,128)S(1)}, u32[]{:S(2)}, u32[]{:S(2)}) collective-permute-start(f32[24,256]{1,0:T(8,128)S(1)} %get-tuple-element.35), channel_id=1, source_target_pairs={{0,16},{8,24},{16,32},{24,40},{32,48},{40,56},{48,0},{56,8},{64,80... | collective-permute-start | bytes 73736 | tf_op jit(solution)/shard_map/ppermute | solution.py:38
  78.2 13.8 %collective-permute-start.30 = (f32[24,256]{1,0:T(8,128)S(1)}, f32[24,256]{1,0:T(8,128)S(1)}, u32[]{:S(2)}, u32[]{:S(2)}) collective-permute-start(f32[24,256]{1,0:T(8,128)S(1)} %get-tuple-element.36), channel_id=1, source_target_pairs={{0,32},{8,40},{16,48},{24,56},{32,0},{40,8},{48,16},{56,24},{64,96... | collective-permute-start | bytes 73736 | tf_op jit(solution)/shard_map/ppermute | solution.py:38
  82.9 9.1 %collective-permute-start.26 = (f32[104,256]{1,0:T(8,128)S(1)}, f32[104,256]{1,0:T(8,128)S(1)}, u32[]{:S(2)}, u32[]{:S(2)}) collective-permute-start(f32[104,256]{1,0:T(8,128)S(1)} %get-tuple-element.24), channel_id=1, source_target_pairs={{0,192},{8,200},{16,208},{24,216},{32,224},{40,232},{48,240},{56,2... | collective-permute-start | bytes 319496 | tf_op jit(solution)/shard_map/ppermute | solution.py:34
  85.7 7.1 %collective-permute-start.25 = (f32[104,256]{1,0:T(8,128)S(1)}, f32[104,256]{1,0:T(8,128)S(1)}, u32[]{:S(2)}, u32[]{:S(2)}) collective-permute-start(f32[104,256]{1,0:T(8,128)S(1)} %get-tuple-element.25), channel_id=1, source_target_pairs={{0,64},{8,72},{16,80},{24,88},{32,96},{40,104},{48,112},{56,120},{... | collective-permute-start | bytes 319496 | tf_op jit(solution)/shard_map/ppermute | solution.py:34
  88.3 12.5 %collective-permute-start.24 = (f32[104,256]{1,0:T(8,128)S(1)}, f32[104,256]{1,0:T(8,128)S(1)}, u32[]{:S(2)}, u32[]{:S(2)}) collective-permute-start(f32[104,256]{1,0:T(8,128)S(1)} %get-tuple-element.26), channel_id=1, source_target_pairs={{0,128},{8,136},{16,144},{24,152},{32,160},{40,168},{48,176},{56,1... | collective-permute-start | bytes 319496 | tf_op jit(solution)/shard_map/ppermute | solution.py:34
  101.3 1.4 collective-permute-start.33
  102.8 7.2 %collective-permute-start.34 = (f32[32,256]{1,0:T(8,128)S(1)}, f32[32,256]{1,0:T(8,128)S(1)}, u32[]{:S(2)}, u32[]{:S(2)}) collective-permute-start(f32[32,256]{1,0:T(8,128)S(1)} %get-tuple-element.31), channel_id=1, source_target_pairs={{0,2},{1,3},{2,0},{3,1},{4,6},{5,7},{6,4},{7,5},{8,10},{9,11},{10,... | collective-permute-start | bytes 98312 | tf_op jit(solution)/shard_map/ppermute | solution.py:46
  105.2 6.4 %collective-permute-start.36 = (f32[32,256]{1,0:T(8,128)S(1)}, f32[32,256]{1,0:T(8,128)S(1)}, u32[]{:S(2)}, u32[]{:S(2)}) collective-permute-start(f32[32,256]{1,0:T(8,128)S(1)} %get-tuple-element.32), channel_id=1, source_target_pairs={{0,3},{1,0},{2,1},{3,2},{4,7},{5,4},{6,5},{7,6},{8,11},{9,8},{10,9... | collective-permute-start | bytes 98312 | tf_op jit(solution)/shard_map/ppermute | solution.py:46
  110.0 5.1 %collective-permute-start.35 = (f32[32,256]{1,0:T(8,128)S(1)}, f32[32,256]{1,0:T(8,128)S(1)}, u32[]{:S(2)}, u32[]{:S(2)}) collective-permute-start(f32[32,256]{1,0:T(8,128)S(1)} %get-tuple-element.33), channel_id=1, source_target_pairs={{0,1},{1,2},{2,3},{3,0},{4,5},{5,6},{6,7},{7,4},{8,9},{9,10},{10,1... | collective-permute-start | bytes 98312 | tf_op jit(solution)/shard_map/ppermute | solution.py:46
  115.1 4.0 %collective-permute-start.39 = (f32[32,256]{1,0:T(8,128)S(1)}, f32[32,256]{1,0:T(8,128)S(1)}, u32[]{:S(2)}, u32[]{:S(2)}) collective-permute-start(f32[32,256]{1,0:T(8,128)S(1)} %add_add_fusion.5), channel_id=1, source_target_pairs={{0,48},{8,56},{16,0},{24,8},{32,16},{40,24},{48,32},{56,40},{64,11... | collective-permute-start | bytes 98312 | tf_op jit(solution)/shard_map/ppermute | solution.py:38
  115.2 4.0 %collective-permute-start.38 = (f32[32,256]{1,0:T(8,128)S(1)}, f32[32,256]{1,0:T(8,128)S(1)}, u32[]{:S(2)}, u32[]{:S(2)}) collective-permute-start(f32[32,256]{1,0:T(8,128)S(1)} %add_add_fusion.5), channel_id=1, source_target_pairs={{0,16},{8,24},{16,32},{24,40},{32,48},{40,56},{48,0},{56,8},{64,80... | collective-permute-start | bytes 98312 | tf_op jit(solution)/shard_map/ppermute | solution.py:38
  117.2 5.4 %collective-permute-start.37 = (f32[32,256]{1,0:T(8,128)S(1)}, f32[32,256]{1,0:T(8,128)S(1)}, u32[]{:S(2)}, u32[]{:S(2)}) collective-permute-start(f32[32,256]{1,0:T(8,128)S(1)} %add_add_fusion.5), channel_id=1, source_target_pairs={{0,32},{8,40},{16,48},{24,56},{32,0},{40,8},{48,16},{56,24},{64,96... | collective-permute-start | bytes 98312 | tf_op jit(solution)/shard_map/ppermute | solution.py:38
  122.6 4.1 %collective-permute-start.40 = (f32[32,256]{1,0:T(8,128)S(1)}, f32[32,256]{1,0:T(8,128)S(1)}, u32[]{:S(2)}, u32[]{:S(2)}) collective-permute-start(f32[32,256]{1,0:T(8,128)S(1)} %add_add_fusion.4), channel_id=1, source_target_pairs={{0,4},{1,5},{2,6},{3,7},{4,0},{5,1},{6,2},{7,3},{8,12},{9,13},{10,... | collective-permute-start | bytes 98312 | tf_op jit(solution)/shard_map/ppermute | solution.py:50
  126.7 5.4 %collective-permute-start.43 = (f32[32,256]{1,0:T(8,128)S(1)}, f32[32,256]{1,0:T(8,128)S(1)}, u32[]{:S(2)}, u32[]{:S(2)}) collective-permute-start(f32[32,256]{1,0:T(8,128)S(1)} %add.164), channel_id=1, source_target_pairs={{0,192},{8,200},{16,208},{24,216},{32,224},{40,232},{48,240},{56,2... | collective-permute-start | bytes 98312 | tf_op jit(solution)/shard_map/ppermute | solution.py:34
  128.1 6.0 %collective-permute-start.42 = (f32[32,256]{1,0:T(8,128)S(1)}, f32[32,256]{1,0:T(8,128)S(1)}, u32[]{:S(2)}, u32[]{:S(2)}) collective-permute-start(f32[32,256]{1,0:T(8,128)S(1)} %add.164), channel_id=1, source_target_pairs={{0,64},{8,72},{16,80},{24,88},{32,96},{40,104},{48,112},{56,120},{... | collective-permute-start | bytes 98312 | tf_op jit(solution)/shard_map/ppermute | solution.py:34
  129.7 7.8 %collective-permute-start.41 = (f32[32,256]{1,0:T(8,128)S(1)}, f32[32,256]{1,0:T(8,128)S(1)}, u32[]{:S(2)}, u32[]{:S(2)}) collective-permute-start(f32[32,256]{1,0:T(8,128)S(1)} %add.164), channel_id=1, source_target_pairs={{0,128},{8,136},{16,144},{24,152},{32,160},{40,168},{48,176},{56,1... | collective-permute-start | bytes 98312 | tf_op jit(solution)/shard_map/ppermute | solution.py:34
  137.5 1.3 collective-permute-start.44
  138.8 6.8 %collective-permute-start.47 = (f32[2,32,256]{2,1,0:T(8,128)S(1)}, f32[2,32,256]{2,1,0:T(8,128)S(1)}, u32[]{:S(2)}, u32[]{:S(2)}) collective-permute-start(f32[2,32,256]{2,1,0:T(8,128)S(1)} %pad_maximum_fusion.2.piece0), channel_id=1, source_target_pairs={{0,1},{1,2},{2,3},{3,0},{4,5},{5,6},{6,7},{7,4},{8,9},{9,10},{10,1... | collective-permute-start | bytes 196616 | tf_op jit(solution)/shard_map/ppermute | solution.py:46
  138.8 6.8 %collective-permute-start.46 = (f32[2,32,256]{2,1,0:T(8,128)S(1)}, f32[2,32,256]{2,1,0:T(8,128)S(1)}, u32[]{:S(2)}, u32[]{:S(2)}) collective-permute-start(f32[2,32,256]{2,1,0:T(8,128)S(1)} %pad_maximum_fusion.2.piece0), channel_id=1, source_target_pairs={{0,2},{1,3},{2,0},{3,1},{4,6},{5,7},{6,4},{7,5},{8,10},{9,11},{10,... | collective-permute-start | bytes 196616 | tf_op jit(solution)/shard_map/ppermute | solution.py:46
  140.5 5.7 %collective-permute-start.45 = (f32[2,32,256]{2,1,0:T(8,128)S(1)}, f32[2,32,256]{2,1,0:T(8,128)S(1)}, u32[]{:S(2)}, u32[]{:S(2)}) collective-permute-start(f32[2,32,256]{2,1,0:T(8,128)S(1)} %pad_maximum_fusion.2.piece0), channel_id=1, source_target_pairs={{0,3},{1,0},{2,1},{3,2},{4,7},{5,4},{6,5},{7,6},{8,11},{9,8},{10,9... | collective-permute-start | bytes 196616 | tf_op jit(solution)/shard_map/ppermute | solution.py:46
  (1 other events, 0.8 us)
